TPU v7x, 32 devices: a whole 2x2x4 slice. The times are simulated.
32 devices in a mesh: items: 16 (over z, y, core), seq: 2 (over x).
Axes of the slice: x: 2, y: 2, z: 4, core: 2. Of those that a mesh axis runs over, the one named last changes fastest.
Arguments:
- frames: bfloat16 [16, 1280, 1024], P('items', 'seq'), may hold values from -6 to 6
- cotangent: bfloat16 [16, 1280, 1024], P('items', 'seq'), may hold values from -6 to 6
- section: int32 [16], P('items'), may hold values from 0 to 7
- prompt_len: int32 [16], P('items'), may hold values from 150 to 600, as said below
- section_embed: float32 [8, 1024], replicated, may hold values from -6 to 6
- ada_proj: bfloat16 [1024, 4096], replicated, may hold values from -0.09375 to 0.09375
- ada_bias: float32 [4096], replicated, may hold values from -4 to 4
- w_qkv: bfloat16 [1024, 3072], replicated, may hold values from -0.1875 to 0.1875
- w_out: bfloat16 [1024, 1024], replicated, may hold values from -3.5 to 3.5
- w_up: bfloat16 [1024, 4096], replicated, may hold values from -0.1875 to 0.1875
- w_down: bfloat16 [4096, 1024], replicated, may hold values from -0.125 to 0.125
Outputs:
- out_frames: bfloat16 [16, 1280, 1024], P('items', 'seq')
- frames_grad: bfloat16 [16, 1280, 1024], P('items', 'seq')
- section_embed_grad: float32 [8, 1024], P(None, 'items')
- ada_proj_grad: float32 [1024, 4096], P('items')
- ada_bias_grad: float32 [4096], P('items')
- w_qkv_grad: float32 [1024, 3072], P('items')
- w_out_grad: float32 [1024, 1024], P('items')
- w_up_grad: float32 [1024, 4096], P('items')
- w_down_grad: float32 [4096, 1024], P('items')
Inputs may be any that keep to these rules, and one draw needn't show every extreme that they name: `prompt_len`: some item has exactly 600 prompt frames.
All inputs are finite; a program needn't handle non-finite values.
Results may differ from a plain program's by a relative error of at most 0.018.
Values may be sent and summed in bfloat16 or wider, within the bound.
A program may use at most 640 MiB of HBM per device.

v0:
```python
import jax
import jax.numpy as jnp
from jax import lax
from jax.sharding import PartitionSpec as P

HEADS = 16


EPS = 1e-05
NEGATIVE = -1e30
SQRT_HALF = 0.7071067811865476
INV_SQRT_TAU = 0.3989422804014327
HIGHEST = lax.Precision.HIGHEST


def normalize(values):
    mean = jnp.mean(values, -1, keepdims=True)
    centered = values - mean
    inverse = lax.rsqrt(jnp.mean(centered * centered, -1, keepdims=True) + EPS)
    return (centered * inverse, inverse)


def norm_back(grad, normed, inverse):
    first = jnp.mean(grad, -1, keepdims=True)
    second = jnp.mean(grad * normed, -1, keepdims=True)
    return (grad - first - normed * second) * inverse


def gelu_exact(values):
    return 0.5 * values * (1.0 + lax.erf(values * SQRT_HALF))


def gelu_slope(values):
    return (
        0.5 * (1.0 + lax.erf(values * SQRT_HALF))
        + values * jnp.exp(-0.5 * values * values) * INV_SQRT_TAU
    )


def project(left, weight):
    flat = left.reshape(-1, left.shape[-1])
    result = jnp.dot(flat, weight, preferred_element_type=jnp.float32)
    return result.reshape(left.shape[:-1] + (weight.shape[1],))


def back_project(grad, weight):
    flat = grad.reshape(-1, grad.shape[-1])
    result = lax.dot_general(
        flat, weight, (((1,), (1,)), ((), ())), preferred_element_type=jnp.float32
    )
    return result.reshape(grad.shape[:-1] + (weight.shape[0],))


def outer_sum(left, right):
    left_flat = left.reshape(-1, left.shape[-1])
    right_flat = right.reshape(-1, right.shape[-1])
    return lax.dot_general(
        left_flat, right_flat, (((0,), (0,)), ((), ())), preferred_element_type=jnp.float32
    )


def per_device(
    frames,
    cotangent,
    section,
    prompt_len,
    section_embed,
    ada_proj,
    ada_bias,
    w_qkv,
    w_out,
    w_up,
    w_down,
):
    group_count, row_count, width = frames.shape
    head_count = HEADS
    head_size = width // head_count
    scale = head_size ** (-0.5)
    section_count = section_embed.shape[0]
    onehot = (section[:, None] == jnp.arange(section_count, dtype=jnp.int32)[None, :]).astype(
        jnp.float32
    )
    cond = jnp.dot(onehot, section_embed, precision=HIGHEST)
    ada_full = ada_proj.astype(jnp.float32)
    modul = jnp.dot(cond, ada_full, precision=HIGHEST) + ada_bias[None, :]
    scale_one, shift_one, scale_two, shift_two = jnp.split(modul, 4, axis=-1)
    inputs = frames.astype(jnp.float32)
    normed_one, inv_one = normalize(inputs)
    attn_in = (normed_one * (1.0 + scale_one[:, None, :]) + shift_one[:, None, :]).astype(
        jnp.bfloat16
    )
    qkv = project(attn_in, w_qkv)
    query = qkv[..., :width].astype(jnp.bfloat16)
    key_local = qkv[..., width : 2 * width].astype(jnp.bfloat16)
    value_local = qkv[..., 2 * width :].astype(jnp.bfloat16)
    query_heads = query.reshape(group_count, row_count, head_count, head_size)

    def key_mask(count):
        position = jnp.arange(count, dtype=jnp.int32)
        valid = (position[None, :] >= row_count) | (position[None, :] < prompt_len[:, None])
        return valid[:, None, None, :]

    run_max = jnp.full((group_count, head_count, row_count), NEGATIVE, jnp.float32)
    key_piece = lax.all_gather(key_local, "seq", axis=1, tiled=True)
    value_piece = lax.all_gather(value_local, "seq", axis=1, tiled=True)
    count = key_piece.shape[1]
    key_heads = key_piece.reshape(group_count, count, head_count, head_size)
    value_heads = value_piece.reshape(group_count, count, head_count, head_size)
    valid = key_mask(count)
    scores = (
        jnp.einsum("grhd,gkhd->ghrk", query_heads, key_heads, preferred_element_type=jnp.float32)
        * scale
    )
    scores = jnp.where(valid, scores, NEGATIVE)
    new_max = jnp.maximum(run_max, jnp.max(scores, -1))
    weights = jnp.where(valid, jnp.exp(scores - new_max[..., None]), 0.0)
    new_sum = jnp.sum(weights, -1)
    update = jnp.einsum(
        "ghrk,gkhd->grhd",
        weights.astype(jnp.bfloat16),
        value_heads,
        preferred_element_type=jnp.float32,
    )
    accum = update
    run_max, run_sum, accum = (new_max, new_sum, accum)
    att_heads = accum / jnp.transpose(run_sum, (0, 2, 1))[..., None]
    log_total = run_max + jnp.log(run_sum)
    att = att_heads.reshape(group_count, row_count, width).astype(jnp.bfloat16)
    mid = inputs + project(att, w_out)
    normed_two, inv_two = normalize(mid)
    ffn_in = (normed_two * (1.0 + scale_two[:, None, :]) + shift_two[:, None, :]).astype(
        jnp.bfloat16
    )
    upper = project(ffn_in, w_up)
    act = gelu_exact(upper).astype(jnp.bfloat16)
    out_frames = (mid + project(act, w_down)).astype(jnp.bfloat16)
    grad_out = cotangent.astype(jnp.float32)
    grad_w_down = outer_sum(act, cotangent)
    grad_upper = (back_project(cotangent, w_down) * gelu_slope(upper)).astype(jnp.bfloat16)
    grad_w_up = outer_sum(ffn_in, grad_upper)
    grad_ffn_in = back_project(grad_upper, w_up)
    grad_scale_two = jnp.sum(grad_ffn_in * normed_two, 1)
    grad_shift_two = jnp.sum(grad_ffn_in, 1)
    grad_mid = grad_out + norm_back(
        grad_ffn_in * (1.0 + scale_two[:, None, :]), normed_two, inv_two
    )
    grad_mid_low = grad_mid.astype(jnp.bfloat16)
    grad_w_out = outer_sum(att, grad_mid_low)
    grad_att = back_project(grad_mid_low, w_out).astype(jnp.bfloat16)
    grad_att_heads = grad_att.reshape(group_count, row_count, head_count, head_size)
    delta = jnp.transpose(jnp.sum(grad_att_heads.astype(jnp.float32) * att_heads, -1), (0, 2, 1))
    key_piece = lax.all_gather(key_local, "seq", axis=1, tiled=True)
    value_piece = lax.all_gather(value_local, "seq", axis=1, tiled=True)
    count = key_piece.shape[1]
    key_heads = key_piece.reshape(group_count, count, head_count, head_size)
    value_heads = value_piece.reshape(group_count, count, head_count, head_size)
    valid = key_mask(count)
    scores = (
        jnp.einsum("grhd,gkhd->ghrk", query_heads, key_heads, preferred_element_type=jnp.float32)
        * scale
    )
    probs = jnp.where(valid, jnp.exp(scores - log_total[..., None]), 0.0)
    value_part = jnp.einsum(
        "ghrk,grhd->gkhd",
        probs.astype(jnp.bfloat16),
        grad_att_heads,
        preferred_element_type=jnp.float32,
    )
    grad_probs = jnp.einsum(
        "grhd,gkhd->ghrk", grad_att_heads, value_heads, preferred_element_type=jnp.float32
    )
    grad_scores = (probs * (grad_probs - delta[..., None])).astype(jnp.bfloat16)
    grad_query = (
        jnp.einsum("ghrk,gkhd->grhd", grad_scores, key_heads, preferred_element_type=jnp.float32)
        * scale
    )
    key_part = (
        jnp.einsum("ghrk,grhd->gkhd", grad_scores, query_heads, preferred_element_type=jnp.float32)
        * scale
    )
    grad_keys = key_part.reshape(group_count, count, width)
    grad_values = value_part.reshape(group_count, count, width)
    back_result = (grad_query, grad_keys, grad_values)
    grad_query, grad_keys, grad_values = back_result
    own_keys, own_values = (
        lax.psum_scatter(
            grad_keys.astype(jnp.bfloat16), "seq", scatter_dimension=1, tiled=True
        ).astype(jnp.float32),
        lax.psum_scatter(
            grad_values.astype(jnp.bfloat16), "seq", scatter_dimension=1, tiled=True
        ).astype(jnp.float32),
    )
    grad_qkv = jnp.concatenate(
        [
            grad_query.reshape(group_count, row_count, width).astype(jnp.bfloat16),
            own_keys.astype(jnp.bfloat16),
            own_values.astype(jnp.bfloat16),
        ],
        -1,
    )
    grad_w_qkv = outer_sum(attn_in, grad_qkv)
    grad_attn_in = back_project(grad_qkv, w_qkv)
    grad_scale_one = jnp.sum(grad_attn_in * normed_one, 1)
    grad_shift_one = jnp.sum(grad_attn_in, 1)
    frames_grad = (
        grad_mid + norm_back(grad_attn_in * (1.0 + scale_one[:, None, :]), normed_one, inv_one)
    ).astype(jnp.bfloat16)
    grad_modul = jnp.concatenate(
        [grad_scale_one, grad_shift_one, grad_scale_two, grad_shift_two], -1
    )
    grad_ada = lax.dot_general(cond, grad_modul, (((0,), (0,)), ((), ())), precision=HIGHEST)
    grad_bias = jnp.sum(grad_modul, 0)
    grad_cond = lax.dot_general(grad_modul, ada_full, (((1,), (1,)), ((), ())), precision=HIGHEST)
    grad_embed = lax.dot_general(onehot, grad_cond, (((0,), (0,)), ((), ())), precision=HIGHEST)
    parts = (
        lax.psum_scatter(
            grad_embed.astype(jnp.bfloat16), "items", scatter_dimension=1, tiled=True
        ).astype(jnp.float32),
        lax.psum_scatter(
            grad_ada.astype(jnp.bfloat16), "items", scatter_dimension=0, tiled=True
        ).astype(jnp.float32),
        lax.psum_scatter(
            grad_bias.astype(jnp.bfloat16), "items", scatter_dimension=0, tiled=True
        ).astype(jnp.float32),
        lax.psum_scatter(
            grad_w_qkv.astype(jnp.bfloat16), "items", scatter_dimension=0, tiled=True
        ).astype(jnp.float32),
        lax.psum_scatter(
            grad_w_out.astype(jnp.bfloat16), "items", scatter_dimension=0, tiled=True
        ).astype(jnp.float32),
        lax.psum_scatter(
            grad_w_up.astype(jnp.bfloat16), "items", scatter_dimension=0, tiled=True
        ).astype(jnp.float32),
        lax.psum_scatter(
            grad_w_down.astype(jnp.bfloat16), "items", scatter_dimension=0, tiled=True
        ).astype(jnp.float32),
    )
    sum_embed, sum_ada, sum_bias, sum_qkv, sum_out, sum_up, sum_down = (
        lax.psum(parts[0].astype(jnp.bfloat16), "seq").astype(jnp.float32),
        lax.psum(parts[1].astype(jnp.bfloat16), "seq").astype(jnp.float32),
        lax.psum(parts[2].astype(jnp.bfloat16), "seq").astype(jnp.float32),
        lax.psum(parts[3].astype(jnp.bfloat16), "seq").astype(jnp.float32),
        lax.psum(parts[4].astype(jnp.bfloat16), "seq").astype(jnp.float32),
        lax.psum(parts[5].astype(jnp.bfloat16), "seq").astype(jnp.float32),
        lax.psum(parts[6].astype(jnp.bfloat16), "seq").astype(jnp.float32),
    )
    return (
        out_frames,
        frames_grad,
        sum_embed,
        sum_ada,
        sum_bias,
        sum_qkv,
        sum_out,
        sum_up,
        sum_down,
    )


def solution(mesh):
    in_specs = (
        P("items", "seq", None),
        P("items", "seq", None),
        P("items"),
        P("items"),
        P(),
        P(),
        P(),
        P(),
        P(),
        P(),
        P(),
    )
    out_specs = (
        P("items", "seq", None),
        P("items", "seq", None),
        P(None, "items"),
        P("items", None),
        P("items"),
        P("items", None),
        P("items", None),
        P("items", None),
        P("items", None),
    )
    return jax.shard_map(
        per_device, mesh=mesh, in_specs=in_specs, out_specs=out_specs, check_vma=False
    )
```

profile of v0, /device:TPU:0, one launch (start us, length us, event | category | flops | bytes accessed | tf_op | source)
XLA Modules:
  0.0 937.6 jit_solution(6268356600912304803)
XLA Ops:
  8.0 1.6 convert_reduce_fusion
  9.6 1.9 fusion.33
  11.8 5.8 fusion.53
  17.7 4.8 fusion.15
  22.6 2.1 fusion.74
  24.7 0.7 all-gather.3.cloned.1.call-update
  26.3 1.7 copy.35
  28.0 38.5 %all-gather.5.cloned.1.call-done = bf16[1,1280,1024]{2,1,0:T(8,128)(2,1)} async-done(((bf16[1,640,1024]{2,1,0:T(8,128)(2,1)}), bf16[1,1280,1024]{2,1,0:T(8,128)(2,1)}) %all-gather.5.cloned.1.call-update) | async-done | bytes 2621456 | tf_op jit(solution)/shard_map/all_gather | solution.py:104
  66.6 4.5 copy.36
  71.0 20.5 %select_reduce_fusion = (f32[16,640]{1,0:T(8,128)S(1)}, f32[16,640,1280]{2,1,0:T(8,128)}) fusion(pred[1280]{0:T(1024)(128)(4,1)S(1)} %fusion.52, bf16[640,16,64]{0,2,1:T(8,128)(2,1)S(1)} %bitcast.164, bf16[1280,16,64]{0,2,1:T(8,128)(2,1)} %bitcast.160), kind=kOutput, calls=%fused_computation.3 | convolution fusion | flops 1717032960 | bytes 56403200 | tf_op jit(solution)/shard_map/grhd,gkhd->ghrk/dot_general | solution.py:111
  91.5 17.1 %fusion.1 = f32[16,640]{1,0:T(8,128)S(1)} fusion(f32[16,640,1280]{2,1,0:T(8,128)} %get-tuple-element.32, f32[16,640]{1,0:T(8,128)S(1)} %broadcast_maximum_fusion, pred[1280]{0:T(1024)(128)(4,1)S(1)} %fusion.52), kind=kLoop, calls=%fused_computation.5 | loop fusion | flops 65525760 | bytes 52512000 | tf_op jit(solution)/shard_map/reduce_sum | solution.py:117
  108.6 4.4 copy.34
  113.0 22.3 %fusion.75 = (bf16[1,640,16,64]{1,3,2,0:T(8,128)(2,1)S(1)}, f32[1,640,16,64]{1,3,2,0:T(8,128)}) fusion(f32[640,16]{0,1:T(8,128)S(1)} %bitcast.178, bf16[1280,16,64]{0,2,1:T(8,128)(2,1)} %bitcast.170, f32[16,640,1280]{2,1,0:T(8,128)} %get-tuple-element.32, f32[16,640]{1,0:T(8,128)S(1)} %broadcast_maximum_fusion, pred[1280]{0:T(1024)(128)(4,1)S(1)} %fusion.52), kind=kOutput, calls=%fused_computation.117 | convolution fusion | flops 1744568320 | bytes 59065600 | tf_op jit(solution)/shard_map/ghrk,gkhd->grhd/dot_general | solution.py:118
  135.3 1.7 fusion.76
  137.4 12.4 %multiply_convert_fusion.2 = (bf16[640,4096]{1,0:T(8,128)(2,1)}, f32[640,4096]{1,0:T(8,128)}) fusion(bf16[1024,4096]{1,0:T(8,128)(2,1)} %param.20, f32[1,640,1024]{2,1,0:T(8,128)S(1)} %get-tuple-element.36, f32[1024]{0:T(1024)S(1)} %bitcast.207, f32[1024]{0:T(1024)S(1)} %bitcast.192, f32[640]{0:T(1024)S(1)} %add_rsqrt_fusion, ...), kind=kOutput, calls=%fused_computation.19 | convolution fusion | flops 5385093120 | bytes 26752000 | tf_op jit(solution)/shard_map/dot_general | solution.py:42
  149.8 14.0 %fusion.14 = bf16[640,4096]{1,0:T(8,128)(2,1)} fusion(f32[640,4096]{1,0:T(8,128)} %get-tuple-element.38, bf16[4096,1024]{1,0:T(8,128)(2,1)} %param.21, bf16[1,640,1024]{2,1,0:T(8,128)(2,1)S(1)} %copy-done.13), kind=kOutput, calls=%fused_computation.18 | convolution fusion | flops 5394923520 | bytes 25427968 | tf_op jit(solution)/shard_map/dot_general | solution.py:48
  163.9 8.5 fusion.34
  172.7 1.0 fusion.37
  173.7 1.5 copy-done.8
  175.2 1.6 convolution_convert_fusion.5
  176.8 0.7 copy.37
  177.5 1.9 copy.38
  179.5 21.6 %fusion.16 = bf16[16,64,1280]{2,1,0:T(8,128)(2,1)} fusion(bf16[640,16,64]{0,2,1:T(8,128)(2,1)S(1)} %bitcast.175, f32[16,640,1280]{2,1,0:T(8,128)} %get-tuple-element.32, f32[16,640]{1,0:T(8,128)S(1)} %log_add_fusion, pred[1280]{0:T(1024)(128)(4,1)S(1)} %fusion.52), kind=kOutput, calls=%fused_computation.31 | convolution fusion | flops 1731461120 | bytes 56403200 | tf_op jit(solution)/shard_map/ghrk,grhd->gkhd/dot_general | solution.py:163
  201.1 11.5 %copy.41 = bf16[1,1280,1024]{2,0,1:T(2,128)(2,1)} copy(bf16[1,1280,1024]{1,2,0:T(8,128)(2,1)} %bitcast.172) | data formatting | bytes 5242880
  212.6 5.0 copy.49
  217.7 3.1 multiply_reduce_fusion
  221.4 33.9 %multiply_convert_fusion = bf16[16,640,1280]{2,1,0:T(8,128)(2,1)} fusion(f32[16,640,1280]{2,1,0:T(8,128)} %get-tuple-element.32, bf16[640,16,64]{0,2,1:T(8,128)(2,1)S(1)} %bitcast.176, bf16[1280,16,64]{0,2,1:T(8,128)(2,1)S(1)} %bitcast.171, f32[16,640]{1,0:T(8,128)S(1)} %bitcast.184, f32[16,640]{1,0:T(8,128)S(1)} %log_add_fusion, pred[1280]{0:T(1024)(128)(4,1)S(1)} %fusion.52), kind=kOutput, calls=%fused_computation | convolution fusion | flops 1756364800 | bytes 82658560 | tf_op jit(solution)/shard_map/grhd,gkhd->ghrk/dot_general | solution.py:169
  255.3 14.6 %multiply_convert_fusion.3 = bf16[16,64,1280]{2,1,0:T(8,128)(2,1)} fusion(bf16[640,16,64]{0,2,1:T(8,128)(2,1)S(1)} %bitcast.165, bf16[16,640,1280]{2,1,0:T(8,128)(2,1)} %multiply_convert_fusion), kind=kOutput, calls=%fused_computation.24 | convolution fusion | flops 1680343040 | bytes 30146560 | tf_op jit(solution)/shard_map/ghrk,grhd->gkhd/dot_general | solution.py:178
  269.9 11.6 %copy.39 = bf16[1,1280,1024]{2,0,1:T(2,128)(2,1)} copy(bf16[1,1280,1024]{1,2,0:T(8,128)(2,1)} %bitcast.166) | data formatting | bytes 5242880
  281.5 5.0 copy.50
  286.7 1.1 copy-done.30
  287.8 4.8 convolution_convert_fusion.4
  292.7 12.2 %convolution_convert_fusion = bf16[1024,4096]{1,0:T(8,128)(2,1)} fusion(bf16[640,4096]{1,0:T(8,128)(2,1)} %fusion.14, f32[1,640,1024]{2,1,0:T(8,128)} %copy-done.9, f32[1024]{0:T(1024)S(1)} %bitcast.208, f32[1024]{0:T(1024)S(1)} %bitcast.196, f32[640]{0:T(1024)S(1)} %add_rsqrt_fusion, f32[640]{0:T(1024)S(1)} %broadcast_multiply_fusion.4), kind=kOutput, calls=%fused_computation.21 | convolution fusion | flops 5376180224 | bytes 16266240 | tf_op jit(solution)/shard_map/dot_general | solution.py:57
  305.0 1.2 copy-done.14
  306.3 11.5 %convolution_convert_fusion.1 = bf16[4096,1024]{1,0:T(8,128)(2,1)} fusion(bf16[640,4096]{1,0:T(8,128)(2,1)} %get-tuple-element.37, bf16[1,640,1024]{2,1,0:T(8,128)(2,1)S(1)} %copy-done.14), kind=kOutput, calls=%fused_computation.22 | convolution fusion | flops 5372903424 | bytes 14942208 | tf_op jit(solution)/shard_map/dot_general | solution.py:57
  318.0 13.9 %multiply_convert_fusion.4 = bf16[16,64,640]{2,1,0:T(8,128)(2,1)S(1)} fusion(bf16[1280,16,64]{0,2,1:T(8,128)(2,1)} %bitcast.161, bf16[16,640,1280]{2,1,0:T(8,128)(2,1)} %multiply_convert_fusion), kind=kOutput, calls=%fused_computation.61 | convolution fusion | flops 1679032320 | bytes 30146560 | tf_op jit(solution)/shard_map/ghrk,gkhd->grhd/dot_general | solution.py:174
  332.0 4.2 reshape_bitcast_fusion
  336.2 6.1 copy.42
  342.3 4.2 reshape_bitcast_fusion.1
  346.6 6.2 copy.40
  352.8 9.9 %convolution_convert_fusion.2 = bf16[1024,3072]{1,0:T(8,128)(2,1)} fusion(bf16[1,640,1024]{1,2,0:T(8,128)(2,1)} %copy.42, bf16[1,640,1024]{1,2,0:T(8,128)(2,1)} %copy.40, bf16[1,640,1024]{1,2,0:T(8,128)(2,1)S(1)} %bitcast.173, bf16[1,640,1024]{2,1,0:T(8,128)(2,1)S(1)} %copy-done.6, f32[1024]{0:T(1024)S(1)} %bitcast.206, f32[1024]{0:T(1024)S(1)} %bitcast.186, ...), kind=kOutput, calls=%fused_computation.23 | convolution fusion | flops 4045406208 | bytes 11547648 | tf_op jit(solution)/shard_map/dot_general | solution.py:57
  363.0 8.7 fusion.32
  371.7 1.5 copy-done.7
  373.6 5.2 multiply_convert_fusion.1
  378.9 8.9 fusion.50
  387.9 0.9 copy.43
  388.8 0.6 dynamic-slice
  390.1 106.0 %reduce-scatter.21.cloned.1.call-done = bf16[64,4096]{1,0:T(8,128)(2,1)} async-done(((bf16[1024,4096]{1,0:T(8,128)(2,1)}), bf16[64,4096]{1,0:T(8,128)(2,1)}) %reduce-scatter.21.cloned.1.call-update) | async-done | bytes 524304 | tf_op jit(solution)/shard_map/reduce_scatter | solution.py:231
  496.1 107.2 %reduce-scatter.23.cloned.1.call-done = bf16[256,1024]{1,0:T(8,128)(2,1)} async-done(((bf16[4096,1024]{1,0:T(8,128)(2,1)}), bf16[256,1024]{1,0:T(8,128)(2,1)}) %reduce-scatter.23.cloned.1.call-update) | async-done | bytes 524304 | tf_op jit(solution)/shard_map/reduce_scatter | solution.py:234
  603.3 88.6 %reduce-scatter.17.cloned.1.call-done = bf16[64,3072]{1,0:T(8,128)(2,1)} async-done(((bf16[1024,3072]{1,0:T(8,128)(2,1)}), bf16[64,3072]{1,0:T(8,128)(2,1)}) %reduce-scatter.17.cloned.1.call-update) | async-done | bytes 393232 | tf_op jit(solution)/shard_map/reduce_scatter | solution.py:225
  691.9 106.7 %reduce-scatter.15.cloned.1.call-done = bf16[64,4096]{1,0:T(8,128)(2,1)} async-done(((bf16[1024,4096]{1,0:T(8,128)(2,1)}), bf16[64,4096]{1,0:T(8,128)(2,1)}) %reduce-scatter.15.cloned.1.call-update) | async-done | bytes 524304 | tf_op jit(solution)/shard_map/reduce_scatter | solution.py:219
  798.7 10.8 %fusion.38 = bf16[1,640,1024]{2,1,0:T(8,128)(2,1)} fusion(f32[1,640,1024]{2,1,0:T(8,128)} %copy-done.9, bf16[640,4096]{1,0:T(8,128)(2,1)} %get-tuple-element.37, bf16[4096,1024]{1,0:T(8,128)(2,1)} %param.21), kind=kOutput, calls=%fused_computation.60 | convolution fusion | flops 5370019840 | bytes 17563648 | tf_op jit(solution)/shard_map/dot_general | solution.py:42
  809.4 32.6 %all-reduce = bf16[4096]{0:T(1024)(128)(2,1)S(1)} all-reduce(bf16[4096]{0:T(1024)(128)(2,1)S(1)} %convert_element_type.227), channel_id=6, replica_groups=mesh['items'=16,'seq'=2] {'items'}, use_global_device_ids=true, to_apply=%region_21.22.clone | all-reduce | flops 4096 | bytes 16384
  842.2 3.9 fusion.31
  846.0 12.0 %reduce-scatter.29.cloned.1.call-done = bf16[64,8]{1,0:T(8,128)(2,1)} async-done(((bf16[1024,8]{1,0:T(8,128)(2,1)}), bf16[64,8]{1,0:T(8,128)(2,1)}) %reduce-scatter.29.cloned.1.call-update) | async-done | bytes 1040
  858.0 0.8 copy.44
  858.8 4.9 all-reduce.1
  864.3 0.6 convert_element_type.224
  864.9 57.8 %all-reduce.5.cloned.1.call-done = (bf16[64,4096]{1,0:T(8,128)(2,1)}, bf16[64,3072]{1,0:T(8,128)(2,1)}, bf16[64,1024]{1,0:T(8,128)(2,1)}, bf16[64,4096]{1,0:T(8,128)(2,1)}, bf16[256,1024]{1,0:T(8,128)(2,1)}) async-done(((bf16[64,4096]{1,0:T(8,128)(2,1)}, bf16[64,3072]{1,0:T(8,128)(2,1)}, bf16[64,1024]{1,0:T(8,128)(2,1)}, bf16[64,4096]{1,0:T(8,128)(2,1)}, bf16[256,1024]{1,0:T(8,128)(2,1)}), ...) | async-done | bytes 2097168 | tf_op jit(solution)/shard_map/psum | solution.py:240
  922.7 1.7 convert_element_type.232
  924.4 2.2 convert_element_type.226
  926.6 1.9 convert_element_type.230
  928.5 1.0 convert_element_type.234
  929.6 1.1 convert_element_type.236
  (117 shorter events, 4.3 us)
Async XLA Ops:
  7.2 128.1 %copy-start = (bf16[1024,1024]{1,0:T(8,128)(2,1)S(1)}, bf16[1024,1024]{1,0:T(8,128)(2,1)}, u32[]{:S(2)}) copy-start(bf16[1024,1024]{1,0:T(8,128)(2,1)} %param.19) | copy-start | bytes 6291460
  7.2 4.4 copy-start.23
  7.2 59.4 %all-gather.5.cloned.1.call-start = ((), (), s32[]{:S(2)}) async-start(), calls=%async_computation.9 | async-start | bytes 3932160 | tf_op jit(solution)/shard_map/all_gather | solution.py:104
  9.6 8.1 copy-start.19
  9.6 8.1 slice-start.2
  11.6 6.1 copy-start.24
  11.7 5.9 copy-start.17
  11.8 5.9 copy-start.26
  11.8 5.9 copy-start.4
  11.8 5.9 slice-start.3
  17.7 4.9 copy-start.21
  17.7 4.9 copy-start.27
  24.7 83.9 %all-gather.3.cloned.1.call-start = ((), (), s32[]{:S(2)}) async-start(), calls=%async_computation.8 | async-start | bytes 3932160 | tf_op jit(solution)/shard_map/all_gather | solution.py:105
  25.4 306.5 %reduce-scatter.27.cloned.1.call-start = ((), (), s32[]{:S(2)}) async-start(), calls=%async_computation.16 | async-start | bytes 3932160
  28.0 43.0 %copy-start.2 = (bf16[1,640,1024]{1,2,0:T(8,128)(2,1)}, bf16[1,640,1024]{1,2,0:T(8,128)(2,1)S(1)}, u32[]{:S(2)}) copy-start(bf16[1,640,1024]{1,2,0:T(8,128)(2,1)S(1)} %copy.35) | copy-start | bytes 3932164
  113.0 22.3 %copy-start.5 = (bf16[1,640,1024]{2,1,0:T(8,128)(2,1)S(1)}, bf16[1,640,1024]{2,1,0:T(8,128)(2,1)}, u32[]{:S(2)}) copy-start(bf16[1,640,1024]{2,1,0:T(8,128)(2,1)} %param.11) | copy-start | bytes 3932164
  135.3 1.7 copy-start.29
  137.0 35.7 %copy-start.9 = (f32[1,640,1024]{2,1,0:T(8,128)}, f32[1,640,1024]{2,1,0:T(8,128)S(1)}, u32[]{:S(2)}) copy-start(f32[1,640,1024]{2,1,0:T(8,128)S(1)} %get-tuple-element.36) | copy-start | bytes 7864324
  137.4 12.4 %copy-start.13 = (bf16[1,640,1024]{2,1,0:T(8,128)(2,1)S(1)}, bf16[1,640,1024]{2,1,0:T(8,128)(2,1)}, u32[]{:S(2)}) copy-start(bf16[1,640,1024]{2,1,0:T(8,128)(2,1)} %param.12) | copy-start | bytes 3932164
  137.4 26.4 %slice-start = ((s8[8388608]{0:T(1024)(128)(4,1)}), s8[4194304]{0:T(1024)(128)(4,1)S(1)}, s32[]{:S(2)}) async-start(s8[8388608]{0:T(1024)(128)(4,1)} %bitcast.209), calls=%async_computation.19 | async-start | bytes 8388608
  149.8 14.0 %slice-start.1 = ((s8[8388608]{0:T(1024)(128)(4,1)}), s8[4194304]{0:T(1024)(128)(4,1)S(1)}, s32[]{:S(2)}) async-start(s8[8388608]{0:T(1024)(128)(4,1)} %bitcast.209), calls=%async_computation.20 | async-start | bytes 8388608
  173.7 1.5 copy-start.8
  177.5 23.5 %copy-start.11 = (bf16[640,1024]{0,1:T(8,128)(2,1)}, bf16[640,1024]{0,1:T(8,128)(2,1)S(1)}, u32[]{:S(2)}) copy-start(bf16[640,1024]{0,1:T(8,128)(2,1)S(1)} %copy.37) | copy-start | bytes 3932164
  217.7 124.6 %reduce-scatter.25.cloned.1.call-start = ((), (), s32[]{:S(2)}) async-start(), calls=%async_computation.15 | async-start | bytes 3932160
  217.7 3.3 copy-start.10
  217.7 3.7 copy-start.12
  221.4 33.9 %copy-start.3 = (bf16[1,640,1024]{1,2,0:T(8,128)(2,1)S(1)}, bf16[1,640,1024]{1,2,0:T(8,128)(2,1)}, u32[]{:S(2)}) copy-start(bf16[1,640,1024]{1,2,0:T(8,128)(2,1)} %copy-done.2) | copy-start | bytes 3932164
  286.5 1.3 copy-start.30
  286.5 103.6 %reduce-scatter.19.cloned.1.call-start = ((), (), s32[]{:S(2)}) async-start(), calls=%async_computation.12 | async-start | bytes 2228224 | tf_op jit(solution)/shard_map/reduce_scatter | solution.py:228
  292.6 203.5 %reduce-scatter.21.cloned.1.call-start = ((), (), s32[]{:S(2)}) async-start(), calls=%async_computation.13 | async-start | bytes 8912896 | tf_op jit(solution)/shard_map/reduce_scatter | solution.py:231
  304.9 1.3 copy-start.14
  305.0 298.4 %reduce-scatter.23.cloned.1.call-start = ((), (), s32[]{:S(2)}) async-start(), calls=%async_computation.14 | async-start | bytes 8912896 | tf_op jit(solution)/shard_map/reduce_scatter | solution.py:234
  317.8 374.2 %reduce-scatter.17.cloned.1.call-start = ((), (), s32[]{:S(2)}) async-start(), calls=%async_computation.11 | async-start | bytes 6684672 | tf_op jit(solution)/shard_map/reduce_scatter | solution.py:225
  346.6 6.2 copy-start.6
  346.6 6.2 copy-start.20
  346.6 6.2 copy-start.22
  346.6 6.3 copy-start.25
  346.6 6.3 copy-start.28
  362.7 435.9 %reduce-scatter.15.cloned.1.call-start = ((), (), s32[]{:S(2)}) async-start(), calls=%async_computation.10 | async-start | bytes 8912896 | tf_op jit(solution)/shard_map/reduce_scatter | solution.py:219
  371.7 1.5 copy-start.7
  371.7 1.9 copy-start.18
  378.9 479.2 %reduce-scatter.29.cloned.1.call-start = ((), (), s32[]{:S(2)}) async-start(), calls=%async_computation.17 | async-start | bytes 278528
  378.9 9.9 %copy-start.31 = (u32[32]{0:T(128)S(1)}, u32[32]{0:T(128)}, u32[]{:S(2)}) copy-start(u32[32]{0:T(128)} %constant.42) | copy-start | bytes 388
  388.8 533.9 %all-reduce.5.cloned.1.call-start = ((), (), s32[]{:S(2)}) async-start(), calls=%async_computation.18 | async-start | bytes 4194304 | tf_op jit(solution)/shard_map/psum | solution.py:240
  922.7 5.9 copy-start.16
  922.7 6.9 copy-start.15
  924.4 6.3 copy-start.1
Sparse Core Ops, SparseCore 0:
  24.8 41.7 all-gather.4
  68.1 38.9 all-gather.2
  217.8 37.9 reduce-scatter.26
  286.6 37.7 reduce-scatter.24
  328.0 61.7 reduce-scatter.18
  393.7 102.4 reduce-scatter.20
  500.2 103.0 reduce-scatter.22
  607.3 84.6 reduce-scatter.16
  696.0 102.5 reduce-scatter.14
  802.6 55.3 reduce-scatter.28
  860.6 62.0 all-reduce.4
where the time goes:
time: 943 us; the launch traced here: 938 us
  waiting for transfers between devices  518 us (55%)
  matrix products  242 us (26%)
  local copies, waits for them, and re-layouts  77.7 us (8%)
  other arithmetic  44.1 us (5%)
  blocking collectives  37.6 us (4%)
  between operations  16.9 us (2%)
    reduce_scatter x1, waiting for transfers between devices, per_device(): lax.psum_scatter(grad_w_down.astype(jnp.bfloat16), 'items', scatter_dimen...  107 us
    reduce_scatter x1, waiting for transfers between devices, per_device(): lax.psum_scatter(grad_ada.astype(jnp.bfloat16), 'items', scatter_dimensio...  107 us
    reduce_scatter x1, waiting for transfers between devices, per_device(): lax.psum_scatter(grad_w_up.astype(jnp.bfloat16), 'items', scatter_dimensi...  106 us
    reduce_scatter x1, waiting for transfers between devices, per_device(): lax.psum_scatter(grad_w_qkv.astype(jnp.bfloat16), 'items', scatter_dimens...  88.6 us
    unnamed x84, local copies, waits for them, and re-layouts  62.4 us
    psum x1, waiting for transfers between devices, per_device(): lax.psum(parts[1].astype(jnp.bfloat16), 'seq').astype(jnp.float32)  57.8 us
    all_gather x1, waiting for transfers between devices, per_device(): key_piece = lax.all_gather(key_local, 'seq', axis=1, tiled=True)  38.5 us
    dot_general x4, matrix products, outer_sum(): lax.dot_general(left_flat, right_flat, (((0,), (0,)), ((), ())), preferre...  38.4 us
  transfers between devices with their start and end apart: 11, of which 7 were waited for; matrix products, arithmetic and copies ran while one was open for 24% of the time, Pallas kernels for 0%

commit v1 on v0

v1 whole, which is shorter than its diff:
```python
import functools

import jax
import jax.numpy as jnp
from jax import lax
from jax.experimental import pallas as pl
from jax.experimental.pallas import tpu as pltpu
from jax.sharding import PartitionSpec as P

HEADS = 16


EPS = 1e-05
NEGATIVE = -1e30
SQRT_HALF = 0.7071067811865476
INV_SQRT_TAU = 0.3989422804014327
HIGHEST = lax.Precision.HIGHEST


def normalize(values):
    mean = jnp.mean(values, -1, keepdims=True)
    centered = values - mean
    inverse = lax.rsqrt(jnp.mean(centered * centered, -1, keepdims=True) + EPS)
    return (centered * inverse, inverse)


def norm_back(grad, normed, inverse):
    first = jnp.mean(grad, -1, keepdims=True)
    second = jnp.mean(grad * normed, -1, keepdims=True)
    return (grad - first - normed * second) * inverse


def gelu_exact(values):
    return 0.5 * values * (1.0 + lax.erf(values * SQRT_HALF))


def gelu_slope(values):
    return (
        0.5 * (1.0 + lax.erf(values * SQRT_HALF))
        + values * jnp.exp(-0.5 * values * values) * INV_SQRT_TAU
    )


def project(left, weight):
    flat = left.reshape(-1, left.shape[-1])
    result = jnp.dot(flat, weight, preferred_element_type=jnp.float32)
    return result.reshape(left.shape[:-1] + (weight.shape[1],))


def back_project(grad, weight):
    flat = grad.reshape(-1, grad.shape[-1])
    result = lax.dot_general(
        flat, weight, (((1,), (1,)), ((), ())), preferred_element_type=jnp.float32
    )
    return result.reshape(grad.shape[:-1] + (weight.shape[0],))


BIG = 1e30

def split3(x):
    hi = x.astype(jnp.bfloat16).astype(jnp.float32)
    rest = x - hi
    mid = rest.astype(jnp.bfloat16).astype(jnp.float32)
    return hi, mid, rest - mid

def dot(a, b, ca, cb):
    return lax.dot_general(a, b, (((ca,), (cb,)), ((), ())), preferred_element_type=jnp.float32)


def fwd_kernel(rows, blocks, lim_ref, q_ref, ko_ref, vo_ref, kt_ref, vt_ref, o_ref, lse_ref):
    lane = lax.broadcasted_iota(jnp.int32, (1, 128), 1)
    low = lane < 64
    row = lax.broadcasted_iota(jnp.int32, (rows, 1), 0)
    q = q_ref[...].astype(jnp.float32) * 0.125
    outs, lses = [], []
    for h in range(2):
        own = low if h == 0 else jnp.logical_not(low)
        first = 64 * (1 - h)
        qa = jnp.where(own, q, jnp.where(lane == first, 1.0, 0.0)).astype(jnp.bfloat16)
        scores, values = [], []
        for j in range(blocks):
            k = ko_ref[...] if j == 0 else kt_ref[pl.ds((j - 1) * rows, rows), :]
            v = vo_ref[...] if j == 0 else vt_ref[pl.ds((j - 1) * rows, rows), :]
            bias = jnp.where(row < lim_ref[j], 0.0, -BIG)
            ka = jnp.where(own, k.astype(jnp.float32), jnp.where(lane == first, bias, 0.0)).astype(jnp.bfloat16)
            va = jnp.where(own, v.astype(jnp.float32), 1.0).astype(jnp.bfloat16)
            scores.append(dot(qa, ka, 1, 1))
            values.append(va)
        top = functools.reduce(jnp.maximum, [jnp.max(s, -1, keepdims=True) for s in scores])
        total = None
        for s, va in zip(scores, values):
            p = jnp.exp(s - top).astype(jnp.bfloat16)
            part = dot(p, va, 1, 0)
            total = part if total is None else total + part
        outs.append(total / pltpu.roll(total, 64, 1))
        lses.append(top + jnp.log(total))
    o_ref[...] = jnp.where(low, outs[0], outs[1]).astype(o_ref.dtype)
    lse_ref[...] = jnp.where(low, lses[1], lses[0])


def bwd_kernel(rows, blocks, lim_ref, q_ref, ko_ref, vo_ref, kt_ref, vt_ref, do_ref, o_ref, lse_ref,
               dq_ref, dko_ref, dvo_ref, dkt_ref, dvt_ref):
    lane = lax.broadcasted_iota(jnp.int32, (1, 128), 1)
    low = lane < 64
    row = lax.broadcasted_iota(jnp.int32, (rows, 1), 0)
    q = q_ref[...].astype(jnp.float32) * 0.125
    qs = q.astype(jnp.bfloat16)
    do_low = do_ref[...]
    do = do_low.astype(jnp.float32)
    prod = do * o_ref[...].astype(jnp.float32)
    lh, lm, ll = split3(lse_ref[...])
    heads = []
    for h in range(2):
        own = low if h == 0 else jnp.logical_not(low)
        f = 64 * (1 - h)
        delta = jnp.sum(jnp.where(own, prod, 0.0), -1, keepdims=True)
        dh, dm, dl = split3(delta)
        qa = jnp.where(own, q, jnp.where(lane == f, 1.0, jnp.where(lane == f + 1, -lh, jnp.where(lane == f + 2, -lm, jnp.where(lane == f + 3, -ll, 0.0))))).astype(jnp.bfloat16)
        doa = jnp.where(own, do, jnp.where(lane == f, -dh, jnp.where(lane == f + 1, -dm, jnp.where(lane == f + 2, -dl, 0.0)))).astype(jnp.bfloat16)
        kone = jnp.where((lane > f) & (lane <= f + 3), 1.0, 0.0)
        vone = jnp.where((lane >= f) & (lane < f + 3), 1.0, 0.0)
        dq = None
        res = []
        for j in range(blocks):
            k = ko_ref[...] if j == 0 else kt_ref[pl.ds((j - 1) * rows, rows), :]
            v = vo_ref[...] if j == 0 else vt_ref[pl.ds((j - 1) * rows, rows), :]
            bias = jnp.where(row < lim_ref[j], 0.0, -BIG)
            ka = jnp.where(own, k.astype(jnp.float32), jnp.where(lane == f, bias, kone)).astype(jnp.bfloat16)
            va = jnp.where(own, v.astype(jnp.float32), vone).astype(jnp.bfloat16)
            pt = jnp.exp(dot(ka, qa, 1, 1))
            dpt = dot(va, doa, 1, 1)
            dst = (pt * dpt).astype(jnp.bfloat16)
            dv = dot(pt.astype(jnp.bfloat16), do_low, 1, 0)
            dk = dot(dst, qs, 1, 0)
            part = dot(dst, k, 0, 0)
            dq = part if dq is None else dq + part
            res.append((dk, dv))
        heads.append((dq, res))
    dq_ref[...] = (jnp.where(low, heads[0][0], heads[1][0]) * 0.125).astype(dq_ref.dtype)
    for j in range(blocks):
        dk = jnp.where(low, heads[0][1][j][0], heads[1][1][j][0]).astype(dko_ref.dtype)
        dv = jnp.where(low, heads[0][1][j][1], heads[1][1][j][1]).astype(dko_ref.dtype)
        if j == 0:
            dko_ref[...] = dk
            dvo_ref[...] = dv
        else:
            dkt_ref[pl.ds((j - 1) * rows, rows), :] = dk
            dvt_ref[pl.ds((j - 1) * rows, rows), :] = dv


def specs_of(rows, others, width):
    pairs = width // 128
    place = lambda count, skip: pl.BlockSpec((count, 128), lambda i, lim: (0, i + skip))
    inputs = [place(rows, 0), place(rows, pairs), place(rows, 2 * pairs), place(others, 0), place(others, pairs)]
    return inputs, place(rows, 0), place(others, 0)


def attend(lim, qkv, kv_rest, width):
    rows, others = qkv.shape[0], kv_rest.shape[0]
    blocks = 1 + others // rows
    inputs, own, oth = specs_of(rows, others, width)
    keys = rows + others
    return pl.pallas_call(
        functools.partial(fwd_kernel, rows, blocks),
        grid_spec=pltpu.PrefetchScalarGridSpec(num_scalar_prefetch=1, grid=(width // 128,),
            in_specs=inputs, out_specs=[own, own]),
        out_shape=[jax.ShapeDtypeStruct((rows, width), jnp.bfloat16), jax.ShapeDtypeStruct((rows, width), jnp.float32)],
        compiler_params=pltpu.CompilerParams(vmem_limit_bytes=56 << 20),
        cost_estimate=pl.CostEstimate(flops=16 * rows * keys * width, transcendentals=rows * keys * width // 64,
            bytes_accessed=2 * width * (2 * rows + 2 * keys) + 4 * rows * width),
    )(lim, qkv, qkv, qkv, kv_rest, kv_rest)


def attend_back(lim, qkv, kv_rest, do, o, lse):
    (rows, width), others = do.shape, kv_rest.shape[0]
    blocks = 1 + others // rows
    inputs, own, oth = specs_of(rows, others, width)
    keys = rows + others
    s = lambda n: jax.ShapeDtypeStruct((n, width), jnp.bfloat16)
    return pl.pallas_call(
        functools.partial(bwd_kernel, rows, blocks),
        grid_spec=pltpu.PrefetchScalarGridSpec(num_scalar_prefetch=1, grid=(width // 128,),
            in_specs=inputs + [own, own, own], out_specs=[own, own, own, oth, oth]),
        out_shape=[s(rows), s(rows), s(rows), s(others), s(others)],
        compiler_params=pltpu.CompilerParams(vmem_limit_bytes=56 << 20),
        cost_estimate=pl.CostEstimate(flops=40 * rows * keys * width, transcendentals=rows * keys * width // 64,
            bytes_accessed=2 * width * (4 * rows + 4 * keys) + 4 * rows * width),
    )(lim, qkv, qkv, qkv, kv_rest, kv_rest, do, o, lse)


def outer_kernel(plan, halves, first_tiles, side_ref, *refs):
    lefts, plan_rights, outs, turned = refs[: plan[0]], refs[plan[0] : plan[1]], refs[plan[1] : plan[1] + 4], refs[plan[1] + 4 :]
    step = pl.program_id(0)

    @pl.when(step == 0)
    def _():
        for left, flip in zip(lefts, turned):
            flip[...] = left[...].T

    at = 0
    place = 0
    for tiles, terms in plan[2]:
        rights = plan_rights[place : place + len(terms)]
        place += len(terms)

        @pl.when((step >= at) & (step < at + tiles))
        def _(rights=rights, terms=terms):
            total = None
            for which, right in zip(terms, rights):
                part = dot(turned[which][...], right[...], 1, 0)
                total = part if total is None else total + part
            rows, columns = total.shape
            split = total.astype(jnp.bfloat16).reshape(halves, 2, rows // (2 * halves), columns)
            even = side_ref[0] == 0
            keep = jnp.where(even, split[:, 0], split[:, 1])
            send = jnp.where(even, split[:, 1], split[:, 0])

            @pl.when(step < first_tiles)
            def _():
                outs[0][...] = send
                outs[1][...] = keep

            @pl.when(step >= first_tiles)
            def _():
                outs[2][...] = send
                outs[3][...] = keep

        at += tiles


def outer(side, lefts, segments, parts, tile):
    rows = lefts[0].shape[1]
    halves = parts // 2
    block = rows // parts
    width = sum(segment[0][1].shape[1] for segment in segments)
    steps = width // tile
    first_tiles = steps // 2
    in_specs = [pl.BlockSpec(left.shape, lambda i, s: (0, 0)) for left in lefts]
    operands = list(lefts)
    plan = []
    at = 0
    flops = 0
    for segment in segments:
        tiles = segment[0][1].shape[1] // tile
        for which, right in segment:
            in_specs.append(
                pl.BlockSpec(
                    (right.shape[0], tile),
                    lambda i, s, at=at, tiles=tiles: (0, jnp.clip(i - at, 0, tiles - 1)),
                )
            )
            operands.append(right)
            flops += 2 * rows * right.shape[0] * right.shape[1]
        plan.append((tiles, tuple(which for which, _ in segment)))
        at += tiles
    first = pl.BlockSpec((halves, block, tile), lambda i, s: (0, 0, jnp.minimum(i, first_tiles - 1)))
    second = pl.BlockSpec((halves, block, tile), lambda i, s: (0, 0, jnp.maximum(i - first_tiles, 0)))
    shape = lambda count: jax.ShapeDtypeStruct((halves, block, count * tile), jnp.bfloat16)
    moved = sum(2 * operand.size for operand in operands) + 2 * rows * width
    return pl.pallas_call(
        functools.partial(
            outer_kernel, (len(lefts), len(operands), tuple(plan)), halves, first_tiles
        ),
        grid_spec=pltpu.PrefetchScalarGridSpec(
            num_scalar_prefetch=1,
            grid=(steps,),
            in_specs=in_specs,
            out_specs=[first, first, second, second],
            scratch_shapes=[pltpu.VMEM(left.shape[::-1], jnp.bfloat16) for left in lefts],
        ),
        out_shape=[shape(first_tiles)] * 2 + [shape(steps - first_tiles)] * 2,
        compiler_params=pltpu.CompilerParams(vmem_limit_bytes=58 << 20),
        cost_estimate=pl.CostEstimate(flops=flops, transcendentals=0, bytes_accessed=moved),
    )(side, *operands)


def swap(values, axis, bit):
    size = lax.axis_size(axis)
    return lax.ppermute(values, axis, [(i, i ^ bit) for i in range(size)])


def bits_of(axis):
    size = lax.axis_size(axis)
    return [1 << place for place in range(size.bit_length() - 1)]


def add_low(left, right):
    return (left.astype(jnp.float32) + right.astype(jnp.float32)).astype(jnp.bfloat16)


def half_of(values, dim, which):
    return lax.dynamic_index_in_dim(values, which, dim, keepdims=False)


def reduce_rows(keep, got, axis):
    me = lax.axis_index(axis)
    for bit in bits_of(axis)[1:]:
        mine = jnp.bitwise_and(me // bit, 1)
        shape = keep.shape
        view = (shape[0] // 2, 2) + shape[1:]
        keep, got = keep.reshape(view), got.reshape(view)
        send = add_low(half_of(keep, 1, 1 - mine), half_of(got, 1, 1 - mine))
        keep = add_low(half_of(keep, 1, mine), half_of(got, 1, mine))
        got = swap(send, axis, bit)
    return keep, got


def finish(pieces, rows_axis, seq_axis):
    send_a, keep_a, send_b, keep_b = pieces
    got_a = swap(send_a, rows_axis, 1)
    got_b = swap(send_b, rows_axis, 1)
    keep_a, got_a = reduce_rows(keep_a, got_a, rows_axis)
    total_a = (keep_a.astype(jnp.float32) + got_a.astype(jnp.float32))[0]
    for bit in bits_of(seq_axis):
        low = total_a.astype(jnp.bfloat16)
        total_a = low.astype(jnp.float32) + swap(low, seq_axis, bit).astype(jnp.float32)
    me = lax.axis_index(seq_axis)
    for bit in bits_of(seq_axis):
        mine = jnp.bitwise_and(me // bit, 1)
        width = keep_b.shape[-1] // 2
        cut = lambda values, which: lax.dynamic_slice_in_dim(values, which * width, width, 2)
        send = add_low(cut(keep_b, 1 - mine), cut(got_b, 1 - mine))
        keep_b = add_low(cut(keep_b, mine), cut(got_b, mine))
        got_b = swap(send, seq_axis, bit)
    keep_b, got_b = reduce_rows(keep_b, got_b, rows_axis)
    total_b = add_low(keep_b, got_b)[0]
    for bit in reversed(bits_of(seq_axis)):
        mine = jnp.bitwise_and(me // bit, 1)
        other = swap(total_b, seq_axis, bit)
        total_b = jnp.where(
            mine == 0,
            jnp.concatenate([total_b, other], -1),
            jnp.concatenate([other, total_b], -1),
        )
    return jnp.concatenate([total_a, total_b.astype(jnp.float32)], -1)


def gather_items(values, axis):
    me = lax.axis_index(axis)
    for bit in bits_of(axis):
        other = swap(values, axis, bit)
        mine = jnp.bitwise_and(me // bit, 1)
        values = jnp.where(
            mine == 0, jnp.concatenate([values, other]), jnp.concatenate([other, values])
        )
    return values


def per_device(
    frames,
    cotangent,
    section,
    prompt_len,
    section_embed,
    ada_proj,
    ada_bias,
    w_qkv,
    w_out,
    w_up,
    w_down,
):
    _, row_count, width = frames.shape
    frames, cotangent = frames[0], cotangent[0]
    seq_size = lax.axis_size("seq")
    item_size = lax.axis_size("items")
    seq_me, item_me = lax.axis_index("seq"), lax.axis_index("items")
    side = jnp.bitwise_and(item_me, 1).astype(jnp.int32).reshape(1)
    turns = list(range(1, seq_size))
    fetch = lambda values, turn: lax.ppermute(
        values, "seq", [((i + turn) % seq_size, i) for i in range(seq_size)]
    )
    give = lambda values, turn: lax.ppermute(
        values, "seq", [(i, (i + turn) % seq_size) for i in range(seq_size)]
    )
    others = [fetch(frames, turn) for turn in turns]
    sources = jnp.stack([(seq_me + turn) % seq_size for turn in [0] + turns])
    limits = jnp.where(sources == 0, prompt_len[0], row_count).astype(jnp.int32)

    section_count = section_embed.shape[0]
    onehot = (section[:, None] == jnp.arange(section_count, dtype=jnp.int32)[None, :]).astype(
        jnp.float32
    )
    cond = jnp.dot(onehot, section_embed, precision=HIGHEST)
    modul = jnp.dot(cond, ada_proj.astype(jnp.float32), precision=HIGHEST) + ada_bias[None, :]
    scale_one, shift_one, scale_two, shift_two = jnp.split(modul, 4, axis=-1)
    inputs = frames.astype(jnp.float32)
    normed_one, inv_one = normalize(inputs)
    modulate = lambda normed: (normed * (1.0 + scale_one) + shift_one).astype(jnp.bfloat16)
    attn_in = modulate(normed_one)
    qkv = project(attn_in, w_qkv).astype(jnp.bfloat16)
    rest = jnp.concatenate(others) if len(others) > 1 else others[0]
    normed_rest, _ = normalize(rest.astype(jnp.float32))
    attn_rest = modulate(normed_rest)
    kv_rest = project(attn_rest, w_qkv[:, width:]).astype(jnp.bfloat16)
    att, lse = attend(limits, qkv, kv_rest, width)
    mid = inputs + project(att, w_out)
    normed_two, inv_two = normalize(mid)
    ffn_in = (normed_two * (1.0 + scale_two) + shift_two).astype(jnp.bfloat16)
    upper = project(ffn_in, w_up)
    act = gelu_exact(upper).astype(jnp.bfloat16)
    out_frames = (mid + project(act, w_down)).astype(jnp.bfloat16)

    grad_out = cotangent.astype(jnp.float32)
    down_pieces = outer(side, [act], [[(0, cotangent)]], item_size, 256)
    grad_upper = (back_project(cotangent, w_down) * gelu_slope(upper)).astype(jnp.bfloat16)
    up_pieces = outer(side, [ffn_in], [[(0, grad_upper)]], item_size, 512)
    grad_ffn_in = back_project(grad_upper, w_up)
    grad_scale_two = jnp.sum(grad_ffn_in * normed_two, 0)
    grad_shift_two = jnp.sum(grad_ffn_in, 0)
    grad_mid = grad_out + norm_back(grad_ffn_in * (1.0 + scale_two), normed_two, inv_two)
    grad_mid_low = grad_mid.astype(jnp.bfloat16)
    out_pieces = outer(side, [att], [[(0, grad_mid_low)]], item_size, 512)
    grad_att = back_project(grad_mid_low, w_out).astype(jnp.bfloat16)
    grad_query, grad_key, grad_value, key_rest, value_rest = attend_back(
        limits, qkv, kv_rest, grad_att, att, lse
    )
    qkv_pieces = outer(
        side,
        [attn_in, attn_rest],
        [
            [(0, grad_query)],
            [(0, grad_key), (1, key_rest)],
            [(0, grad_value), (1, value_rest)],
        ],
        item_size,
        512,
    )
    w_key, w_value = w_qkv[:, width : 2 * width], w_qkv[:, 2 * width :]
    share = back_project(key_rest, w_key) + back_project(value_rest, w_value)
    grad_rest = [
        give(share[i * row_count : (i + 1) * row_count].astype(jnp.bfloat16), turn)
        for i, turn in enumerate(turns)
    ]
    partial = (
        back_project(grad_query, w_qkv[:, :width])
        + back_project(grad_key, w_key)
        + back_project(grad_value, w_value)
    )
    grad_scale_one = jnp.sum(partial * normed_one, 0) + jnp.sum(share * normed_rest, 0)
    grad_shift_one = jnp.sum(partial, 0) + jnp.sum(share, 0)
    grad_attn_in = partial
    for got in grad_rest:
        grad_attn_in = grad_attn_in + got.astype(jnp.float32)
    frames_grad = (
        grad_mid + norm_back(grad_attn_in * (1.0 + scale_one), normed_one, inv_one)
    ).astype(jnp.bfloat16)

    sum_down = finish(down_pieces, "items", "seq")
    sum_up = finish(up_pieces, "items", "seq")
    sum_out = finish(out_pieces, "items", "seq")
    sum_qkv = finish(qkv_pieces, "items", "seq")

    grad_modul = jnp.concatenate(
        [grad_scale_one, grad_shift_one, grad_scale_two, grad_shift_two]
    )[None, :]
    for bit in bits_of("seq"):
        grad_modul = grad_modul + swap(grad_modul, "seq", bit)
    tagged = jnp.concatenate([grad_modul, jnp.pad(onehot, ((0, 0), (0, 128 - section_count)))], -1)
    tagged = gather_items(tagged, "items")
    modul_all, onehot_all = tagged[:, : 4 * width], tagged[:, 4 * width :][:, :section_count]
    block = width // item_size
    own_embed = lax.dynamic_slice_in_dim(section_embed, item_me * block, block, 1)
    own_cond = jnp.dot(onehot_all, own_embed, precision=HIGHEST)
    sum_ada = lax.dot_general(own_cond, modul_all, (((0,), (0,)), ((), ())), precision=HIGHEST)
    sum_bias = jnp.sum(
        lax.dynamic_slice_in_dim(modul_all, item_me * 4 * block, 4 * block, 1), 0
    )
    own_ada = lax.dynamic_slice_in_dim(ada_proj, item_me * block, block, 0).astype(jnp.float32)
    grad_cond = lax.dot_general(modul_all, own_ada, (((1,), (1,)), ((), ())), precision=HIGHEST)
    sum_embed = lax.dot_general(
        onehot_all, grad_cond, (((0,), (0,)), ((), ())), precision=HIGHEST
    )
    return (
        out_frames[None],
        frames_grad[None],
        sum_embed,
        sum_ada,
        sum_bias,
        sum_qkv,
        sum_out,
        sum_up,
        sum_down,
    )


def solution(mesh):
    in_specs = (
        P("items", "seq", None),
        P("items", "seq", None),
        P("items"),
        P("items"),
        P(),
        P(),
        P(),
        P(),
        P(),
        P(),
        P(),
    )
    out_specs = (
        P("items", "seq", None),
        P("items", "seq", None),
        P(None, "items"),
        P("items", None),
        P("items"),
        P("items", None),
        P("items", None),
        P("items", None),
        P("items", None),
    )
    return jax.shard_map(
        per_device, mesh=mesh, in_specs=in_specs, out_specs=out_specs, check_vma=False
    )
```

time: 943 us -> 455 us (0.48)
  waiting for transfers between devices: 518 us -> 157 us
  matrix products: 242 us -> 95.2 us
  Pallas kernels: 0 us -> 111 us
  local copies, waits for them, and re-layouts: 77.7 us -> 0.18 us
  starting transfers between devices: 1.26 us -> 47.3 us
  blocking collectives: 37.6 us -> 0 us
  between operations: 16.9 us -> 3.19 us
  other arithmetic: 44.1 us -> 32.4 us
    reduce_scatter x5 -> x0, waiting for transfers between devices: 409 us -> none  [the longest x1 107 us: per_device(): lax.psum_scatter(grad_w_down.astype(jnp.bfloat16), 'items', scatter_dimen...]
    dot_general x12 -> x5, matrix products: 180 us -> 11 us  [the longest x1 5.77 us: per_device(): jnp.dot(cond, ada_proj.astype(jnp.float32), precision=HIGHEST)]
    ppermute x0 -> x51, waiting for transfers between devices: none -> 157 us  [the longest x49 138 us: swap(): return lax.ppermute(values, axis, [(i, i ^ bit) for i in range(size)])]
    pallas_call x0 -> x6, Pallas kernels: none -> 111 us  [the longest x4 47.9 us: outer(): pl.pallas_call(functools.partial(outer_kernel, (len(lefts), len(operands)...]
    unnamed x84 -> x70, local copies, waits for them, and re-layouts: 62.4 us -> 0.16 us
    psum x1 -> x0, waiting for transfers between devices: 57.8 us -> none  [per_device(): lax.psum(parts[1].astype(jnp.bfloat16), 'seq').astype(jnp.float32)]
    ppermute x0 -> x51, starting transfers between devices: none -> 47.3 us  [the longest x49 42.5 us: swap(): return lax.ppermute(values, axis, [(i, i ^ bit) for i in range(size)])]
    all_gather x2 -> x0, waiting for transfers between devices: 38.5 us -> none  [the longest x1 38.5 us: per_device(): key_piece = lax.all_gather(key_local, 'seq', axis=1, tiled=True)]
  transfers between devices with their start and end apart: 11 -> 51, of which waited for: 7 -> 25; matrix products, arithmetic and copies ran while one was open for 24% -> 12% of each run, Pallas kernels for 0% -> 16%
where the time goes in v1:
time: 455 us; the launch traced here: 446 us
  waiting for transfers between devices  157 us (35%)
  Pallas kernels  111 us (24%)
  matrix products  95.2 us (21%)
  starting transfers between devices  47.3 us (10%)
  other arithmetic  32.4 us (7%)
    ppermute x49, waiting for transfers between devices, swap(): return lax.ppermute(values, axis, [(i, i ^ bit) for i in range(size)])  138 us
    pallas_call x4, Pallas kernels, outer(): pl.pallas_call(functools.partial(outer_kernel, (len(lefts), len(operands)...  47.9 us
    dot_general x8, matrix products, back_project(): lax.dot_general(flat, weight, (((1,), (1,)), ((), ())), preferred_element...  47.1 us
    ppermute x49, starting transfers between devices, swap(): return lax.ppermute(values, axis, [(i, i ^ bit) for i in range(size)])  42.5 us
    pallas_call x1, Pallas kernels, attend_back(): pl.pallas_call(functools.partial(bwd_kernel, rows, blocks), grid_spec=plt...  41.3 us
    dot_general x5, matrix products, project(): result = jnp.dot(flat, weight, preferred_element_type=jnp.float32)  36.2 us
    pallas_call x1, Pallas kernels, attend(): pl.pallas_call(functools.partial(fwd_kernel, rows, blocks), grid_spec=plt...  22.2 us
    ppermute x1, waiting for transfers between devices, per_device(): lax.ppermute(values, 'seq', [((i + turn) % seq_size, i) for i in range(se...  19 us
  transfers between devices with their start and end apart: 51, of which 25 were waited for; matrix products, arithmetic and copies ran while one was open for 12% of the time, Pallas kernels for 16%

profile of v1, /device:TPU:0, one launch (start us, length us, event | category | flops | bytes accessed | tf_op | source)
XLA Modules:
  0.0 446.2 jit_solution(9267339841444462280)
XLA Ops:
  0.7 3.0 collective-permute-start
  5.3 5.8 %fusion.114 = f32[1,4096]{1,0:T(1,128)S(1)} fusion(f32[1024,1]{0,1:T(1,128)S(1)} %convolution_bitcast_fusion, bf16[1024,4096]{1,0:T(8,128)(2,1)} %param.16), kind=kOutput, calls=%fused_computation.228 | convolution fusion | flops 50331648 | bytes 8409088 | tf_op jit(solution)/shard_map/dot_general | solution.py:384
  13.8 19.0 %collective-permute-done = bf16[640,1024]{1,0:T(8,128)(2,1)} collective-permute-done((bf16[640,1024]{1,0:T(8,128)(2,1)}, bf16[640,1024]{1,0:T(8,128)(2,1)}, u32[]{:S(2)}, u32[]{:S(2)}) %collective-permute-start) | collective-permute-done | bytes 1310752 | tf_op jit(solution)/shard_map/ppermute | solution.py:369
  32.8 1.6 convert_reduce_fusion.1
  34.4 1.9 fusion.33
  36.3 2.5 fusion.22
  38.9 4.2 fusion.8.kt_ref.vt_ref
  43.1 5.8 %convolution_convert_fusion.q_ref.ko_ref.vo_ref = bf16[640,3072]{1,0:T(8,128)(2,1)} fusion(bf16[640,1024]{1,0:T(8,128)(2,1)S(1)} %get-tuple-element.113.refs_0_, bf16[1024,3072]{1,0:T(8,128)(2,1)S(1)} %copy-done.24), kind=kOutput, calls=%fused_computation.9 | convolution fusion | flops 4028497920 | bytes 11534336 | tf_op jit(solution)/shard_map/dot_general | solution.py:46
  48.9 22.2 %shard_map.178 = (bf16[640,1024]{1,0:T(8,128)(2,1)}, f32[640,1024]{1,0:T(8,128)}) custom-call(s32[2]{0:T(128)} %compare_select_fusion.lim_ref, bf16[640,3072]{1,0:T(8,128)(2,1)} %convolution_convert_fusion.q_ref.ko_ref.vo_ref, bf16[640,3072]{1,0:T(8,128)(2,1)} %convolution_convert_fusion.q_ref.ko_ref.vo_ref, ...), custom_call_target="tpu_custom_call" | custom-call | flops 13421772800 | bytes 10485760 | tf_op jit(solution)/shard_map/pallas_call | solution.py:163
  71.1 2.9 fusion.113
  74.9 12.4 %multiply_convert_fusion = (bf16[640,4096]{1,0:T(8,128)(2,1)}, f32[640,4096]{1,0:T(8,128)}) fusion(bf16[640,1024]{1,0:T(8,128)(2,1)S(1)} %add_convert_fusion.1.refs_0_, bf16[1024,4096]{1,0:T(8,128)(2,1)} %param.20), kind=kOutput, calls=%fused_computation.7 | convolution fusion | flops 5381816320 | bytes 25427968 | tf_op jit(solution)/shard_map/dot_general | solution.py:46
  87.4 12.1 %fusion.5.refs_1_ = bf16[640,4096]{1,0:T(8,128)(2,1)S(1)} fusion(f32[640,4096]{1,0:T(8,128)} %get-tuple-element.117, bf16[4096,1024]{1,0:T(8,128)(2,1)} %param.21, bf16[1,640,1024]{2,1,0:T(8,128)(2,1)S(1)} %copy-done.10), kind=kOutput, calls=%fused_computation.6 | convolution fusion | flops 5394923520 | bytes 25427968 | tf_op jit(solution)/shard_map/dot_general | solution.py:52
  99.4 10.7 %multiply_reduce_fusion = (f32[1024]{0:T(1024)S(1)}, f32[640]{0:T(1024)S(1)}, f32[640]{0:T(1024)S(1)}, f32[1024]{0:T(1024)S(1)}, f32[640,1024]{1,0:T(8,128)S(1)}) fusion(f32[640,1024]{1,0:T(8,128)S(1)} %get-tuple-element.115, f32[640]{0:T(1024)S(1)} %add_rsqrt_fusion, f32[640]{0:T(1024)S(1)} %broadcast_multiply_fusion.4, f32[1024]{0:T(1024)S(1)} %bitcast.229, ...), kind=kOutput, calls=%fused_computation.41 | convolution fusion | flops 5374604288 | bytes 18896896 | tf_op jit(solution)/shard_map/dot_general | solution.py:52
  110.1 2.4 fusion.112
  112.6 2.6 convolution_convert_fusion.1.do_ref
  115.2 5.4 %shard_map.181 = (bf16[8,64,512]{2,1,0:T(8,128)(2,1)}, bf16[8,64,512]{2,1,0:T(8,128)(2,1)}, bf16[8,64,512]{2,1,0:T(8,128)(2,1)}, bf16[8,64,512]{2,1,0:T(8,128)(2,1)}) custom-call(s32[1]{0:T(128)} %bitcast.18.side_ref, bf16[640,1024]{1,0:T(8,128)(2,1)} %get-tuple-element.32.o_ref.refs_0_, bf16[640,1024]{1,0:T(8,128)(2,1)} %copy-done.13), custom_call_target="tpu_custom_call" | custom-call | flops 1342177280 | bytes 4718592 | tf_op jit(solution)/shard_map/pallas_call | solution.py:260
  120.6 13.2 %shard_map.182 = (bf16[8,64,2048]{2,1,0:T(8,128)(2,1)}, bf16[8,64,2048]{2,1,0:T(8,128)(2,1)}, bf16[8,64,2048]{2,1,0:T(8,128)(2,1)}, bf16[8,64,2048]{2,1,0:T(8,128)(2,1)}) custom-call(s32[1]{0:T(128)} %bitcast.18.side_ref, bf16[640,1024]{1,0:T(8,128)(2,1)} %copy-done.14, bf16[640,4096]{1,0:T(8,128)(2,1)} %copy-done.34), custom_call_target="tpu_custom_call" | custom-call | flops 5368709120 | bytes 14942208 | tf_op jit(solution)/shard_map/pallas_call | solution.py:260
  133.8 10.8 %fusion.49 = bf16[1,640,1024]{2,1,0:T(8,128)(2,1)} fusion(f32[640,1024]{1,0:T(8,128)S(1)} %get-tuple-element.115, bf16[640,4096]{1,0:T(8,128)(2,1)} %get-tuple-element.116.refs_0_, bf16[4096,1024]{1,0:T(8,128)(2,1)} %param.21), kind=kOutput, calls=%fused_computation.75 | convolution fusion | flops 5370019840 | bytes 17563648 | tf_op jit(solution)/shard_map/dot_general | solution.py:46
  145.6 41.3 %shard_map.179 = (bf16[640,1024]{1,0:T(8,128)(2,1)}, bf16[640,1024]{1,0:T(8,128)(2,1)}, bf16[640,1024]{1,0:T(8,128)(2,1)}, bf16[640,1024]{1,0:T(8,128)(2,1)}, bf16[640,1024]{1,0:T(8,128)(2,1)}) custom-call(s32[2]{0:T(128)} %compare_select_fusion.lim_ref, bf16[640,3072]{1,0:T(8,128)(2,1)} %convolution_convert_fusion.q_ref.ko_ref.vo_ref, ...), custom_call_target="tpu_custom_call" | custom-call | flops 33554432000 | bytes 18350080 | tf_op jit(solution)/shard_map/pallas_call | solution.py:180
  186.9 3.6 fusion.36
  190.6 4.9 %fusion.23 = (f32[1024]{0:T(1024)S(1)}, f32[1024]{0:T(1024)S(1)}, bf16[640,1024]{1,0:T(8,128)(2,1)}) fusion(bf16[640,1024]{1,0:T(8,128)(2,1)} %collective-permute-done, f32[640]{0:T(1024)S(1)} %add_rsqrt_fusion.1, f32[640]{0:T(1024)S(1)} %broadcast_multiply_fusion.5, f32[640,1024]{1,0:T(8,128)S(1)} %fusion.36, bf16[640,1024]{1,0:T(8,128)(2,1)S(1)} %copy-done.32, ...), kind=kOutput, calls=%fused_computation.30 | convolution fusion | flops 1347418112 | bytes 8664064 | tf_op jit(solution)/shard_map/dot_general | solution.py:52
  195.5 1.7 collective-permute-start.1
  197.2 4.8 %fusion.38 = f32[640,1024]{1,0:T(8,128)} fusion(bf16[640,1024]{1,0:T(8,128)(2,1)S(1)} %copy-done.33, bf16[1024,3072]{1,0:T(8,128)(2,1)} %param.18), kind=kOutput, calls=%fused_computation.63 | convolution fusion | flops 1342177280 | bytes 6029312 | tf_op jit(solution)/shard_map/dot_general | solution.py:52
  203.1 15.2 %shard_map.180 = (bf16[8,64,1536]{2,1,0:T(8,128)(2,1)}, bf16[8,64,1536]{2,1,0:T(8,128)(2,1)}, bf16[8,64,1536]{2,1,0:T(8,128)(2,1)}, bf16[8,64,1536]{2,1,0:T(8,128)(2,1)}) custom-call(s32[1]{0:T(128)} %bitcast.18.side_ref, bf16[640,1024]{1,0:T(8,128)(2,1)} %copy-done.12, bf16[640,1024]{1,0:T(8,128)(2,1)} %copy-done.11, ...), custom_call_target="tpu_custom_call" | custom-call | flops 6710886400 | bytes 15466496 | tf_op jit(solution)/shard_map/pallas_call | solution.py:260
  218.3 2.1 add_convert_fusion.35
  220.4 1.8 collective-permute-start.19
  222.1 10.0 %collective-permute-done.24 = bf16[8,64,256]{2,1,0:T(8,128)(2,1)} collective-permute-done((bf16[8,64,256]{2,1,0:T(8,128)(2,1)}, bf16[8,64,256]{2,1,0:T(8,128)(2,1)}, u32[]{:S(2)}, u32[]{:S(2)}) %collective-permute-start.24) | collective-permute-done | bytes 262176 | tf_op jit(solution)/shard_map/ppermute | solution.py:279
  232.2 1.7 add_convert_fusion.42
  233.8 1.8 collective-permute-start.25
  235.6 14.1 %shard_map.183 = (bf16[8,256,512]{2,1,0:T(8,128)(2,1)}, bf16[8,256,512]{2,1,0:T(8,128)(2,1)}, bf16[8,256,512]{2,1,0:T(8,128)(2,1)}, bf16[8,256,512]{2,1,0:T(8,128)(2,1)}) custom-call(s32[1]{0:T(128)} %bitcast.18.side_ref, bf16[640,4096]{1,0:T(8,128)(2,1)} %get-tuple-element.116.refs_0_, bf16[640,1024]{1,0:T(8,128)(2,1)} %bitcast.206), custom_call_target="tpu_custom_call" | custom-call | flops 5368709120 | bytes 14942208 | tf_op jit(solution)/shard_map/pallas_call | solution.py:260
  250.7 1.6 collective-permute-start.20
  253.0 3.8 fusion.34
  257.0 2.7 collective-permute-start.27
  259.6 2.2 collective-permute-done.27
  261.8 2.6 collective-permute-start.21
  264.5 4.0 collective-permute-done.21
  269.9 2.4 collective-permute-done.28
  273.8 2.8 collective-permute-done.22
  276.7 4.7 %fusion.31 = (f32[1024]{0:T(1024)S(1)}, f32[640]{0:T(1024)S(1)}, f32[640]{0:T(1024)S(1)}, f32[1024]{0:T(1024)S(1)}, f32[640,1024]{1,0:T(8,128)S(1)}) fusion(f32[640]{0:T(1024)S(1)} %copy-done.19, f32[640]{0:T(1024)S(1)} %copy-done.17, bf16[1,640,1024]{2,1,0:T(8,128)(2,1)S(1)} %copy-done.2, f32[1024]{0:T(1024)S(1)} %bitcast.226, ...), kind=kOutput, calls=%fused_computation.38 | convolution fusion | flops 1351348992 | bytes 13916160 | tf_op jit(solution)/shard_map/dot_general | solution.py:52
  281.4 1.5 collective-permute-start.2
  283.7 1.5 collective-permute-done.2
  287.0 3.5 collective-permute-done.4
  291.1 3.6 fusion.50
  296.1 3.1 collective-permute-start.6
  299.6 6.2 %collective-permute-done.6 = f32[8,4224]{1,0:T(8,128)S(1)} collective-permute-done((f32[8,4224]{1,0:T(8,128)S(1)}, f32[8,4224]{1,0:T(8,128)S(1)}, u32[]{:S(2)}, u32[]{:S(2)}) %collective-permute-start.6) | collective-permute-done | bytes 135200 | tf_op jit(solution)/shard_map/ppermute | solution.py:279
  307.3 1.6 fusion.63
  311.7 2.0 fusion.109
  314.5 10.3 %collective-permute-done.13 = bf16[8,64,768]{2,1,0:T(8,128)(2,1)S(1)} collective-permute-done((bf16[8,64,768]{2,1,0:T(8,128)(2,1)S(1)}, bf16[8,64,768]{2,1,0:T(8,128)(2,1)S(1)}, u32[]{:S(2)}, u32[]{:S(2)}) %collective-permute-start.13) | collective-permute-done | bytes 786464 | tf_op jit(solution)/shard_map/ppermute | solution.py:279
  325.6 5.1 %collective-permute-done.8 = bf16[4,64,1536]{2,1,0:T(8,128)(2,1)S(1)} collective-permute-done((bf16[4,64,1536]{2,1,0:T(8,128)(2,1)S(1)}, bf16[4,64,1536]{2,1,0:T(8,128)(2,1)S(1)}, u32[]{:S(2)}, u32[]{:S(2)}) %collective-permute-start.8) | collective-permute-done | bytes 786464 | tf_op jit(solution)/shard_map/ppermute | solution.py:279
  333.8 26.1 %collective-permute-done.14 = bf16[4,64,768]{2,1,0:T(8,128)(2,1)S(1)} collective-permute-done((bf16[4,64,768]{2,1,0:T(8,128)(2,1)S(1)}, bf16[4,64,768]{2,1,0:T(8,128)(2,1)S(1)}, u32[]{:S(2)}, u32[]{:S(2)}) %collective-permute-start.14) | collective-permute-done | bytes 393248 | tf_op jit(solution)/shard_map/ppermute | solution.py:279
  360.7 2.9 collective-permute-start.10
  364.3 4.7 %collective-permute-done.15 = bf16[2,64,768]{2,1,0:T(8,128)(2,1)S(1)} collective-permute-done((bf16[2,64,768]{2,1,0:T(8,128)(2,1)S(1)}, bf16[2,64,768]{2,1,0:T(8,128)(2,1)S(1)}, u32[]{:S(2)}, u32[]{:S(2)}) %collective-permute-start.15) | collective-permute-done | bytes 196640 | tf_op jit(solution)/shard_map/ppermute | solution.py:279
  369.6 2.7 collective-permute-done.10
  372.4 5.7 %collective-permute-done.16 = bf16[1,64,768]{2,1,0:T(8,128)(2,1)S(1)} collective-permute-done((bf16[1,64,768]{2,1,0:T(8,128)(2,1)S(1)}, bf16[1,64,768]{2,1,0:T(8,128)(2,1)S(1)}, u32[]{:S(2)}, u32[]{:S(2)}) %collective-permute-start.16) | collective-permute-done | bytes 98336 | tf_op jit(solution)/shard_map/ppermute | solution.py:279
  381.1 2.3 collective-permute-done.41
  384.2 10.2 %collective-permute-done.46 = bf16[8,256,256]{2,1,0:T(8,128)(2,1)S(1)} collective-permute-done((bf16[8,256,256]{2,1,0:T(8,128)(2,1)S(1)}, bf16[8,256,256]{2,1,0:T(8,128)(2,1)S(1)}, u32[]{:S(2)}, u32[]{:S(2)}) %collective-permute-start.46) | collective-permute-done | bytes 1048608 | tf_op jit(solution)/shard_map/ppermute | solution.py:279
  394.7 1.8 collective-permute-done.11
  399.9 1.8 collective-permute-start.37
  401.7 17.3 %collective-permute-done.42 = bf16[2,256,512]{2,1,0:T(8,128)(2,1)S(1)} collective-permute-done((bf16[2,256,512]{2,1,0:T(8,128)(2,1)S(1)}, bf16[2,256,512]{2,1,0:T(8,128)(2,1)S(1)}, u32[]{:S(2)}, u32[]{:S(2)}) %collective-permute-start.42) | collective-permute-done | bytes 524320 | tf_op jit(solution)/shard_map/ppermute | solution.py:279
  419.3 1.7 collective-permute-start.48
  421.1 1.6 collective-permute-start.33
  422.8 9.6 %collective-permute-done.43 = bf16[1,256,512]{2,1,0:T(8,128)(2,1)S(1)} collective-permute-done((bf16[1,256,512]{2,1,0:T(8,128)(2,1)S(1)}, bf16[1,256,512]{2,1,0:T(8,128)(2,1)S(1)}, u32[]{:S(2)}, u32[]{:S(2)}) %collective-permute-start.43) | collective-permute-done | bytes 262176 | tf_op jit(solution)/shard_map/ppermute | solution.py:279
  434.9 4.8 %collective-permute-done.49 = bf16[1,256,256]{2,1,0:T(8,128)(2,1)S(1)} collective-permute-done((bf16[1,256,256]{2,1,0:T(8,128)(2,1)S(1)}, bf16[1,256,256]{2,1,0:T(8,128)(2,1)S(1)}, u32[]{:S(2)}, u32[]{:S(2)}) %collective-permute-start.49) | collective-permute-done | bytes 131104 | tf_op jit(solution)/shard_map/ppermute | solution.py:279
  442.4 2.4 collective-permute-done.50
  (215 shorter events, 40.8 us)
Async XLA Ops:
  0.6 70.4 %copy-start = (bf16[1024,1024]{1,0:T(8,128)(2,1)S(1)}, bf16[1024,1024]{1,0:T(8,128)(2,1)}, u32[]{:S(2)}) copy-start(bf16[1024,1024]{1,0:T(8,128)(2,1)} %param.19) | copy-start | bytes 6291460
  0.7 32.1 %collective-permute-start = (bf16[640,1024]{1,0:T(8,128)(2,1)}, bf16[640,1024]{1,0:T(8,128)(2,1)}, u32[]{:S(2)}, u32[]{:S(2)}) collective-permute-start(bf16[640,1024]{1,0:T(8,128)(2,1)} %bitcast.190), channel_id=1, source_target_pairs={{1,0},{0,1},{3,2},{2,3},{5,4},{4,5},{7,6},{6,7},{9,8},{8,9},{11,10... | collective-permute-start | bytes 3932168 | tf_op jit(solution)/shard_map/ppermute | solution.py:369
  13.3 25.5 %copy-start.16 = (f32[640]{0:T(1024)}, f32[640]{0:T(1024)S(1)}, u32[]{:S(2)}) copy-start(f32[640]{0:T(1024)S(1)} %broadcast_multiply_fusion.6) | copy-start | bytes 7684
  13.7 25.1 %copy-start.18 = (f32[640]{0:T(1024)}, f32[640]{0:T(1024)S(1)}, u32[]{:S(2)}) copy-start(f32[640]{0:T(1024)S(1)} %add_rsqrt_fusion.2) | copy-start | bytes 7684
  13.8 25.0 %copy-start.20 = (f32[1,1024]{1,0:T(1,128)}, f32[1,1024]{1,0:T(1,128)S(1)}, u32[]{:S(2)}) copy-start(f32[1,1024]{1,0:T(1,128)S(1)} %get-tuple-element.111) | copy-start | bytes 12292
  144.6 73.7 %collective-permute-start.18 = (bf16[8,64,512]{2,1,0:T(8,128)(2,1)}, bf16[8,64,512]{2,1,0:T(8,128)(2,1)}, u32[]{:S(2)}, u32[]{:S(2)}) collective-permute-start(bf16[8,64,512]{2,1,0:T(8,128)(2,1)} %get-tuple-element.44), channel_id=1, source_target_pairs={{0,2},{2,0},{4,6},{6,4},{8,10},{10,8},{12,14},{14,12},{16,18},{18,... | collective-permute-start | bytes 1572872 | tf_op jit(solution)/shard_map/ppermute | solution.py:279
  144.6 57.4 %collective-permute-start.23 = (bf16[8,64,512]{2,1,0:T(8,128)(2,1)S(1)}, bf16[8,64,512]{2,1,0:T(8,128)(2,1)S(1)}, u32[]{:S(2)}, u32[]{:S(2)}) collective-permute-start(bf16[8,64,512]{2,1,0:T(8,128)(2,1)S(1)} %copy-done.29), channel_id=1, source_target_pairs={{0,2},{2,0},{4,6},{6,4},{8,10},{10,8},{12,14},{14,12},{16,18},{18,... | collective-permute-start | bytes 1572872 | tf_op jit(solution)/shard_map/ppermute | solution.py:279
  145.1 165.2 %collective-permute-start.29 = (bf16[8,64,2048]{2,1,0:T(8,128)(2,1)}, bf16[8,64,2048]{2,1,0:T(8,128)(2,1)S(1)}, u32[]{:S(2)}, u32[]{:S(2)}) collective-permute-start(bf16[8,64,2048]{2,1,0:T(8,128)(2,1)} %get-tuple-element.48), channel_id=1, source_target_pairs={{0,2},{2,0},{4,6},{6,4},{8,10},{10,8},{12,14},{14,12},{16,18},{18,... | collective-permute-start | bytes 6291464 | tf_op jit(solution)/shard_map/ppermute | solution.py:279
  145.2 186.3 %collective-permute-start.34 = (bf16[8,64,2048]{2,1,0:T(8,128)(2,1)}, bf16[8,64,2048]{2,1,0:T(8,128)(2,1)S(1)}, u32[]{:S(2)}, u32[]{:S(2)}) collective-permute-start(bf16[8,64,2048]{2,1,0:T(8,128)(2,1)} %get-tuple-element.50), channel_id=1, source_target_pairs={{0,2},{2,0},{4,6},{6,4},{8,10},{10,8},{12,14},{14,12},{16,18},{18,... | collective-permute-start | bytes 6291464 | tf_op jit(solution)/shard_map/ppermute | solution.py:279
  195.5 81.2 %collective-permute-start.1 = (bf16[640,1024]{1,0:T(8,128)(2,1)}, bf16[640,1024]{1,0:T(8,128)(2,1)}, u32[]{:S(2)}, u32[]{:S(2)}) collective-permute-start(bf16[640,1024]{1,0:T(8,128)(2,1)} %get-tuple-element.79), channel_id=1, source_target_pairs={{0,1},{1,0},{2,3},{3,2},{4,5},{5,4},{6,7},{7,6},{8,9},{9,8},{10,11... | collective-permute-start | bytes 3932168 | tf_op jit(solution)/shard_map/ppermute | solution.py:372
  202.8 29.3 %collective-permute-start.24 = (bf16[8,64,256]{2,1,0:T(8,128)(2,1)}, bf16[8,64,256]{2,1,0:T(8,128)(2,1)}, u32[]{:S(2)}, u32[]{:S(2)}) collective-permute-start(bf16[8,64,256]{2,1,0:T(8,128)(2,1)} %get-tuple-element.99), channel_id=1, source_target_pairs={{0,1},{1,0},{2,3},{3,2},{4,5},{5,4},{6,7},{7,6},{8,9},{9,8},{10,11... | collective-permute-start | bytes 786440 | tf_op jit(solution)/shard_map/ppermute | solution.py:279
  220.4 29.3 %collective-permute-start.19 = (bf16[4,64,512]{2,1,0:T(8,128)(2,1)}, bf16[4,64,512]{2,1,0:T(8,128)(2,1)}, u32[]{:S(2)}, u32[]{:S(2)}) collective-permute-start(bf16[4,64,512]{2,1,0:T(8,128)(2,1)} %get-tuple-element.97), channel_id=1, source_target_pairs={{0,4},{2,6},{4,0},{6,2},{8,12},{10,14},{12,8},{14,10},{16,20},{18,... | collective-permute-start | bytes 786440 | tf_op jit(solution)/shard_map/ppermute | solution.py:279
  233.8 18.5 %collective-permute-start.25 = (bf16[4,64,256]{2,1,0:T(8,128)(2,1)}, bf16[4,64,256]{2,1,0:T(8,128)(2,1)S(1)}, u32[]{:S(2)}, u32[]{:S(2)}) collective-permute-start(bf16[4,64,256]{2,1,0:T(8,128)(2,1)} %get-tuple-element.105), channel_id=1, source_target_pairs={{0,4},{2,6},{4,0},{6,2},{8,12},{10,14},{12,8},{14,10},{16,20},{18,... | collective-permute-start | bytes 393224 | tf_op jit(solution)/shard_map/ppermute | solution.py:279
  250.7 6.2 %collective-permute-start.20 = (bf16[2,64,512]{2,1,0:T(8,128)(2,1)S(1)}, bf16[2,64,512]{2,1,0:T(8,128)(2,1)S(1)}, u32[]{:S(2)}, u32[]{:S(2)}) collective-permute-start(bf16[2,64,512]{2,1,0:T(8,128)(2,1)S(1)} %get-tuple-element.103), channel_id=1, source_target_pairs={{0,8},{2,10},{4,12},{6,14},{8,0},{10,2},{12,4},{14,6},{16,24},{18,... | collective-permute-start | bytes 393224 | tf_op jit(solution)/shard_map/ppermute | solution.py:279
  252.4 24.2 %copy-start.27 = (bf16[8,64,1536]{2,1,0:T(8,128)(2,1)S(1)}, bf16[8,64,1536]{2,1,0:T(8,128)(2,1)}, u32[]{:S(2)}) copy-start(bf16[8,64,1536]{2,1,0:T(8,128)(2,1)} %get-tuple-element.42) | copy-start | bytes 4718596
  252.4 24.2 %copy-start.17 = (f32[640]{0:T(1024)S(1)}, f32[640]{0:T(1024)}, u32[]{:S(2)}) copy-start(f32[640]{0:T(1024)} %copy-done.16) | copy-start | bytes 7684
  252.4 24.2 %copy-start.19 = (f32[640]{0:T(1024)S(1)}, f32[640]{0:T(1024)}, u32[]{:S(2)}) copy-start(f32[640]{0:T(1024)} %copy-done.18) | copy-start | bytes 7684
  252.5 24.2 %copy-start.21 = (f32[1,1024]{1,0:T(1,128)S(1)}, f32[1,1024]{1,0:T(1,128)}, u32[]{:S(2)}) copy-start(f32[1,1024]{1,0:T(1,128)} %copy-done.20) | copy-start | bytes 12292
  252.5 24.2 %copy-start.30 = (f32[640,1024]{1,0:T(8,128)S(1)}, f32[640,1024]{1,0:T(8,128)}, u32[]{:S(2)}) copy-start(f32[640,1024]{1,0:T(8,128)} %fusion.38) | copy-start | bytes 7864324
  252.5 24.2 %copy-start.31 = (bf16[640,1024]{1,0:T(8,128)(2,1)S(1)}, bf16[640,1024]{1,0:T(8,128)(2,1)}, u32[]{:S(2)}) copy-start(bf16[640,1024]{1,0:T(8,128)(2,1)} %get-tuple-element.35.refs_3_) | copy-start | bytes 3932164
  252.5 4.3 collective-permute-start.26
  256.8 38.2 %collective-permute-start.7 = (bf16[8,64,1536]{2,1,0:T(8,128)(2,1)S(1)}, bf16[8,64,1536]{2,1,0:T(8,128)(2,1)S(1)}, u32[]{:S(2)}, u32[]{:S(2)}) collective-permute-start(bf16[8,64,1536]{2,1,0:T(8,128)(2,1)S(1)} %copy-done.28), channel_id=1, source_target_pairs={{0,2},{2,0},{4,6},{6,4},{8,10},{10,8},{12,14},{14,12},{16,18},{18,... | collective-permute-start | bytes 4718600 | tf_op jit(solution)/shard_map/ppermute | solution.py:279
  257.0 4.9 %collective-permute-start.27 = (bf16[1,64,256]{2,1,0:T(8,128)(2,1)S(1)}, bf16[1,64,256]{2,1,0:T(8,128)(2,1)S(1)}, u32[]{:S(2)}, u32[]{:S(2)}) collective-permute-start(bf16[1,64,256]{2,1,0:T(8,128)(2,1)S(1)} %fusion.95), channel_id=1, source_target_pairs={{0,16},{2,18},{4,20},{6,22},{8,24},{10,26},{12,28},{14,30},{16,0},... | collective-permute-start | bytes 98312 | tf_op jit(solution)/shard_map/ppermute | solution.py:279
  261.8 6.6 %collective-permute-start.21 = (bf16[1,64,512]{2,1,0:T(8,128)(2,1)S(1)}, bf16[1,64,512]{2,1,0:T(8,128)(2,1)S(1)}, u32[]{:S(2)}, u32[]{:S(2)}) collective-permute-start(bf16[1,64,512]{2,1,0:T(8,128)(2,1)S(1)} %fusion.89), channel_id=1, source_target_pairs={{0,16},{2,18},{4,20},{6,22},{8,24},{10,26},{12,28},{14,30},{16,0},... | collective-permute-start | bytes 196616 | tf_op jit(solution)/shard_map/ppermute | solution.py:279
  268.4 3.9 collective-permute-start.28
  272.3 4.3 collective-permute-start.22
  276.6 19.5 %collective-permute-start.12 = (bf16[8,64,1536]{2,1,0:T(8,128)(2,1)S(1)}, bf16[8,64,1536]{2,1,0:T(8,128)(2,1)S(1)}, u32[]{:S(2)}, u32[]{:S(2)}) collective-permute-start(bf16[8,64,1536]{2,1,0:T(8,128)(2,1)S(1)} %copy-done.27), channel_id=1, source_target_pairs={{0,2},{2,0},{4,6},{6,4},{8,10},{10,8},{12,14},{14,12},{16,18},{18,... | collective-permute-start | bytes 4718600 | tf_op jit(solution)/shard_map/ppermute | solution.py:279
  276.7 14.4 %copy-start.3 = (f32[640,1024]{1,0:T(8,128)S(1)}, f32[640,1024]{1,0:T(8,128)}, u32[]{:S(2)}) copy-start(f32[640,1024]{1,0:T(8,128)} %get-tuple-element.66) | copy-start | bytes 7864324
  281.4 3.8 collective-permute-start.2
  285.3 1.2 collective-permute-start.3
  286.6 4.0 collective-permute-start.4
  290.6 4.4 collective-permute-start.5
  295.0 37.5 %collective-permute-start.40 = (bf16[8,256,512]{2,1,0:T(8,128)(2,1)S(1)}, bf16[8,256,512]{2,1,0:T(8,128)(2,1)S(1)}, u32[]{:S(2)}, u32[]{:S(2)}) collective-permute-start(bf16[8,256,512]{2,1,0:T(8,128)(2,1)S(1)} %copy-done.26), channel_id=1, source_target_pairs={{0,2},{2,0},{4,6},{6,4},{8,10},{10,8},{12,14},{14,12},{16,18},{18,... | collective-permute-start | bytes 6291464 | tf_op jit(solution)/shard_map/ppermute | solution.py:279
  295.1 65.6 %collective-permute-start.45 = (bf16[8,256,512]{2,1,0:T(8,128)(2,1)S(1)}, bf16[8,256,512]{2,1,0:T(8,128)(2,1)S(1)}, u32[]{:S(2)}, u32[]{:S(2)}) collective-permute-start(bf16[8,256,512]{2,1,0:T(8,128)(2,1)S(1)} %copy-done.25), channel_id=1, source_target_pairs={{0,2},{2,0},{4,6},{6,4},{8,10},{10,8},{12,14},{14,12},{16,18},{18,... | collective-permute-start | bytes 6291464 | tf_op jit(solution)/shard_map/ppermute | solution.py:279
  296.1 9.8 %collective-permute-start.6 = (f32[8,4224]{1,0:T(8,128)S(1)}, f32[8,4224]{1,0:T(8,128)S(1)}, u32[]{:S(2)}, u32[]{:S(2)}) collective-permute-start(f32[8,4224]{1,0:T(8,128)S(1)} %maximum_select_fusion.4), channel_id=1, source_target_pairs={{0,16},{2,18},{4,20},{6,22},{8,24},{10,26},{12,28},{14,30},{16,0},... | collective-permute-start | bytes 405512 | tf_op jit(solution)/shard_map/ppermute | solution.py:279
  305.8 19.0 %collective-permute-start.13 = (bf16[8,64,768]{2,1,0:T(8,128)(2,1)S(1)}, bf16[8,64,768]{2,1,0:T(8,128)(2,1)S(1)}, u32[]{:S(2)}, u32[]{:S(2)}) collective-permute-start(bf16[8,64,768]{2,1,0:T(8,128)(2,1)S(1)} %get-tuple-element.78), channel_id=1, source_target_pairs={{0,1},{1,0},{2,3},{3,2},{4,5},{5,4},{6,7},{7,6},{8,9},{9,8},{10,11... | collective-permute-start | bytes 2359304 | tf_op jit(solution)/shard_map/ppermute | solution.py:279
  310.3 20.4 %collective-permute-start.8 = (bf16[4,64,1536]{2,1,0:T(8,128)(2,1)S(1)}, bf16[4,64,1536]{2,1,0:T(8,128)(2,1)S(1)}, u32[]{:S(2)}, u32[]{:S(2)}) collective-permute-start(bf16[4,64,1536]{2,1,0:T(8,128)(2,1)S(1)} %get-tuple-element.76), channel_id=1, source_target_pairs={{0,4},{2,6},{4,0},{6,2},{8,12},{10,14},{12,8},{14,10},{16,20},{18,... | collective-permute-start | bytes 2359304 | tf_op jit(solution)/shard_map/ppermute | solution.py:279
  314.5 17.1 %copy-start.4 = (bf16[8,64,2048]{2,1,0:T(8,128)(2,1)S(1)}, bf16[8,64,2048]{2,1,0:T(8,128)(2,1)}, u32[]{:S(2)}) copy-start(bf16[8,64,2048]{2,1,0:T(8,128)(2,1)} %get-tuple-element.49) | copy-start | bytes 6291460
  324.8 54.0 %collective-permute-start.30 = (bf16[4,64,2048]{2,1,0:T(8,128)(2,1)S(1)}, bf16[4,64,2048]{2,1,0:T(8,128)(2,1)S(1)}, u32[]{:S(2)}, u32[]{:S(2)}) collective-permute-start(bf16[4,64,2048]{2,1,0:T(8,128)(2,1)S(1)} %get-tuple-element.72), channel_id=1, source_target_pairs={{0,4},{2,6},{4,0},{6,2},{8,12},{10,14},{12,8},{14,10},{16,20},{18,... | collective-permute-start | bytes 3145736 | tf_op jit(solution)/shard_map/ppermute | solution.py:279
  330.7 29.2 %collective-permute-start.14 = (bf16[4,64,768]{2,1,0:T(8,128)(2,1)S(1)}, bf16[4,64,768]{2,1,0:T(8,128)(2,1)S(1)}, u32[]{:S(2)}, u32[]{:S(2)}) collective-permute-start(bf16[4,64,768]{2,1,0:T(8,128)(2,1)S(1)} %get-tuple-element.91), channel_id=1, source_target_pairs={{0,4},{2,6},{4,0},{6,2},{8,12},{10,14},{12,8},{14,10},{16,20},{18,... | collective-permute-start | bytes 1179656 | tf_op jit(solution)/shard_map/ppermute | solution.py:279
  331.4 29.1 %collective-permute-start.9 = (bf16[2,64,1536]{2,1,0:T(8,128)(2,1)S(1)}, bf16[2,64,1536]{2,1,0:T(8,128)(2,1)S(1)}, u32[]{:S(2)}, u32[]{:S(2)}) collective-permute-start(bf16[2,64,1536]{2,1,0:T(8,128)(2,1)S(1)} %get-tuple-element.89), channel_id=1, source_target_pairs={{0,8},{2,10},{4,12},{6,14},{8,0},{10,2},{12,4},{14,6},{16,24},{18,... | collective-permute-start | bytes 1179656 | tf_op jit(solution)/shard_map/ppermute | solution.py:279
  332.5 48.1 %collective-permute-start.35 = (bf16[8,64,1024]{2,1,0:T(8,128)(2,1)S(1)}, bf16[8,64,1024]{2,1,0:T(8,128)(2,1)S(1)}, u32[]{:S(2)}, u32[]{:S(2)}) collective-permute-start(bf16[8,64,1024]{2,1,0:T(8,128)(2,1)S(1)} %get-tuple-element.74), channel_id=1, source_target_pairs={{0,1},{1,0},{2,3},{3,2},{4,5},{5,4},{6,7},{7,6},{8,9},{9,8},{10,11... | collective-permute-start | bytes 3145736 | tf_op jit(solution)/shard_map/ppermute | solution.py:279
  333.1 30.5 %copy-start.6 = (bf16[8,256,512]{2,1,0:T(8,128)(2,1)S(1)}, bf16[8,256,512]{2,1,0:T(8,128)(2,1)}, u32[]{:S(2)}) copy-start(bf16[8,256,512]{2,1,0:T(8,128)(2,1)} %get-tuple-element.53) | copy-start | bytes 6291460
  360.0 23.5 %collective-permute-start.41 = (bf16[4,256,512]{2,1,0:T(8,128)(2,1)S(1)}, bf16[4,256,512]{2,1,0:T(8,128)(2,1)S(1)}, u32[]{:S(2)}, u32[]{:S(2)}) collective-permute-start(bf16[4,256,512]{2,1,0:T(8,128)(2,1)S(1)} %get-tuple-element.68), channel_id=1, source_target_pairs={{0,4},{2,6},{4,0},{6,2},{8,12},{10,14},{12,8},{14,10},{16,20},{18,... | collective-permute-start | bytes 3145736 | tf_op jit(solution)/shard_map/ppermute | solution.py:279
  360.5 8.5 %collective-permute-start.15 = (bf16[2,64,768]{2,1,0:T(8,128)(2,1)S(1)}, bf16[2,64,768]{2,1,0:T(8,128)(2,1)S(1)}, u32[]{:S(2)}, u32[]{:S(2)}) collective-permute-start(bf16[2,64,768]{2,1,0:T(8,128)(2,1)S(1)} %get-tuple-element.101), channel_id=1, source_target_pairs={{0,8},{2,10},{4,12},{6,14},{8,0},{10,2},{12,4},{14,6},{16,24},{18,... | collective-permute-start | bytes 589832 | tf_op jit(solution)/shard_map/ppermute | solution.py:279
  360.7 11.7 %collective-permute-start.10 = (bf16[1,64,1536]{2,1,0:T(8,128)(2,1)S(1)}, bf16[1,64,1536]{2,1,0:T(8,128)(2,1)S(1)}, u32[]{:S(2)}, u32[]{:S(2)}) collective-permute-start(bf16[1,64,1536]{2,1,0:T(8,128)(2,1)S(1)} %fusion.67), channel_id=1, source_target_pairs={{0,16},{2,18},{4,20},{6,22},{8,24},{10,26},{12,28},{14,30},{16,0},... | collective-permute-start | bytes 589832 | tf_op jit(solution)/shard_map/ppermute | solution.py:279
  369.0 25.4 %collective-permute-start.46 = (bf16[8,256,256]{2,1,0:T(8,128)(2,1)S(1)}, bf16[8,256,256]{2,1,0:T(8,128)(2,1)S(1)}, u32[]{:S(2)}, u32[]{:S(2)}) collective-permute-start(bf16[8,256,256]{2,1,0:T(8,128)(2,1)S(1)} %get-tuple-element.70), channel_id=1, source_target_pairs={{0,1},{1,0},{2,3},{3,2},{4,5},{5,4},{6,7},{7,6},{8,9},{9,8},{10,11... | collective-permute-start | bytes 3145736 | tf_op jit(solution)/shard_map/ppermute | solution.py:279
  372.3 5.8 %collective-permute-start.16 = (bf16[1,64,768]{2,1,0:T(8,128)(2,1)S(1)}, bf16[1,64,768]{2,1,0:T(8,128)(2,1)S(1)}, u32[]{:S(2)}, u32[]{:S(2)}) collective-permute-start(bf16[1,64,768]{2,1,0:T(8,128)(2,1)S(1)} %fusion.83), channel_id=1, source_target_pairs={{0,16},{2,18},{4,20},{6,22},{8,24},{10,26},{12,28},{14,30},{16,0},... | collective-permute-start | bytes 294920 | tf_op jit(solution)/shard_map/ppermute | solution.py:279
  378.1 18.4 %collective-permute-start.11 = (bf16[64,1536]{1,0:T(8,128)(2,1)S(1)}, bf16[64,1536]{1,0:T(8,128)(2,1)S(1)}, u32[]{:S(2)}, u32[]{:S(2)}) collective-permute-start(bf16[64,1536]{1,0:T(8,128)(2,1)S(1)} %fusion.80), channel_id=1, source_target_pairs={{0,1},{1,0},{2,3},{3,2},{4,5},{5,4},{6,7},{7,6},{8,9},{9,8},{10,11... | collective-permute-start | bytes 589832 | tf_op jit(solution)/shard_map/ppermute | solution.py:279
  378.8 19.3 %collective-permute-start.17 = (bf16[64,768]{1,0:T(8,128)(2,1)S(1)}, bf16[64,768]{1,0:T(8,128)(2,1)S(1)}, u32[]{:S(2)}, u32[]{:S(2)}) collective-permute-start(bf16[64,768]{1,0:T(8,128)(2,1)S(1)} %fusion.91), channel_id=1, source_target_pairs={{0,1},{1,0},{2,3},{3,2},{4,5},{5,4},{6,7},{7,6},{8,9},{9,8},{10,11... | collective-permute-start | bytes 294920 | tf_op jit(solution)/shard_map/ppermute | solution.py:279
  380.6 18.4 %collective-permute-start.31 = (bf16[2,64,2048]{2,1,0:T(8,128)(2,1)S(1)}, bf16[2,64,2048]{2,1,0:T(8,128)(2,1)S(1)}, u32[]{:S(2)}, u32[]{:S(2)}) collective-permute-start(bf16[2,64,2048]{2,1,0:T(8,128)(2,1)S(1)} %get-tuple-element.85), channel_id=1, source_target_pairs={{0,8},{2,10},{4,12},{6,14},{8,0},{10,2},{12,4},{14,6},{16,24},{18,... | collective-permute-start | bytes 1572872 | tf_op jit(solution)/shard_map/ppermute | solution.py:279
  383.4 16.3 %collective-permute-start.36 = (bf16[4,64,1024]{2,1,0:T(8,128)(2,1)S(1)}, bf16[4,64,1024]{2,1,0:T(8,128)(2,1)S(1)}, u32[]{:S(2)}, u32[]{:S(2)}) collective-permute-start(bf16[4,64,1024]{2,1,0:T(8,128)(2,1)S(1)} %get-tuple-element.87), channel_id=1, source_target_pairs={{0,4},{2,6},{4,0},{6,2},{8,12},{10,14},{12,8},{14,10},{16,20},{18,... | collective-permute-start | bytes 1572872 | tf_op jit(solution)/shard_map/ppermute | solution.py:279
  394.4 24.6 %collective-permute-start.42 = (bf16[2,256,512]{2,1,0:T(8,128)(2,1)S(1)}, bf16[2,256,512]{2,1,0:T(8,128)(2,1)S(1)}, u32[]{:S(2)}, u32[]{:S(2)}) collective-permute-start(bf16[2,256,512]{2,1,0:T(8,128)(2,1)S(1)} %get-tuple-element.81), channel_id=1, source_target_pairs={{0,8},{2,10},{4,12},{6,14},{8,0},{10,2},{12,4},{14,6},{16,24},{18,... | collective-permute-start | bytes 1572872 | tf_op jit(solution)/shard_map/ppermute | solution.py:279
  396.5 22.6 %collective-permute-start.47 = (bf16[4,256,256]{2,1,0:T(8,128)(2,1)S(1)}, bf16[4,256,256]{2,1,0:T(8,128)(2,1)S(1)}, u32[]{:S(2)}, u32[]{:S(2)}) collective-permute-start(bf16[4,256,256]{2,1,0:T(8,128)(2,1)S(1)} %get-tuple-element.83), channel_id=1, source_target_pairs={{0,4},{2,6},{4,0},{6,2},{8,12},{10,14},{12,8},{14,10},{16,20},{18,... | collective-permute-start | bytes 1572872 | tf_op jit(solution)/shard_map/ppermute | solution.py:279
  399.1 21.9 %collective-permute-start.32 = (bf16[1,64,2048]{2,1,0:T(8,128)(2,1)S(1)}, bf16[1,64,2048]{2,1,0:T(8,128)(2,1)S(1)}, u32[]{:S(2)}, u32[]{:S(2)}) collective-permute-start(bf16[1,64,2048]{2,1,0:T(8,128)(2,1)S(1)} %fusion.61), channel_id=1, source_target_pairs={{0,16},{2,18},{4,20},{6,22},{8,24},{10,26},{12,28},{14,30},{16,0},... | collective-permute-start | bytes 786440 | tf_op jit(solution)/shard_map/ppermute | solution.py:279
  399.9 22.8 %collective-permute-start.37 = (bf16[2,64,1024]{2,1,0:T(8,128)(2,1)S(1)}, bf16[2,64,1024]{2,1,0:T(8,128)(2,1)S(1)}, u32[]{:S(2)}, u32[]{:S(2)}) collective-permute-start(bf16[2,64,1024]{2,1,0:T(8,128)(2,1)S(1)} %get-tuple-element.95), channel_id=1, source_target_pairs={{0,8},{2,10},{4,12},{6,14},{8,0},{10,2},{12,4},{14,6},{16,24},{18,... | collective-permute-start | bytes 786440 | tf_op jit(solution)/shard_map/ppermute | solution.py:279
  419.1 13.4 %collective-permute-start.43 = (bf16[1,256,512]{2,1,0:T(8,128)(2,1)S(1)}, bf16[1,256,512]{2,1,0:T(8,128)(2,1)S(1)}, u32[]{:S(2)}, u32[]{:S(2)}) collective-permute-start(bf16[1,256,512]{2,1,0:T(8,128)(2,1)S(1)} %fusion.59), channel_id=1, source_target_pairs={{0,16},{2,18},{4,20},{6,22},{8,24},{10,26},{12,28},{14,30},{16,0},... | collective-permute-start | bytes 786440 | tf_op jit(solution)/shard_map/ppermute | solution.py:279
  419.3 14.0 %collective-permute-start.48 = (bf16[2,256,256]{2,1,0:T(8,128)(2,1)S(1)}, bf16[2,256,256]{2,1,0:T(8,128)(2,1)S(1)}, u32[]{:S(2)}, u32[]{:S(2)}) collective-permute-start(bf16[2,256,256]{2,1,0:T(8,128)(2,1)S(1)} %get-tuple-element.93), channel_id=1, source_target_pairs={{0,8},{2,10},{4,12},{6,14},{8,0},{10,2},{12,4},{14,6},{16,24},{18,... | collective-permute-start | bytes 786440 | tf_op jit(solution)/shard_map/ppermute | solution.py:279
  421.1 20.0 %collective-permute-start.33 = (bf16[64,2048]{1,0:T(8,128)(2,1)S(1)}, bf16[64,2048]{1,0:T(8,128)(2,1)S(1)}, u32[]{:S(2)}, u32[]{:S(2)}) collective-permute-start(bf16[64,2048]{1,0:T(8,128)(2,1)S(1)} %fusion.70), channel_id=1, source_target_pairs={{0,1},{1,0},{2,3},{3,2},{4,5},{5,4},{6,7},{7,6},{8,9},{9,8},{10,11... | collective-permute-start | bytes 786440 | tf_op jit(solution)/shard_map/ppermute | solution.py:279
  422.8 11.1 %collective-permute-start.38 = (bf16[1,64,1024]{2,1,0:T(8,128)(2,1)S(1)}, bf16[1,64,1024]{2,1,0:T(8,128)(2,1)S(1)}, u32[]{:S(2)}, u32[]{:S(2)}) collective-permute-start(bf16[1,64,1024]{2,1,0:T(8,128)(2,1)S(1)} %fusion.78), channel_id=1, source_target_pairs={{0,16},{2,18},{4,20},{6,22},{8,24},{10,26},{12,28},{14,30},{16,0},... | collective-permute-start | bytes 393224 | tf_op jit(solution)/shard_map/ppermute | solution.py:279
  432.5 9.7 %collective-permute-start.44 = (bf16[256,512]{1,0:T(8,128)(2,1)S(1)}, bf16[256,512]{1,0:T(8,128)(2,1)S(1)}, u32[]{:S(2)}, u32[]{:S(2)}) collective-permute-start(bf16[256,512]{1,0:T(8,128)(2,1)S(1)} %fusion.72), channel_id=1, source_target_pairs={{0,1},{1,0},{2,3},{3,2},{4,5},{5,4},{6,7},{7,6},{8,9},{9,8},{10,11... | collective-permute-start | bytes 786440 | tf_op jit(solution)/shard_map/ppermute | solution.py:279
  433.3 6.3 %collective-permute-start.49 = (bf16[1,256,256]{2,1,0:T(8,128)(2,1)S(1)}, bf16[1,256,256]{2,1,0:T(8,128)(2,1)S(1)}, u32[]{:S(2)}, u32[]{:S(2)}) collective-permute-start(bf16[1,256,256]{2,1,0:T(8,128)(2,1)S(1)} %fusion.76), channel_id=1, source_target_pairs={{0,16},{2,18},{4,20},{6,22},{8,24},{10,26},{12,28},{14,30},{16,0},... | collective-permute-start | bytes 393224 | tf_op jit(solution)/shard_map/ppermute | solution.py:279
  433.9 7.2 %collective-permute-start.39 = (bf16[64,1024]{1,0:T(8,128)(2,1)S(1)}, bf16[64,1024]{1,0:T(8,128)(2,1)S(1)}, u32[]{:S(2)}, u32[]{:S(2)}) collective-permute-start(bf16[64,1024]{1,0:T(8,128)(2,1)S(1)} %fusion.87), channel_id=1, source_target_pairs={{0,1},{1,0},{2,3},{3,2},{4,5},{5,4},{6,7},{7,6},{8,9},{9,8},{10,11... | collective-permute-start | bytes 393224 | tf_op jit(solution)/shard_map/ppermute | solution.py:279
  439.7 5.0 %collective-permute-start.50 = (bf16[256,256]{1,0:T(8,128)(2,1)S(1)}, bf16[256,256]{1,0:T(8,128)(2,1)S(1)}, u32[]{:S(2)}, u32[]{:S(2)}) collective-permute-start(bf16[256,256]{1,0:T(8,128)(2,1)S(1)} %fusion.88), channel_id=1, source_target_pairs={{0,1},{1,0},{2,3},{3,2},{4,5},{5,4},{6,7},{7,6},{8,9},{9,8},{10,11... | collective-permute-start | bytes 393224 | tf_op jit(solution)/shard_map/ppermute | solution.py:279
  (22 other events, 141.9 us)

commit v2 on v1

--- a/solution.py
+++ b/solution.py
@@ -188,6 +188,12 @@
     )(lim, qkv, qkv, qkv, kv_rest, kv_rest, do, o, lse)
 
 
+def outer_sum(left, right):
+    return lax.dot_general(
+        left, right, (((0,), (0,)), ((), ())), preferred_element_type=jnp.float32
+    )
+
+
 def outer_kernel(plan, halves, first_tiles, side_ref, *refs):
     lefts, plan_rights, outs, turned = refs[: plan[0]], refs[plan[0] : plan[1]], refs[plan[1] : plan[1] + 4], refs[plan[1] + 4 :]
     step = pl.program_id(0)
@@ -346,6 +352,314 @@
     return values
 
 
+LAG = 2
+STAGES = 6
+MESH = pl.DeviceIdType.MESH
+
+
+def sum_kernel(units, plan, left_count, right_count, *refs):
+    lefts = refs[:left_count]
+    rights = refs[left_count : left_count + right_count]
+    vector = refs[left_count + right_count]
+    rest = refs[left_count + right_count + 1 :]
+    outs, gathered_out, rest = rest[: len(plan)], rest[len(plan)], rest[len(plan) + 1 :]
+    turned, rest = rest[:left_count], rest[left_count:]
+    (send0, recv0, keep0, send_y, recv_y, send_x, recv_x) = rest[:7]
+    (send_z, recv_z, send_w, recv_w, keep_a, keep_b, last_a, last_b) = rest[7:15]
+    (gathered, got_vector, out_sem, in_sem, vec_out, vec_in) = rest[15:]
+    tick = pl.program_id(0)
+    item, seq = lax.axis_index("items"), lax.axis_index("seq")
+    bit = lambda value, place: jnp.bitwise_and(value // (1 << place), 1)
+    core, y, z0, z1, x = bit(item, 0), bit(item, 1), bit(item, 2), bit(item, 3), seq
+    flip = lambda place: item + (1 - 2 * bit(item, place)) * (1 << place)
+    partners = {
+        "core": (flip(0), seq),
+        "y": (flip(1), seq),
+        "z0": (flip(2), seq),
+        "z1": (flip(3), seq),
+        "x": (item, 1 - seq),
+    }
+
+    @pl.when(tick == 0)
+    def _():
+        barrier = pltpu.get_barrier_semaphore()
+        for partner in partners.values():
+            pl.semaphore_signal(barrier, inc=1, device_id=partner, device_id_type=MESH)
+        pl.semaphore_wait(barrier, len(partners))
+
+    def copy(kind, number, unit, source, target, to):
+        slot, landing = unit % 2, unit % 4
+        return pltpu.make_async_remote_copy(
+            src_ref=source.at[slot],
+            dst_ref=target.at[landing],
+            send_sem=out_sem.at[number, slot],
+            recv_sem=in_sem.at[number, landing],
+            device_id=partners[to],
+            device_id_type=MESH,
+        )
+
+    wide = lambda values: values.astype(jnp.float32)
+    low = lambda values: values.astype(jnp.bfloat16)
+
+    def choose(values, axis, which):
+        first = lax.index_in_dim(values, 0, axis, keepdims=False)
+        second = lax.index_in_dim(values, 1, axis, keepdims=False)
+        mine = jnp.where(which == 0, first, second)
+        other = jnp.where(which == 0, second, first)
+        return mine, other
+
+    names = [
+        ("d", send0, recv0, "core"),
+        ("ay", send_y[0], recv_y[0], "y"),
+        ("az", send_z[0], recv_z[0], "z0"),
+        ("aw", send_w[0], recv_w[0], "z1"),
+        ("ax", send_x[0], recv_x[0], "x"),
+        ("bx", send_x[1], recv_x[1], "x"),
+        ("by", send_y[1], recv_y[1], "y"),
+        ("bz", send_z[1], recv_z[1], "z0"),
+        ("bw", send_w[1], recv_w[1], "z1"),
+        ("bg", send_x[2], recv_x[2], "x"),
+    ]
+    table = {name: (i, source, target, to) for i, (name, source, target, to) in enumerate(names)}
+
+    def post(name, unit, values):
+        number, source, target, to = table[name]
+        source[unit % 2] = low(values)
+        copy(name, number, unit, source, target, to).start()
+
+    def take(name, unit):
+        number, source, target, to = table[name]
+        copy(name, number, unit, source, target, to).wait()
+        return wide(target[unit % 4])
+
+    def stage_final(unit, offset):
+        other = take("bg", unit)
+        mine = last_b[unit % 2]
+        top = jnp.where(x == 0, mine, other)
+        bottom = jnp.where(x == 0, other, mine)
+        block = jnp.concatenate(
+            [last_a[unit % 2], jnp.concatenate([top, bottom], 0)], 1
+        )
+        at = 0
+        for (count, _, _), out in zip(plan, outs):
+
+            @pl.when((unit >= at) & (unit < at + count))
+            def _(out=out):
+                out[...] = block
+
+            at += count
+
+    def stage_five(unit):
+        last_a[unit % 2] = keep_a[3][unit % 2] + take("ax", unit)
+        total = low(keep_b[3][unit % 2] + take("bw", unit))
+        last_b[unit % 2] = wide(total)
+        post("bg", unit, total)
+
+    def stage_four(unit):
+        total = low(keep_a[2][unit % 2] + take("aw", unit))
+        keep_a[3][unit % 2] = wide(total)
+        post("ax", unit, total)
+        mine, other = choose(keep_b[2][unit % 2] + take("bz", unit), 0, z1)
+        keep_b[3][unit % 2] = mine
+        post("bw", unit, other)
+
+    def stage_three(unit):
+        mine, other = choose(keep_a[1][unit % 2] + take("az", unit), 0, z1)
+        keep_a[2][unit % 2] = mine
+        post("aw", unit, other)
+        total = keep_b[1][unit % 2] + take("by", unit)
+        mine, other = choose(total.reshape(2, 2, 32, 128), 1, z0)
+        keep_b[2][unit % 2] = mine
+        post("bz", unit, other)
+
+    def stage_two(unit):
+        total = keep_a[0][unit % 2] + take("ay", unit)
+        mine, other = choose(total.reshape(2, 2, 64, 128), 1, z0)
+        keep_a[1][unit % 2] = mine
+        post("az", unit, other)
+        total = keep_b[0][unit % 2] + take("bx", unit)
+        mine, other = choose(total.reshape(4, 2, 32, 128), 1, y)
+        keep_b[1][unit % 2] = mine
+        post("by", unit, other)
+
+    def stage_one(unit):
+        total = keep0[unit % 2] + take("d", unit)
+        mine, other = choose(total[:, :, :128].reshape(4, 2, 64, 128), 1, y)
+        keep_a[0][unit % 2] = mine
+        post("ay", unit, other)
+        mine, other = choose(total[:, :, 128:].reshape(8, 2, 32, 128), 1, x)
+        keep_b[0][unit % 2] = mine
+        post("bx", unit, other)
+
+    def stage_zero(unit):
+        at = 0
+        for count, terms, turns in plan:
+
+            @pl.when((unit >= at) & (unit < at + count))
+            def _(at=at, terms=terms, turns=turns):
+                for which, start in turns:
+
+                    @pl.when(unit == at + start)
+                    def _(which=which):
+                        turned[which][...] = lefts[which][...].T
+
+                place = 0
+                for segment, pairs in terms:
+
+                    @pl.when((unit >= at + place) & (unit < at + place + segment))
+                    def _(pairs=pairs):
+                        total = None
+                        for which, right in pairs:
+                            part = dot(turned[which][...], rights[right][...], 1, 0)
+                            total = part if total is None else total + part
+                        mine, other = choose(total.reshape(8, 2, 64, 256), 1, core)
+                        keep0[unit % 2] = mine
+                        post("d", unit, other)
+
+                    place += segment
+
+            at += count
+
+    steps = [stage_zero, stage_one, stage_two, stage_three, stage_four, stage_five, stage_final]
+    for number in range(STAGES, -1, -1):
+        unit = tick - LAG * number
+
+        @pl.when((unit >= 0) & (unit < units))
+        def _(number=number, unit=unit):
+            if number == STAGES:
+                stage_final(unit, 0)
+            else:
+                steps[number](unit)
+
+    def vec_copy(number, source, target, to):
+        return pltpu.make_async_remote_copy(
+            src_ref=source,
+            dst_ref=target,
+            send_sem=vec_out.at[number],
+            recv_sem=vec_in.at[number],
+            device_id=partners[to],
+            device_id_type=MESH,
+        )
+
+    first = vec_copy(0, vector, got_vector, "x")
+    hops = []
+    for number, to in enumerate(("core", "y", "z0", "z1")):
+        count = 1 << number
+        run = gathered.at[pl.ds((item // count) * count, count)]
+        hops.append(vec_copy(number + 1, run, run, to))
+
+    @pl.when(tick == 0)
+    def _():
+        first.start()
+
+    @pl.when(tick == LAG)
+    def _():
+        first.wait()
+        heights = lax.broadcasted_iota(jnp.int32, vector.shape, 0)
+        gathered[item] = vector[...] + jnp.where(heights < vector.shape[0] - 8, got_vector[...], 0.0)
+        hops[0].start()
+
+    for number in range(4):
+
+        @pl.when(tick == LAG * (number + 2))
+        def _(number=number):
+            hops[number].wait()
+            if number < 3:
+                hops[number + 1].start()
+            else:
+                gathered_out[...] = gathered[...]
+
+
+def sum_weights(weights, lefts, vector):
+    tile = 256
+    rows = lefts[0].shape[1]
+    operands, in_specs, plan, out_specs, out_shape = [], [], [], [], []
+    for left in lefts:
+        in_specs.append(
+            pl.BlockSpec(left.shape, lambda i: (0, 0), pipeline_mode=pl.Buffered(1))
+        )
+    seen = set()
+    at = 0
+    flops = 0
+    for weight in weights:
+        terms, turns = [], []
+        place = 0
+        for segment in weight:
+            count = segment[0][1].shape[1] // tile
+            pairs = []
+            for which, right in segment:
+                if which not in seen:
+                    seen.add(which)
+                    turns.append((which, place))
+                pairs.append((which, len(operands)))
+                operands.append(right)
+                flops += 2 * rows * right.shape[0] * right.shape[1]
+                in_specs.append(
+                    pl.BlockSpec(
+                        (right.shape[0], tile),
+                        lambda i, start=at + place, count=count: (
+                            0,
+                            jnp.clip(i - start, 0, count - 1),
+                        ),
+                    )
+                )
+            terms.append((count, tuple(pairs)))
+            place += count
+        plan.append((place, tuple(terms), tuple(turns)))
+        out_specs.append(
+            pl.BlockSpec(
+                (64, tile),
+                lambda i, start=at, count=place: (
+                    0,
+                    jnp.clip(i - LAG * STAGES - start, 0, count - 1),
+                ),
+            )
+        )
+        out_shape.append(jax.ShapeDtypeStruct((64, place * tile), jnp.float32))
+        at += place
+    units = at
+    in_specs.append(pl.BlockSpec(vector.shape, lambda i: (0, 0)))
+    out_specs.append(pl.BlockSpec((16,) + vector.shape, lambda i: (0, 0, 0)))
+    out_shape.append(jax.ShapeDtypeStruct((16,) + vector.shape, jnp.float32))
+    low = lambda *shape: pltpu.VMEM(shape, jnp.bfloat16)
+    full = lambda *shape: pltpu.VMEM(shape, jnp.float32)
+    scratch = [low(*left.shape[::-1]) for left in lefts]
+    scratch += [low(2, 8, 64, 256), low(4, 8, 64, 256), full(2, 8, 64, 256)]
+    scratch += [
+        (low(2, 4, 64, 128), low(2, 4, 32, 128)),
+        (low(4, 4, 64, 128), low(4, 4, 32, 128)),
+        (low(2, 64, 128), low(2, 8, 32, 128), low(2, 32, 128)),
+        (low(4, 64, 128), low(4, 8, 32, 128), low(4, 32, 128)),
+        (low(2, 2, 64, 128), low(2, 2, 32, 128)),
+        (low(4, 2, 64, 128), low(4, 2, 32, 128)),
+        (low(2, 64, 128), low(2, 32, 128)),
+        (low(4, 64, 128), low(4, 32, 128)),
+        (full(2, 4, 64, 128), full(2, 2, 64, 128), full(2, 64, 128), full(2, 64, 128)),
+        (full(2, 8, 32, 128), full(2, 4, 32, 128), full(2, 2, 32, 128), full(2, 32, 128)),
+        full(2, 64, 128),
+        full(2, 32, 128),
+        full(16, *vector.shape),
+        full(*vector.shape),
+        pltpu.SemaphoreType.DMA((10, 2)),
+        pltpu.SemaphoreType.DMA((10, 4)),
+        pltpu.SemaphoreType.DMA((5,)),
+        pltpu.SemaphoreType.DMA((5,)),
+    ]
+    moved = sum(2 * a.size for a in operands) + sum(2 * a.size for a in lefts)
+    return pl.pallas_call(
+        functools.partial(sum_kernel, units, tuple(plan), len(lefts), len(operands)),
+        grid=(units + LAG * STAGES,),
+        in_specs=in_specs,
+        out_specs=out_specs,
+        out_shape=out_shape,
+        scratch_shapes=scratch,
+        compiler_params=pltpu.CompilerParams(
+            vmem_limit_bytes=58 << 20, collective_id=0, has_side_effects=True
+        ),
+        cost_estimate=pl.CostEstimate(flops=flops, transcendentals=0, bytes_accessed=moved),
+    )(*lefts, *operands, vector)
+
+
 def per_device(
     frames,
     cotangent,
@@ -401,30 +715,33 @@
     out_frames = (mid + project(act, w_down)).astype(jnp.bfloat16)
 
     grad_out = cotangent.astype(jnp.float32)
-    down_pieces = outer(side, [act], [[(0, cotangent)]], item_size, 256)
+    fused = seq_size == 2 and item_size == 16 and width == 1024
+    if fused:
+        sum_down = lax.psum_scatter(
+            outer_sum(act, cotangent).astype(jnp.bfloat16),
+            "items",
+            scatter_dimension=0,
+            tiled=True,
+        )
+    else:
+        down_pieces = outer(side, [act], [[(0, cotangent)]], item_size, 256)
     grad_upper = (back_project(cotangent, w_down) * gelu_slope(upper)).astype(jnp.bfloat16)
-    up_pieces = outer(side, [ffn_in], [[(0, grad_upper)]], item_size, 512)
     grad_ffn_in = back_project(grad_upper, w_up)
     grad_scale_two = jnp.sum(grad_ffn_in * normed_two, 0)
     grad_shift_two = jnp.sum(grad_ffn_in, 0)
     grad_mid = grad_out + norm_back(grad_ffn_in * (1.0 + scale_two), normed_two, inv_two)
     grad_mid_low = grad_mid.astype(jnp.bfloat16)
-    out_pieces = outer(side, [att], [[(0, grad_mid_low)]], item_size, 512)
     grad_att = back_project(grad_mid_low, w_out).astype(jnp.bfloat16)
     grad_query, grad_key, grad_value, key_rest, value_rest = attend_back(
         limits, qkv, kv_rest, grad_att, att, lse
     )
-    qkv_pieces = outer(
-        side,
-        [attn_in, attn_rest],
-        [
-            [(0, grad_query)],
-            [(0, grad_key), (1, key_rest)],
-            [(0, grad_value), (1, value_rest)],
-        ],
-        item_size,
-        512,
-    )
+    up_terms = [[(0, grad_upper)]]
+    out_terms = [[(1, grad_mid_low)]]
+    qkv_terms = [
+        [(2, grad_query)],
+        [(2, grad_key), (3, key_rest)],
+        [(2, grad_value), (3, value_rest)],
+    ]
     w_key, w_value = w_qkv[:, width : 2 * width], w_qkv[:, 2 * width :]
     share = back_project(key_rest, w_key) + back_project(value_rest, w_value)
     grad_rest = [
@@ -445,18 +762,39 @@
         grad_mid + norm_back(grad_attn_in * (1.0 + scale_one), normed_one, inv_one)
     ).astype(jnp.bfloat16)
 
-    sum_down = finish(down_pieces, "items", "seq")
-    sum_up = finish(up_pieces, "items", "seq")
-    sum_out = finish(out_pieces, "items", "seq")
-    sum_qkv = finish(qkv_pieces, "items", "seq")
-
     grad_modul = jnp.concatenate(
         [grad_scale_one, grad_shift_one, grad_scale_two, grad_shift_two]
     )[None, :]
-    for bit in bits_of("seq"):
-        grad_modul = grad_modul + swap(grad_modul, "seq", bit)
-    tagged = jnp.concatenate([grad_modul, jnp.pad(onehot, ((0, 0), (0, 128 - section_count)))], -1)
-    tagged = gather_items(tagged, "items")
+    if fused:
+        vector = jnp.concatenate(
+            [
+                grad_modul.reshape(4 * width // 128, 128),
+                jnp.pad(onehot, ((0, 7), (0, 128 - section_count))),
+            ]
+        )
+        sum_up, sum_out, sum_qkv, tagged = sum_weights(
+            [up_terms, out_terms, qkv_terms], [ffn_in, att, attn_in, attn_rest], vector
+        )
+        tagged = tagged[:, : 4 * width // 128 + 1].reshape(item_size, 4 * width + 128)
+        sum_down = sum_down.astype(jnp.float32) + swap(sum_down, "seq", 1).astype(jnp.float32)
+    else:
+        shift = lambda terms, by: [[(i - by, right) for i, right in run] for run in terms]
+        sum_down = finish(down_pieces, "items", "seq")
+        sum_up = finish(outer(side, [ffn_in], up_terms, item_size, 512), "items", "seq")
+        sum_out = finish(
+            outer(side, [att], shift(out_terms, 1), item_size, 512), "items", "seq"
+        )
+        sum_qkv = finish(
+            outer(side, [attn_in, attn_rest], shift(qkv_terms, 2), item_size, 512),
+            "items",
+            "seq",
+        )
+        for bit in bits_of("seq"):
+            grad_modul = grad_modul + swap(grad_modul, "seq", bit)
+        tagged = jnp.concatenate(
+            [grad_modul, jnp.pad(onehot, ((0, 0), (0, 128 - section_count)))], -1
+        )
+        tagged = gather_items(tagged, "items")
     modul_all, onehot_all = tagged[:, : 4 * width], tagged[:, 4 * width :][:, :section_count]
     block = width // item_size
     own_embed = lax.dynamic_slice_in_dim(section_embed, item_me * block, block, 1)

time: 455 us -> 359 us (0.79); the launches traced: 446 us -> 356 us
  waiting for transfers between devices: 157 us -> 40 us
  Pallas kernels: 111 us -> 163 us
  starting transfers between devices: 47.3 us -> 6.08 us
  other arithmetic: 32.4 us -> 16.8 us
  between operations: 3.19 us -> 16 us
  matrix products: 95.2 us -> 105 us
  local copies, waits for them, and re-layouts: 0.18 us -> 9.05 us
    ppermute x49 -> x1, waiting for transfers between devices: 138 us -> 3.68 us  [swap(): return lax.ppermute(values, axis, [(i, i ^ bit) for i in range(size)])]
    pallas_call x4 -> x1, Pallas kernels: 47.9 us -> 99 us  [sum_weights(): pl.pallas_call(functools.partial(sum_kernel, units, tuple(plan), len(left...]
    ppermute x49 -> x1, starting transfers between devices: 42.5 us -> 1.19 us  [swap(): return lax.ppermute(values, axis, [(i, i ^ bit) for i in range(size)])]
    ppermute x1, waiting for transfers between devices: 0.01 us -> 17.1 us  [per_device(): lax.ppermute(values, 'seq', [(i, (i + turn) % seq_size) for i in range(se...]
    convert_element_type x36 -> x0, other arithmetic: 12.6 us -> none  [the longest x28 12.1 us: add_low(): (left.astype(jnp.float32) + right.astype(jnp.float32)).astype(jnp.bfloat16)]
    dot_general x0 -> x1, matrix products: none -> 9.07 us  [outer_sum(): lax.dot_general(left, right, (((0,), (0,)), ((), ())), preferred_element_...]
    unnamed x70 -> x68, local copies, waits for them, and re-layouts: 0.16 us -> 9.03 us
    dot_general x5, matrix products: 36.2 us -> 43 us  [project(): result = jnp.dot(flat, weight, preferred_element_type=jnp.float32)]
  transfers between devices with their start and end apart: 51 -> 4, of which waited for: 25 -> 3; matrix products, arithmetic and copies ran while one was open for 12% -> 20% of each run, Pallas kernels for 16% -> 40%
where the time goes in v2:
time: 359 us; the launch traced here: 356 us
  Pallas kernels  163 us (45%)
  matrix products  105 us (29%)
  waiting for transfers between devices  40 us (11%)
  other arithmetic  16.8 us (5%)
  between operations  16 us (4%)
  local copies, waits for them, and re-layouts  9.05 us (3%)
  starting transfers between devices  6.08 us (2%)
    pallas_call x1, Pallas kernels, sum_weights(): pl.pallas_call(functools.partial(sum_kernel, units, tuple(plan), len(left...  99 us
    dot_general x5, matrix products, project(): result = jnp.dot(flat, weight, preferred_element_type=jnp.float32)  43 us
    pallas_call x1, Pallas kernels, attend_back(): pl.pallas_call(functools.partial(bwd_kernel, rows, blocks), grid_spec=plt...  41.7 us
    dot_general x8, matrix products, back_project(): lax.dot_general(flat, weight, (((1,), (1,)), ((), ())), preferred_element...  41.2 us
    pallas_call x1, Pallas kernels, attend(): pl.pallas_call(functools.partial(fwd_kernel, rows, blocks), grid_spec=plt...  22.2 us
    ppermute x1, waiting for transfers between devices, per_device(): lax.ppermute(values, 'seq', [((i + turn) % seq_size, i) for i in range(se...  19.2 us
    ppermute x1, waiting for transfers between devices, per_device(): lax.ppermute(values, 'seq', [(i, (i + turn) % seq_size) for i in range(se...  17.1 us
    dot_general x1, matrix products, outer_sum(): lax.dot_general(left, right, (((0,), (0,)), ((), ())), preferred_element_...  9.07 us
  transfers between devices with their start and end apart: 4, of which 3 were waited for; matrix products, arithmetic and copies ran while one was open for 20% of the time, Pallas kernels for 40%

profile of v2, /device:TPU:0, one launch (start us, length us, event | category | flops | bytes accessed | tf_op | source)
XLA Modules:
  0.0 356.0 jit_solution(5936919085526725444)
XLA Ops:
  7.2 0.0 copy-start
  7.2 0.0 reduce-scatter.2.cloned.1.call-start
  7.2 3.0 collective-permute-start
  10.9 0.9 convolution_bitcast_fusion
  11.8 0.0 copy-start.15
  11.8 0.0 copy-start.4
  11.8 5.8 %fusion.73 = f32[1,4096]{1,0:T(1,128)S(1)} fusion(f32[1024,1]{0,1:T(1,128)S(1)} %convolution_bitcast_fusion, bf16[1024,4096]{1,0:T(8,128)(2,1)} %param.16), kind=kOutput, calls=%fused_computation.111 | convolution fusion | flops 50331648 | bytes 8409088 | tf_op jit(solution)/shard_map/dot_general | solution.py:698
  18.3 0.5 iota_compare_fusion
  18.8 0.6 compare_select_fusion.lim_ref
  19.4 0.2 convert_reduce_fusion
  19.7 0.5 fusion.32
  20.2 19.2 %collective-permute-done = bf16[640,1024]{1,0:T(8,128)(2,1)} collective-permute-done((bf16[640,1024]{1,0:T(8,128)(2,1)}, bf16[640,1024]{1,0:T(8,128)(2,1)}, u32[]{:S(2)}, u32[]{:S(2)}) %collective-permute-start) | collective-permute-done | bytes 1310752 | tf_op jit(solution)/shard_map/ppermute | solution.py:683
  39.4 1.6 convert_reduce_fusion.1
  40.9 0.0 copy-start.18
  40.9 1.9 fusion.33
  42.9 2.5 fusion.22
  45.4 4.2 %fusion.8.kt_ref.vt_ref = bf16[640,2048]{1,0:T(8,128)(2,1)} fusion(bf16[640,1024]{1,0:T(8,128)(2,1)S(1)} %get-tuple-element.48.refs_3_, bf16[1024,3072]{1,0:T(8,128)(2,1)S(1)} %copy-done.18), kind=kOutput, calls=%fused_computation.18 | convolution fusion | flops 2685665280 | bytes 8126464 | tf_op jit(solution)/shard_map/dot_general | solution.py:46
  49.6 5.7 %convolution_convert_fusion.1.q_ref.ko_ref.vo_ref = bf16[640,3072]{1,0:T(8,128)(2,1)} fusion(bf16[640,1024]{1,0:T(8,128)(2,1)S(1)} %get-tuple-element.49.refs_2_, bf16[1024,3072]{1,0:T(8,128)(2,1)S(1)} %copy-done.18), kind=kOutput, calls=%fused_computation.10 | convolution fusion | flops 4028497920 | bytes 11534336 | tf_op jit(solution)/shard_map/dot_general | solution.py:46
  55.4 22.2 %shard_map.178 = (bf16[640,1024]{1,0:T(8,128)(2,1)}, f32[640,1024]{1,0:T(8,128)}) custom-call(s32[2]{0:T(128)} %compare_select_fusion.lim_ref, bf16[640,3072]{1,0:T(8,128)(2,1)} %convolution_convert_fusion.1.q_ref.ko_ref.vo_ref, bf16[640,3072]{1,0:T(8,128)(2,1)} %convolution_convert_fusion.1.q_ref.ko_ref.vo_ref, ...), custom_call_target="tpu_custom_call" | custom-call | flops 13421772800 | bytes 10485760 | tf_op jit(solution)/shard_map/pallas_call | solution.py:163
  77.6 2.9 fusion.72
  80.5 0.4 multiply_reduce_fusion.2
  80.9 1.2 copy-done.2
  82.1 0.5 add_convert_fusion.1.refs_0_
  82.6 0.0 copy-start.5
  82.6 23.4 %multiply_convert_fusion = (bf16[640,4096]{1,0:T(8,128)(2,1)S(1)}, f32[640,4096]{1,0:T(8,128)}) fusion(bf16[640,1024]{1,0:T(8,128)(2,1)S(1)} %add_convert_fusion.1.refs_0_, bf16[1024,4096]{1,0:T(8,128)(2,1)} %param.20), kind=kOutput, calls=%fused_computation.7 | convolution fusion | flops 5381816320 | bytes 25427968 | tf_op jit(solution)/shard_map/dot_general | solution.py:46
  106.0 2.3 copy-done.23
  108.3 9.1 %convolution_convert_fusion = bf16[4096,1024]{1,0:T(8,128)(2,1)} fusion(bf16[640,4096]{1,0:T(8,128)(2,1)S(1)} %get-tuple-element.52, bf16[1,640,1024]{2,1,0:T(8,128)(2,1)S(1)} %copy-done.5), kind=kOutput, calls=%fused_computation.9 | convolution fusion | flops 5372903424 | bytes 14942208 | tf_op jit(solution)/shard_map/dot_general | solution.py:192
  117.4 0.0 reduce-scatter.2.cloned.1.call-update
  117.4 12.5 %fusion.5.refs_4_ = bf16[640,4096]{1,0:T(8,128)(2,1)S(1)} fusion(f32[640,4096]{1,0:T(8,128)} %get-tuple-element.53, bf16[4096,1024]{1,0:T(8,128)(2,1)} %param.21, bf16[1,640,1024]{2,1,0:T(8,128)(2,1)} %param.12), kind=kOutput, calls=%fused_computation.6 | convolution fusion | flops 5394923520 | bytes 25427968 | tf_op jit(solution)/shard_map/dot_general | solution.py:52
  129.9 0.0 copy-start.6
  129.9 11.4 %multiply_reduce_fusion = (f32[1024]{0:T(1024)S(1)}, f32[640]{0:T(1024)S(1)}, f32[640]{0:T(1024)S(1)}, f32[1024]{0:T(1024)S(1)}, f32[640,1024]{1,0:T(8,128)S(1)}) fusion(f32[640,1024]{1,0:T(8,128)S(1)} %copy-done.3, f32[640]{0:T(1024)S(1)} %add_rsqrt_fusion, f32[640]{0:T(1024)S(1)} %broadcast_multiply_fusion.4, f32[1024]{0:T(1024)S(1)} %bitcast.89, ...), kind=kOutput, calls=%fused_computation.42 | convolution fusion | flops 5374604288 | bytes 18896896 | tf_op jit(solution)/shard_map/dot_general | solution.py:52
  141.4 2.3 fusion.71
  143.8 2.6 convolution_convert_fusion.2.do_ref
  146.4 41.7 %shard_map.179 = (bf16[640,1024]{1,0:T(8,128)(2,1)}, bf16[640,1024]{1,0:T(8,128)(2,1)}, bf16[640,1024]{1,0:T(8,128)(2,1)}, bf16[640,1024]{1,0:T(8,128)(2,1)}, bf16[640,1024]{1,0:T(8,128)(2,1)}) custom-call(s32[2]{0:T(128)} %compare_select_fusion.lim_ref, bf16[640,3072]{1,0:T(8,128)(2,1)} %convolution_convert_fusion.1.q_ref.ko_ref.vo_ref, ...), custom_call_target="tpu_custom_call" | custom-call | flops 33554432000 | bytes 18350080 | tf_op jit(solution)/shard_map/pallas_call | solution.py:180
  188.1 0.0 slice-start.2
  188.1 3.8 %fusion.36 = f32[640,1024]{1,0:T(8,128)S(1)} fusion(bf16[640,1024]{1,0:T(8,128)(2,1)} %get-tuple-element.26.refs_10_, bf16[1024,3072]{1,0:T(8,128)(2,1)} %param.18), kind=kOutput, calls=%fused_computation.54 | convolution fusion | flops 1342177280 | bytes 6029312 | tf_op jit(solution)/shard_map/dot_general | solution.py:52
  191.8 0.0 slice-start.3
  191.9 4.0 %fusion.70 = (f32[1024]{0:T(1024)S(1)}, f32[1024]{0:T(1024)S(1)}, bf16[640,1024]{1,0:T(8,128)(2,1)S(1)}) fusion(f32[640]{0:T(1024)S(1)} %add_rsqrt_fusion.1, f32[640]{0:T(1024)S(1)} %broadcast_multiply_fusion.5, bf16[640,1024]{1,0:T(8,128)(2,1)} %collective-permute-done, f32[640,1024]{1,0:T(8,128)S(1)} %fusion.36, bf16[640,1024]{1,0:T(8,128)(2,1)S(1)} %copy-done.20, ...), kind=kOutput, calls=%fused_computation.108 | convolution fusion | flops 1347418112 | bytes 8664064 | tf_op jit(solution)/shard_map/dot_general | solution.py:52
  195.8 1.8 collective-permute-start.1
  197.7 0.0 slice-start
  197.7 0.0 slice-start.5
  197.7 1.6 fusion.34
  199.3 0.0 slice-start.1
  199.3 1.6 fusion.38
  200.9 1.2 slice-done.1
  202.1 6.7 %fusion.49 = bf16[1,640,1024]{2,1,0:T(8,128)(2,1)} fusion(f32[640,1024]{1,0:T(8,128)S(1)} %copy-done.3, bf16[640,4096]{1,0:T(8,128)(2,1)S(1)} %bitcast.98, bf16[4096,1024]{1,0:T(8,128)(2,1)S(1)} %bitcast.94), kind=kOutput, calls=%fused_computation.64 | convolution fusion | flops 5370019840 | bytes 17563648 | tf_op jit(solution)/shard_map/dot_general | solution.py:46
  208.8 17.1 %collective-permute-done.1 = bf16[640,1024]{1,0:T(8,128)(2,1)S(1)} collective-permute-done((bf16[640,1024]{1,0:T(8,128)(2,1)S(1)}, bf16[640,1024]{1,0:T(8,128)(2,1)S(1)}, u32[]{:S(2)}, u32[]{:S(2)}) %collective-permute-start.1) | collective-permute-done | bytes 1310752 | tf_op jit(solution)/shard_map/ppermute | solution.py:686
  225.9 3.8 %fusion.31 = (f32[1024]{0:T(1024)S(1)}, f32[640]{0:T(1024)S(1)}, f32[640]{0:T(1024)S(1)}, f32[1024]{0:T(1024)S(1)}, f32[640,1024]{1,0:T(8,128)}) fusion(f32[640]{0:T(1024)S(1)} %add_rsqrt_fusion.2, f32[640]{0:T(1024)S(1)} %broadcast_multiply_fusion.6, bf16[1,640,1024]{2,1,0:T(8,128)(2,1)S(1)} %copy-done.4, f32[1024]{0:T(1024)S(1)} %bitcast.86, ...), kind=kOutput, calls=%fused_computation.39 | convolution fusion | flops 1351348992 | bytes 13919232 | tf_op jit(solution)/shard_map/dot_general | solution.py:52
  229.8 0.0 copy-start.16
  229.8 0.6 copy-done.16
  230.4 99.0 %shard_map.180 = (f32[64,4096]{1,0:T(8,128)}, f32[64,1024]{1,0:T(8,128)}, f32[64,3072]{1,0:T(8,128)}, f32[16,40,128]{2,1,0:T(8,128)}) custom-call(bf16[640,1024]{1,0:T(8,128)(2,1)} %copy-done.10, bf16[640,1024]{1,0:T(8,128)(2,1)} %get-tuple-element.20.o_ref.refs_1_, bf16[640,1024]{1,0:T(8,128)(2,1)} %copy-done.8, bf16[640,1024]{1,0:T(8,128)(2,1)} %copy-done.7, ...), custom_call_target="tpu_custom_call" | custom-call | flops 13421772800 | bytes 18350080 | tf_op jit(solution)/shard_map/pallas_call | solution.py:649
  329.5 1.0 copy.22
  330.5 0.9 fusion.56
  331.4 1.6 fusion.54
  332.9 0.8 fusion.58
  333.8 2.0 fusion.67
  335.7 1.2 collective-permute-start.2
  337.0 0.6 dynamic-slice_reduce_fusion
  337.5 4.0 %fusion.50 = bf16[1,640,1024]{2,1,0:T(8,128)(2,1)} fusion(f32[640,1024]{1,0:T(8,128)} %get-tuple-element.42, f32[640]{0:T(1024)S(1)} %broadcast_multiply_fusion, f32[640]{0:T(1024)S(1)} %broadcast_multiply_fusion.1, f32[640]{0:T(1024)S(1)} %add_rsqrt_fusion.2, f32[640]{0:T(1024)S(1)} %broadcast_multiply_fusion.6, f32[1024]{0:T(1024)S(1)} %bitcast.87, ...), kind=kLoop, calls=%fused_computation.65 | loop fusion | flops 7864320 | bytes 9189376 | tf_op jit(solution)/shard_map/broadcast_in_dim | solution.py:813
  341.6 3.7 %collective-permute-done.2 = bf16[256,1024]{1,0:T(8,128)(2,1)S(1)} collective-permute-done((bf16[256,1024]{1,0:T(8,128)(2,1)}, bf16[256,1024]{1,0:T(8,128)(2,1)S(1)}, u32[]{:S(2)}, u32[]{:S(2)}) %collective-permute-start.2) | collective-permute-done | bytes 524320 | tf_op jit(solution)/shard_map/ppermute | solution.py:285
  345.3 1.2 convert_add_fusion.1
  346.4 0.9 copy.32
  347.3 0.7 copy.33
  348.0 1.0 copy.34
  (67 shorter events, 0.2 us)
Async XLA Ops:
  7.2 70.4 %copy-start = (bf16[1024,1024]{1,0:T(8,128)(2,1)S(1)}, bf16[1024,1024]{1,0:T(8,128)(2,1)}, u32[]{:S(2)}) copy-start(bf16[1024,1024]{1,0:T(8,128)(2,1)} %param.19) | copy-start | bytes 6291460
  7.2 328.6 %reduce-scatter.2.cloned.1.call-start = ((), (), s32[]{:S(2)}) async-start(), calls=%async_computation.1 | async-start | bytes 8912896 | tf_op jit(solution)/shard_map/reduce_scatter | solution.py:720
  7.2 32.1 %collective-permute-start = (bf16[640,1024]{1,0:T(8,128)(2,1)}, bf16[640,1024]{1,0:T(8,128)(2,1)}, u32[]{:S(2)}, u32[]{:S(2)}) collective-permute-start(bf16[640,1024]{1,0:T(8,128)(2,1)} %bitcast.76), channel_id=1, source_target_pairs={{1,0},{0,1},{3,2},{2,3},{5,4},{4,5},{7,6},{6,7},{9,8},{8,9},{11,10... | collective-permute-start | bytes 3932168 | tf_op jit(solution)/shard_map/ppermute | solution.py:683
  11.8 6.5 %copy-start.15 = (f32[4096]{0:T(1024)S(1)}, f32[4096]{0:T(1024)}, u32[]{:S(2)}) copy-start(f32[4096]{0:T(1024)} %param.17) | copy-start | bytes 49156
  11.8 7.6 %copy-start.4 = (bf16[1,640,1024]{2,1,0:T(8,128)(2,1)S(1)}, bf16[1,640,1024]{2,1,0:T(8,128)(2,1)}, u32[]{:S(2)}) copy-start(bf16[1,640,1024]{2,1,0:T(8,128)(2,1)} %param.11) | copy-start | bytes 3932164
  40.9 4.5 %copy-start.18 = (bf16[1024,3072]{1,0:T(8,128)(2,1)S(1)}, bf16[1024,3072]{1,0:T(8,128)(2,1)}, u32[]{:S(2)}) copy-start(bf16[1024,3072]{1,0:T(8,128)(2,1)} %param.18) | copy-start | bytes 18874372
  45.4 4.3 %copy-start.7 = (bf16[640,1024]{1,0:T(8,128)(2,1)}, bf16[640,1024]{1,0:T(8,128)(2,1)S(1)}, u32[]{:S(2)}) copy-start(bf16[640,1024]{1,0:T(8,128)(2,1)S(1)} %get-tuple-element.48.refs_3_) | copy-start | bytes 3932164
  45.4 4.3 %copy-start.8 = (bf16[640,1024]{1,0:T(8,128)(2,1)}, bf16[640,1024]{1,0:T(8,128)(2,1)S(1)}, u32[]{:S(2)}) copy-start(bf16[640,1024]{1,0:T(8,128)(2,1)S(1)} %get-tuple-element.49.refs_2_) | copy-start | bytes 3932164
  80.5 1.6 copy-start.2
  82.6 23.5 %copy-start.10 = (bf16[640,1024]{1,0:T(8,128)(2,1)}, bf16[640,1024]{1,0:T(8,128)(2,1)S(1)}, u32[]{:S(2)}) copy-start(bf16[640,1024]{1,0:T(8,128)(2,1)S(1)} %add_convert_fusion.1.refs_0_) | copy-start | bytes 3932164
  82.6 25.8 %copy-start.5 = (bf16[1,640,1024]{2,1,0:T(8,128)(2,1)S(1)}, bf16[1,640,1024]{2,1,0:T(8,128)(2,1)}, u32[]{:S(2)}) copy-start(bf16[1,640,1024]{2,1,0:T(8,128)(2,1)} %param.12) | copy-start | bytes 3932164
  106.0 2.3 copy-start.23
  117.4 12.5 %copy-start.3 = (f32[640,1024]{1,0:T(8,128)S(1)}, f32[640,1024]{1,0:T(8,128)}, u32[]{:S(2)}) copy-start(f32[640,1024]{1,0:T(8,128)} %copy-done.2) | copy-start | bytes 7864324
  129.9 11.5 %copy-start.24 = (bf16[640,4096]{1,0:T(8,128)(2,1)}, bf16[640,4096]{1,0:T(8,128)(2,1)S(1)}, u32[]{:S(2)}) copy-start(bf16[640,4096]{1,0:T(8,128)(2,1)S(1)} %fusion.5.refs_4_) | copy-start | bytes 15728644
  129.9 11.5 %copy-start.6 = (bf16[1,640,1024]{2,1,0:T(8,128)(2,1)S(1)}, bf16[1,640,1024]{2,1,0:T(8,128)(2,1)}, u32[]{:S(2)}) copy-start(bf16[1,640,1024]{2,1,0:T(8,128)(2,1)} %param.12) | copy-start | bytes 3932164
  143.8 2.6 copy-start.9
  188.0 3.8 %copy-start.20 = (bf16[640,1024]{1,0:T(8,128)(2,1)S(1)}, bf16[640,1024]{1,0:T(8,128)(2,1)}, u32[]{:S(2)}) copy-start(bf16[640,1024]{1,0:T(8,128)(2,1)} %get-tuple-element.25.refs_8_) | copy-start | bytes 3932164
  188.1 9.6 %slice-start.2 = ((s8[6291456]{0:T(1024)(128)(4,1)}), s8[4194304]{0:T(1024)(128)(4,1)S(1)}, s32[]{:S(2)}) async-start(s8[6291456]{0:T(1024)(128)(4,1)} %bitcast.95), calls=%async_computation.4 | async-start | bytes 8388608
  191.8 5.8 %slice-start.3 = ((s8[6291456]{0:T(1024)(128)(4,1)}), s8[2097152]{0:T(1024)(128)(4,1)S(1)}, s32[]{:S(2)}) async-start(s8[6291456]{0:T(1024)(128)(4,1)} %bitcast.95), calls=%async_computation.5 | async-start | bytes 4194304
  191.9 5.8 %copy-start.21 = (bf16[640,1024]{1,0:T(8,128)(2,1)S(1)}, bf16[640,1024]{1,0:T(8,128)(2,1)}, u32[]{:S(2)}) copy-start(bf16[640,1024]{1,0:T(8,128)(2,1)} %get-tuple-element.22.refs_6_) | copy-start | bytes 3932164
  191.9 9.0 %slice-start.4 = ((s8[5242880]{0:T(1024)(128)(4,1)}), s8[4194304]{0:T(1024)(128)(4,1)S(1)}, s32[]{:S(2)}) async-start(s8[5242880]{0:T(1024)(128)(4,1)} %bitcast.97), calls=%async_computation.6 | async-start | bytes 8388608
  195.8 30.1 %collective-permute-start.1 = (bf16[640,1024]{1,0:T(8,128)(2,1)S(1)}, bf16[640,1024]{1,0:T(8,128)(2,1)S(1)}, u32[]{:S(2)}, u32[]{:S(2)}) collective-permute-start(bf16[640,1024]{1,0:T(8,128)(2,1)S(1)} %get-tuple-element.43), channel_id=1, source_target_pairs={{0,1},{1,0},{2,3},{3,2},{4,5},{5,4},{6,7},{7,6},{8,9},{9,8},{10,11... | collective-permute-start | bytes 3932168 | tf_op jit(solution)/shard_map/ppermute | solution.py:686
  197.7 1.6 copy-start.22
  197.7 3.2 slice-start
  197.7 3.2 slice-start.5
  199.3 2.8 slice-start.1
  202.1 23.8 %copy-start.19 = (bf16[640,1024]{1,0:T(8,128)(2,1)S(1)}, bf16[640,1024]{1,0:T(8,128)(2,1)}, u32[]{:S(2)}) copy-start(bf16[640,1024]{1,0:T(8,128)(2,1)} %get-tuple-element.23.refs_7_) | copy-start | bytes 3932164
  225.9 3.9 %copy-start.17 = (pred[1,8]{1,0:T(4,128)(4,1)S(1)}, pred[1,8]{1,0:T(4,128)(4,1)}, u32[]{:S(2)}) copy-start(pred[1,8]{1,0:T(4,128)(4,1)} %iota_compare_fusion) | copy-start | bytes 28
  229.8 0.6 copy-start.16
  335.7 9.5 %collective-permute-start.2 = (bf16[256,1024]{1,0:T(8,128)(2,1)}, bf16[256,1024]{1,0:T(8,128)(2,1)S(1)}, u32[]{:S(2)}, u32[]{:S(2)}) collective-permute-start(bf16[256,1024]{1,0:T(8,128)(2,1)} %reduce-scatter.2.cloned.1.call-done), channel_id=1, source_target_pairs={{0,1},{1,0},{2,3},{3,2},{4,5},{5,4},{6,7},{7,6},{8,9},{9,8},{10,11... | collective-permute-start | bytes 1572872 | tf_op jit(solution)/shard_map/ppermute | solution.py:285
  337.5 7.7 %copy-start.13 = (bf16[256,1024]{1,0:T(8,128)(2,1)S(1)}, bf16[256,1024]{1,0:T(8,128)(2,1)}, u32[]{:S(2)}) copy-start(bf16[256,1024]{1,0:T(8,128)(2,1)} %reduce-scatter.2.cloned.1.call-done) | copy-start | bytes 1572868
  341.6 4.8 %copy-start.12 = (f32[64,3072]{1,0:T(8,128)S(1)}, f32[64,3072]{1,0:T(8,128)}, u32[]{:S(2)}) copy-start(f32[64,3072]{1,0:T(8,128)} %get-tuple-element.73) | copy-start | bytes 2359300
  341.6 5.7 %copy-start.14 = (f32[64,1024]{1,0:T(8,128)S(1)}, f32[64,1024]{1,0:T(8,128)}, u32[]{:S(2)}) copy-start(f32[64,1024]{1,0:T(8,128)} %get-tuple-element.74) | copy-start | bytes 786436
  341.6 6.4 %copy-start.11 = (f32[64,4096]{1,0:T(8,128)S(1)}, f32[64,4096]{1,0:T(8,128)}, u32[]{:S(2)}) copy-start(f32[64,4096]{1,0:T(8,128)} %get-tuple-element.75) | copy-start | bytes 3145732
  345.3 3.7 %copy-start.1 = (bf16[1024,1024]{1,0:T(8,128)(2,1)S(1)}, bf16[1024,1024]{1,0:T(8,128)(2,1)}, u32[]{:S(2)}) copy-start(bf16[1024,1024]{1,0:T(8,128)(2,1)} %param.19) | copy-start | bytes 6291460
Sparse Core Ops, SparseCore 0:
  117.6 104.9 reduce-scatter.1

commit v3 on v1

--- a/solution.py
+++ b/solution.py
@@ -188,6 +188,12 @@
     )(lim, qkv, qkv, qkv, kv_rest, kv_rest, do, o, lse)
 
 
+def outer_sum(left, right):
+    return lax.dot_general(
+        left, right, (((0,), (0,)), ((), ())), preferred_element_type=jnp.float32
+    )
+
+
 def outer_kernel(plan, halves, first_tiles, side_ref, *refs):
     lefts, plan_rights, outs, turned = refs[: plan[0]], refs[plan[0] : plan[1]], refs[plan[1] : plan[1] + 4], refs[plan[1] + 4 :]
     step = pl.program_id(0)
@@ -346,6 +352,432 @@
     return values
 
 
+LAG = 2
+MESH = pl.DeviceIdType.MESH
+
+
+def attention_step(step, lim_ref, q_ref, ko_ref, vo_ref, kt_ref, vt_ref, do_ref, o_ref, lse_ref,
+                   dq_ref, dko_ref, dvo_ref, dkt_ref, dvt_ref, qa_ref, doa_ref, dq_sum):
+    rows = q_ref.shape[0]
+    head, j = (step // 2) % 2, step % 2
+    lane = lax.broadcasted_iota(jnp.int32, (1, 128), 1)
+    own = (lane // 64) == head
+    f = 64 * (1 - head)
+
+    @pl.when(j == 0)
+    def _():
+        q = q_ref[...].astype(jnp.float32) * 0.125
+        do = do_ref[...].astype(jnp.float32)
+        prod = do * o_ref[...].astype(jnp.float32)
+        lh, lm, ll = split3(lse_ref[...])
+        delta = jnp.sum(jnp.where(own, prod, 0.0), -1, keepdims=True)
+        dh, dm, dl = split3(delta)
+        qa_ref[...] = jnp.where(own, q, jnp.where(lane == f, 1.0, jnp.where(lane == f + 1, -lh, jnp.where(lane == f + 2, -lm, jnp.where(lane == f + 3, -ll, 0.0))))).astype(jnp.bfloat16)
+        doa_ref[...] = jnp.where(own, do, jnp.where(lane == f, -dh, jnp.where(lane == f + 1, -dm, jnp.where(lane == f + 2, -dl, 0.0)))).astype(jnp.bfloat16)
+
+    row = lax.broadcasted_iota(jnp.int32, (rows, 1), 0)
+    wide = lambda ref: ref[...].astype(jnp.float32)
+    k = jnp.where(j == 0, wide(ko_ref), wide(kt_ref))
+    v = jnp.where(j == 0, wide(vo_ref), wide(vt_ref))
+    kone = jnp.where((lane > f) & (lane <= f + 3), 1.0, 0.0)
+    vone = jnp.where((lane >= f) & (lane < f + 3), 1.0, 0.0)
+    bias = jnp.where(row < lim_ref[j], 0.0, -BIG)
+    ka = jnp.where(own, k, jnp.where(lane == f, bias, kone)).astype(jnp.bfloat16)
+    va = jnp.where(own, v, vone).astype(jnp.bfloat16)
+    qa, doa = qa_ref[...], doa_ref[...]
+    pt = jnp.exp(dot(ka, qa, 1, 1))
+    dpt = dot(va, doa, 1, 1)
+    dst = (pt * dpt).astype(jnp.bfloat16)
+    dv = dot(pt.astype(jnp.bfloat16), doa, 1, 0)
+    dk = dot(dst, qa, 1, 0)
+    part = dot(dst, ka, 0, 0)
+
+    def put(ref, values):
+        @pl.when(head == 0)
+        def _():
+            ref[...] = values.astype(ref.dtype)
+
+        @pl.when(head == 1)
+        def _():
+            ref[...] = jnp.where(lane < 64, wide(ref), values).astype(ref.dtype)
+
+    @pl.when(j == 0)
+    def _():
+        dq_sum[...] = part
+        put(dko_ref, dk)
+        put(dvo_ref, dv)
+
+    @pl.when(j == 1)
+    def _():
+        put(dq_ref, (dq_sum[...] + part) * 0.125)
+        put(dkt_ref, dk)
+        put(dvt_ref, dv)
+
+
+def sum_kernel(units, plan, layout, sides, *refs):
+    at = 0
+    parts = {}
+    for name, count in layout:
+        parts[name] = refs[at : at + count]
+        at += count
+    lefts, rights, outs, turned = (parts[name] for name in ("lefts", "rights", "outs", "turned"))
+    send, recv, keep = parts["send"], parts["recv"], parts["keep"]
+    out_sem, in_sem = parts["sems"]
+    stages = 4 + sides
+    cut = 256 // sides
+    tick = pl.program_id(0)
+    item, seq = lax.axis_index("items"), lax.axis_index("seq")
+    bit = lambda value, place: jnp.bitwise_and(value // (1 << place), 1)
+    core, y, z0, z1, x = bit(item, 0), bit(item, 1), bit(item, 2), bit(item, 3), seq
+    flip = lambda place: item + (1 - 2 * bit(item, place)) * (1 << place)
+    partners = {
+        "core": (flip(0), seq),
+        "y": (flip(1), seq),
+        "z0": (flip(2), seq),
+        "z1": (flip(3), seq),
+        "x": (item, 1 - seq),
+    }
+
+    @pl.when(tick == 0)
+    def _():
+        barrier = pltpu.get_barrier_semaphore()
+        for partner in partners.values():
+            pl.semaphore_signal(barrier, inc=1, device_id=partner, device_id_type=MESH)
+        pl.semaphore_wait(barrier, len(partners))
+
+    wide = lambda values: values.astype(jnp.float32)
+    low = lambda values: values.astype(jnp.bfloat16)
+
+    def choose(values, axis, which):
+        first = lax.index_in_dim(values, 0, axis, keepdims=False)
+        second = lax.index_in_dim(values, 1, axis, keepdims=False)
+        mine = jnp.where(which == 0, first, second)
+        other = jnp.where(which == 0, second, first)
+        return mine, other
+
+    table = {name: (i, to) for i, (name, to, _) in enumerate(HOPS[sides])}
+
+    def copy(name, unit):
+        number, to = table[name]
+        slot, landing = unit % 2, unit % 4
+        return pltpu.make_async_remote_copy(
+            src_ref=send[number].at[slot],
+            dst_ref=recv[number].at[landing],
+            send_sem=out_sem.at[number, slot],
+            recv_sem=in_sem.at[number, landing],
+            device_id=partners[to],
+            device_id_type=MESH,
+        )
+
+    def post(name, unit, mine, other):
+        number, _ = table[name]
+        keep[number][unit % 2] = mine
+        send[number][unit % 2] = low(other)
+        copy(name, unit).start()
+
+    def take(name, unit):
+        number, _ = table[name]
+        copy(name, unit).wait()
+        return keep[number][unit % 2] + wide(recv[number][unit % 4])
+
+    def stage_zero(unit):
+        at = 0
+        for count, terms, turns in plan:
+
+            @pl.when((unit >= at) & (unit < at + count))
+            def _(at=at, terms=terms, turns=turns):
+                for which, start in turns:
+
+                    @pl.when(unit == at + start)
+                    def _(which=which):
+                        turned[which][...] = lefts[which][...].T
+
+                place = 0
+                for segment, pairs in terms:
+
+                    @pl.when((unit >= at + place) & (unit < at + place + segment))
+                    def _(pairs=pairs):
+                        total = None
+                        for which, right in pairs:
+                            part = dot(turned[which][...], rights[right][...], 1, 0)
+                            total = part if total is None else total + part
+                        post("d", unit, *choose(total.reshape(8, 2, 64, 256), 1, core))
+
+                    place += segment
+
+            at += count
+
+    def stage_one(unit):
+        total = take("d", unit)
+        post("ay", unit, *choose(total[:, :, :cut].reshape(4, 2, 64, cut), 1, y))
+        if sides == 2:
+            post("bx", unit, *choose(total[:, :, cut:].reshape(8, 2, 32, cut), 1, x))
+
+    def stage_two(unit):
+        post("az", unit, *choose(take("ay", unit).reshape(2, 2, 64, cut), 1, z0))
+        if sides == 2:
+            post("by", unit, *choose(take("bx", unit).reshape(4, 2, 32, cut), 1, y))
+
+    def stage_three(unit):
+        post("aw", unit, *choose(take("az", unit), 0, z1))
+        if sides == 2:
+            post("bz", unit, *choose(take("by", unit).reshape(2, 2, 32, cut), 1, z0))
+
+    def stage_four(unit):
+        total = low(take("aw", unit))
+        post("ax", unit, wide(total), total)
+        if sides == 2:
+            post("bw", unit, *choose(take("bz", unit), 0, z1))
+
+    def stage_five(unit):
+        parts["last"][0][unit % 2] = take("ax", unit)
+        total = low(take("bw", unit))
+        post("bg", unit, wide(total), total)
+
+    def stage_final(unit):
+        if sides == 1:
+            block = take("ax", unit)
+        else:
+            number, _ = table["bg"]
+            copy("bg", unit).wait()
+            other = wide(recv[number][unit % 4])
+            mine = keep[number][unit % 2]
+            top = jnp.where(x == 0, mine, other)
+            bottom = jnp.where(x == 0, other, mine)
+            block = jnp.concatenate(
+                [parts["last"][0][unit % 2], jnp.concatenate([top, bottom], 0)], 1
+            )
+        at = 0
+        for (count, _, _), out in zip(plan, outs):
+
+            @pl.when((unit >= at) & (unit < at + count))
+            def _(out=out):
+                out[...] = block
+
+            at += count
+
+    steps = [stage_zero, stage_one, stage_two, stage_three, stage_four, stage_five][:stages]
+    steps.append(stage_final)
+    for number in range(stages, -1, -1):
+        unit = tick - LAG * number
+
+        @pl.when((unit >= 0) & (unit < units))
+        def _(number=number, unit=unit):
+            steps[number](unit)
+
+    if parts["attention"]:
+
+        @pl.when(tick < ATTENTION_STEPS)
+        def _():
+            attention_step(tick, *parts["attention"], *parts["grads"], *parts["held"])
+
+    if parts["vector"]:
+        vector, gathered_out = parts["vector"][0], parts["gathered"][0]
+        gathered, got_vector, vec_out, vec_in = parts["gather"]
+        give_ref, got_ref = parts["give"][0], parts["got"][0]
+        give_out, give_in = parts["give_sems"]
+        ticks = pl.num_programs(0)
+        chunk = give_ref.shape[0] // GIVES
+
+        def other_copy(source, target, out, into, to):
+            return pltpu.make_async_remote_copy(
+                src_ref=source,
+                dst_ref=target,
+                send_sem=out,
+                recv_sem=into,
+                device_id=partners[to],
+                device_id_type=MESH,
+            )
+
+        give_copy = lambda source, target: other_copy(
+            source, target, give_out.at[0], give_in.at[0], "x"
+        )
+
+        @pl.when(tick < GIVES)
+        def _():
+            run = pl.ds(pl.multiple_of(tick * chunk, chunk), chunk)
+            give_copy(give_ref.at[run], got_ref.at[run]).start()
+
+        @pl.when(tick == ticks - 1)
+        def _():
+            give_copy(give_ref, got_ref).wait()
+
+        first = other_copy(vector, got_vector, vec_out.at[0], vec_in.at[0], "x")
+        hops = []
+        for number, to in enumerate(("core", "y", "z0", "z1")):
+            count = 1 << number
+            run = gathered.at[pl.ds((item // count) * count, count)]
+            hops.append(other_copy(run, run, vec_out.at[number + 1], vec_in.at[number + 1], to))
+
+        @pl.when(tick == 0)
+        def _():
+            first.start()
+
+        @pl.when(tick == LAG)
+        def _():
+            first.wait()
+            heights = lax.broadcasted_iota(jnp.int32, vector.shape, 0)
+            gathered[item] = vector[...] + jnp.where(
+                heights < vector.shape[0] - 8, got_vector[...], 0.0
+            )
+            hops[0].start()
+
+        for number in range(4):
+
+            @pl.when(tick == LAG * (number + 2))
+            def _(number=number):
+                hops[number].wait()
+                if number < 3:
+                    hops[number + 1].start()
+                else:
+                    gathered_out[...] = gathered[...]
+
+
+ATTENTION_STEPS = 32
+GIVES = 20
+HOPS = {
+    1: [
+        ("d", "core", (8, 64, 256)),
+        ("ay", "y", (4, 64, 256)),
+        ("az", "z0", (2, 64, 256)),
+        ("aw", "z1", (64, 256)),
+        ("ax", "x", (64, 256)),
+    ],
+    2: [
+        ("d", "core", (8, 64, 256)),
+        ("ay", "y", (4, 64, 128)),
+        ("az", "z0", (2, 64, 128)),
+        ("aw", "z1", (64, 128)),
+        ("ax", "x", (64, 128)),
+        ("bx", "x", (8, 32, 128)),
+        ("by", "y", (4, 32, 128)),
+        ("bz", "z0", (2, 32, 128)),
+        ("bw", "z1", (32, 128)),
+        ("bg", "x", (32, 128)),
+    ],
+}
+
+
+def sum_weights(weights, lefts, sides, vector=None, share=None, attention=None):
+    tile = 256
+    stages = 4 + sides
+    rows = lefts[0].shape[1]
+    low = lambda *shape: pltpu.VMEM(shape, jnp.bfloat16)
+    full = lambda *shape: pltpu.VMEM(shape, jnp.float32)
+    units = sum(segment[0][1].shape[1] for weight in weights for segment in weight) // tile
+    inputs, outputs, scratch = [], [], []
+    for left in lefts:
+        spec = pl.BlockSpec(left.shape, lambda i: (0, 0), pipeline_mode=pl.Buffered(1))
+        inputs.append(("lefts", left, spec))
+        scratch.append(("turned", low(*left.shape[::-1])))
+    seen, plan = set(), []
+    at = flops = rights = 0
+    for weight in weights:
+        terms, turns = [], []
+        place = 0
+        for segment in weight:
+            count = segment[0][1].shape[1] // tile
+            pairs = []
+            for which, right in segment:
+                if which not in seen:
+                    seen.add(which)
+                    turns.append((which, place))
+                pairs.append((which, rights))
+                rights += 1
+                flops += 2 * rows * right.shape[0] * right.shape[1]
+                spec = pl.BlockSpec(
+                    (right.shape[0], tile),
+                    lambda i, start=at + place, count=count: (
+                        0,
+                        jnp.clip(i - start, 0, count - 1),
+                    ),
+                )
+                inputs.append(("rights", right, spec))
+            terms.append((count, tuple(pairs)))
+            place += count
+        plan.append((place, tuple(terms), tuple(turns)))
+        spec = pl.BlockSpec(
+            (64, tile),
+            lambda i, start=at, count=place: (
+                0,
+                jnp.clip(i - LAG * stages - start, 0, count - 1),
+            ),
+        )
+        outputs.append(("outs", jax.ShapeDtypeStruct((64, place * tile), jnp.float32), spec))
+        at += place
+    hops = HOPS[sides]
+    for _, _, shape in hops:
+        scratch.append(("send", low(2, *shape)))
+        scratch.append(("recv", low(4, *shape)))
+        scratch.append(("keep", full(2, *shape)))
+    scratch.append(("last", full(2, 64, 128)))
+    scratch.append(("sems", pltpu.SemaphoreType.DMA((len(hops), 2))))
+    scratch.append(("sems", pltpu.SemaphoreType.DMA((len(hops), 4))))
+    transcendentals = 0
+    if vector is not None:
+        anywhere = pl.BlockSpec(memory_space=pl.ANY)
+        inputs.append(("vector", vector, pl.BlockSpec(vector.shape, lambda i: (0, 0))))
+        inputs.append(("give", share, anywhere))
+        shape = (16,) + vector.shape
+        outputs.append(("gathered", jax.ShapeDtypeStruct(shape, jnp.float32), pl.BlockSpec(shape, lambda i: (0, 0, 0))))
+        outputs.append(("got", jax.ShapeDtypeStruct(share.shape, share.dtype), anywhere))
+        scratch += [("gather", full(*shape)), ("gather", full(*vector.shape))]
+        scratch += [("gather", pltpu.SemaphoreType.DMA((5,)))] * 2
+        scratch += [("give_sems", pltpu.SemaphoreType.DMA((1,)))] * 2
+    if attention is not None:
+        lim, qkv, kv_rest, do, o, lse = attention
+        count, width = do.shape
+        pairs = width // 128
+        place = lambda skip: pl.BlockSpec(
+            (count, 128), lambda i: (0, jnp.minimum(i // 4, pairs - 1) + skip)
+        )
+        inputs.append(("attention", lim, pl.BlockSpec(memory_space=pltpu.SMEM)))
+        for operand, skip in (
+            (qkv, 0),
+            (qkv, pairs),
+            (qkv, 2 * pairs),
+            (kv_rest, 0),
+            (kv_rest, pairs),
+            (do, 0),
+            (o, 0),
+            (lse, 0),
+        ):
+            inputs.append(("attention", operand, place(skip)))
+        for _ in range(5):
+            outputs.append(("grads", jax.ShapeDtypeStruct(do.shape, jnp.bfloat16), place(0)))
+        scratch += [("held", low(count, 128)), ("held", low(count, 128)), ("held", full(count, 128))]
+        flops += 40 * count * 2 * count * width
+        transcendentals += count * 2 * count * width // 64
+    groups = (
+        ("lefts", "rights", "vector", "give", "attention"),
+        ("outs", "gathered", "got", "grads"),
+        ("turned", "send", "recv", "keep", "last", "sems", "gather", "give_sems", "held"),
+    )
+    layout, ordered = [], []
+    for names, entries in zip(groups, (inputs, outputs, scratch)):
+        found = [[entry[1:] for entry in entries if entry[0] == name] for name in names]
+        layout += [(name, len(run)) for name, run in zip(names, found)]
+        ordered.append([entry for run in found for entry in run])
+    operands = [operand for operand, _ in ordered[0]]
+    results = pl.pallas_call(
+        functools.partial(sum_kernel, units, tuple(plan), tuple(layout), sides),
+        grid=(units + LAG * stages,),
+        in_specs=[spec for _, spec in ordered[0]],
+        out_specs=[spec for _, spec in ordered[1]],
+        out_shape=[shape for shape, _ in ordered[1]],
+        scratch_shapes=[shape for shape, in ordered[2]],
+        compiler_params=pltpu.CompilerParams(
+            vmem_limit_bytes=58 << 20, collective_id=sides - 1, has_side_effects=True
+        ),
+        cost_estimate=pl.CostEstimate(
+            flops=flops,
+            transcendentals=transcendentals,
+            bytes_accessed=sum(2 * operand.size for operand in operands),
+        ),
+    )(*operands)
+    return results
+
+
 def per_device(
     frames,
     cotangent,
@@ -388,6 +820,8 @@
     modulate = lambda normed: (normed * (1.0 + scale_one) + shift_one).astype(jnp.bfloat16)
     attn_in = modulate(normed_one)
     qkv = project(attn_in, w_qkv).astype(jnp.bfloat16)
+    grad_act = back_project(cotangent, w_down).astype(jnp.bfloat16)
+    others, qkv, grad_act = lax.optimization_barrier((others, qkv, grad_act))
     rest = jnp.concatenate(others) if len(others) > 1 else others[0]
     normed_rest, _ = normalize(rest.astype(jnp.float32))
     attn_rest = modulate(normed_rest)
@@ -398,46 +832,93 @@
     ffn_in = (normed_two * (1.0 + scale_two) + shift_two).astype(jnp.bfloat16)
     upper = project(ffn_in, w_up)
     act = gelu_exact(upper).astype(jnp.bfloat16)
+    grad_upper = (grad_act.astype(jnp.float32) * gelu_slope(upper)).astype(jnp.bfloat16)
     out_frames = (mid + project(act, w_down)).astype(jnp.bfloat16)
 
     grad_out = cotangent.astype(jnp.float32)
-    down_pieces = outer(side, [act], [[(0, cotangent)]], item_size, 256)
-    grad_upper = (back_project(cotangent, w_down) * gelu_slope(upper)).astype(jnp.bfloat16)
-    up_pieces = outer(side, [ffn_in], [[(0, grad_upper)]], item_size, 512)
-    grad_ffn_in = back_project(grad_upper, w_up)
+    fused = seq_size == 2 and item_size == 16 and width == 1024
+    if fused:
+        sum_down = lax.psum_scatter(
+            outer_sum(act, cotangent).astype(jnp.bfloat16),
+            "items",
+            scatter_dimension=0,
+            tiled=True,
+        )
+    else:
+        down_pieces = outer(side, [act], [[(0, cotangent)]], item_size, 256)
+    grad_ffn_in = lax.optimization_barrier(back_project(grad_upper, w_up))
     grad_scale_two = jnp.sum(grad_ffn_in * normed_two, 0)
     grad_shift_two = jnp.sum(grad_ffn_in, 0)
     grad_mid = grad_out + norm_back(grad_ffn_in * (1.0 + scale_two), normed_two, inv_two)
     grad_mid_low = grad_mid.astype(jnp.bfloat16)
-    out_pieces = outer(side, [att], [[(0, grad_mid_low)]], item_size, 512)
     grad_att = back_project(grad_mid_low, w_out).astype(jnp.bfloat16)
-    grad_query, grad_key, grad_value, key_rest, value_rest = attend_back(
-        limits, qkv, kv_rest, grad_att, att, lse
-    )
-    qkv_pieces = outer(
-        side,
-        [attn_in, attn_rest],
-        [
-            [(0, grad_query)],
-            [(0, grad_key), (1, key_rest)],
-            [(0, grad_value), (1, value_rest)],
-        ],
-        item_size,
-        512,
-    )
+    up_terms = [[(0, grad_upper)]]
+    out_terms = [[(1, grad_mid_low)]]
+    if fused:
+        sum_up, sum_out, grad_query, grad_key, grad_value, key_rest, value_rest = sum_weights(
+            [up_terms, out_terms],
+            [ffn_in, att],
+            2,
+            attention=(limits, qkv, kv_rest, grad_att, att, lse),
+        )
+    else:
+        grad_query, grad_key, grad_value, key_rest, value_rest = attend_back(
+            limits, qkv, kv_rest, grad_att, att, lse
+        )
+    qkv_terms = [
+        [(0, grad_query)],
+        [(0, grad_key), (1, key_rest)],
+        [(0, grad_value), (1, value_rest)],
+    ]
     w_key, w_value = w_qkv[:, width : 2 * width], w_qkv[:, 2 * width :]
     share = back_project(key_rest, w_key) + back_project(value_rest, w_value)
-    grad_rest = [
-        give(share[i * row_count : (i + 1) * row_count].astype(jnp.bfloat16), turn)
-        for i, turn in enumerate(turns)
-    ]
     partial = (
         back_project(grad_query, w_qkv[:, :width])
         + back_project(grad_key, w_key)
         + back_project(grad_value, w_value)
     )
+    partial, share = lax.optimization_barrier((partial, share))
+    share_low = share.astype(jnp.bfloat16)
     grad_scale_one = jnp.sum(partial * normed_one, 0) + jnp.sum(share * normed_rest, 0)
     grad_shift_one = jnp.sum(partial, 0) + jnp.sum(share, 0)
+    grad_modul = jnp.concatenate(
+        [grad_scale_one, grad_shift_one, grad_scale_two, grad_shift_two]
+    )[None, :]
+    if fused:
+        vector = jnp.concatenate(
+            [
+                grad_modul.reshape(4 * width // 128, 128),
+                jnp.pad(onehot, ((0, 7), (0, 128 - section_count))),
+            ]
+        )
+        sum_qkv, tagged, got_share = sum_weights(
+            [qkv_terms], [attn_in, attn_rest], 1, vector=vector, share=share_low
+        )
+        grad_rest = [got_share]
+        tagged = tagged[:, : 4 * width // 128 + 1].reshape(item_size, 4 * width + 128)
+        sum_down = sum_down.astype(jnp.float32) + swap(sum_down, "seq", 1).astype(jnp.float32)
+    else:
+        grad_rest = [
+            give(share_low[i * row_count : (i + 1) * row_count], turn)
+            for i, turn in enumerate(turns)
+        ]
+        shift = lambda terms, by: [[(i - by, right) for i, right in run] for run in terms]
+        sum_down = finish(down_pieces, "items", "seq")
+        sum_up = finish(outer(side, [ffn_in], up_terms, item_size, 512), "items", "seq")
+        sum_out = finish(
+            outer(side, [att], shift(out_terms, 1), item_size, 512), "items", "seq"
+        )
+        sum_qkv = finish(
+            outer(side, [attn_in, attn_rest], qkv_terms, item_size, 512),
+            "items",
+            "seq",
+        )
+        for bit in bits_of("seq"):
+            grad_modul = grad_modul + swap(grad_modul, "seq", bit)
+        tagged = jnp.concatenate(
+            [grad_modul, jnp.pad(onehot, ((0, 0), (0, 128 - section_count)))], -1
+        )
+        tagged = gather_items(tagged, "items")
     grad_attn_in = partial
     for got in grad_rest:
         grad_attn_in = grad_attn_in + got.astype(jnp.float32)
@@ -445,18 +926,6 @@
         grad_mid + norm_back(grad_attn_in * (1.0 + scale_one), normed_one, inv_one)
     ).astype(jnp.bfloat16)
 
-    sum_down = finish(down_pieces, "items", "seq")
-    sum_up = finish(up_pieces, "items", "seq")
-    sum_out = finish(out_pieces, "items", "seq")
-    sum_qkv = finish(qkv_pieces, "items", "seq")
-
-    grad_modul = jnp.concatenate(
-        [grad_scale_one, grad_shift_one, grad_scale_two, grad_shift_two]
-    )[None, :]
-    for bit in bits_of("seq"):
-        grad_modul = grad_modul + swap(grad_modul, "seq", bit)
-    tagged = jnp.concatenate([grad_modul, jnp.pad(onehot, ((0, 0), (0, 128 - section_count)))], -1)
-    tagged = gather_items(tagged, "items")
     modul_all, onehot_all = tagged[:, : 4 * width], tagged[:, 4 * width :][:, :section_count]
     block = width // item_size
     own_embed = lax.dynamic_slice_in_dim(section_embed, item_me * block, block, 1)

time: 455 us -> 361 us (0.79)
  waiting for transfers between devices: 157 us -> 7.01 us
  Pallas kernels: 111 us -> 181 us
  starting transfers between devices: 47.3 us -> 4.11 us
  between operations: 3.19 us -> 16.1 us
  other arithmetic: 32.4 us -> 44.6 us
  local copies, waits for them, and re-layouts: 0.18 us -> 11.2 us
  matrix products: 95.2 us -> 90.5 us
    ppermute x49 -> x1, waiting for transfers between devices: 138 us -> 6.99 us  [swap(): return lax.ppermute(values, axis, [(i, i ^ bit) for i in range(size)])]
    pallas_call x5 -> x2, Pallas kernels: 89.1 us -> 158 us  [sum_weights(): pl.pallas_call(functools.partial(sum_kernel, units, tuple(plan), tuple(la...]
    ppermute x49 -> x1, starting transfers between devices: 42.5 us -> 1.04 us  [swap(): return lax.ppermute(values, axis, [(i, i ^ bit) for i in range(size)])]
    ppermute x1, waiting for transfers between devices: 19 us -> 0.01 us  [per_device(): lax.ppermute(values, 'seq', [((i + turn) % seq_size, i) for i in range(se...]
    dot_general x8, matrix products: 47.1 us -> 35.3 us  [back_project(): lax.dot_general(flat, weight, (((1,), (1,)), ((), ())), preferred_element...]
    convert_element_type x1, other arithmetic: 2.41 us -> 13.9 us  [per_device(): grad_mid_low = grad_mid.astype(jnp.bfloat16)]
    unnamed x70 -> x76, local copies, waits for them, and re-layouts: 0.16 us -> 11.2 us
    dot_general x0 -> x1, matrix products: none -> 9.02 us  [outer_sum(): lax.dot_general(left, right, (((0,), (0,)), ((), ())), preferred_element_...]
  transfers between devices with their start and end apart: 51 -> 3, of which waited for: 25 -> 1; matrix products, arithmetic and copies ran while one was open for 12% -> 28% of each run, Pallas kernels for 16% -> 45%
where the time goes in v3:
time: 361 us; the launch traced here: 354 us
  Pallas kernels  181 us (50%)
  matrix products  90.5 us (25%)
  other arithmetic  44.6 us (12%)
  between operations  16.1 us (4%)
  local copies, waits for them, and re-layouts  11.2 us (3%)
  waiting for transfers between devices  7.01 us (2%)
  starting transfers between devices  4.11 us (1%)
    pallas_call x2, Pallas kernels, sum_weights(): pl.pallas_call(functools.partial(sum_kernel, units, tuple(plan), tuple(la...  158 us
    dot_general x8, matrix products, back_project(): lax.dot_general(flat, weight, (((1,), (1,)), ((), ())), preferred_element...  35.3 us
    dot_general x5, matrix products, project(): result = jnp.dot(flat, weight, preferred_element_type=jnp.float32)  34.3 us
    pallas_call x1, Pallas kernels, attend(): pl.pallas_call(functools.partial(fwd_kernel, rows, blocks), grid_spec=plt...  22.4 us
    convert_element_type x1, other arithmetic, per_device(): grad_mid_low = grad_mid.astype(jnp.bfloat16)  13.9 us
    unnamed x76, local copies, waits for them, and re-layouts  11.2 us
    dot_general x1, matrix products, outer_sum(): lax.dot_general(left, right, (((0,), (0,)), ((), ())), preferred_element_...  9.02 us
  transfers between devices with their start and end apart: 3, of which 1 were waited for; matrix products, arithmetic and copies ran while one was open for 28% of the time, Pallas kernels for 45%

profile of v3, /device:TPU:0, one launch (start us, length us, event | category | flops | bytes accessed | tf_op | source)
XLA Modules:
  0.0 354.2 jit_solution(2609095710455364760)
XLA Ops:
  7.2 0.0 copy-start
  7.2 0.0 reduce-scatter.2.cloned.1.call-start
  7.2 3.0 collective-permute-start
  10.3 1.6 convert_reduce_fusion
  13.2 0.9 convolution_bitcast_fusion
  14.1 0.0 copy-start.23
  14.1 0.0 copy-start.2
  14.1 5.8 %fusion.74 = f32[1,4096]{1,0:T(1,128)S(1)} fusion(f32[1024,1]{0,1:T(1,128)S(1)} %convolution_bitcast_fusion, bf16[1024,4096]{1,0:T(8,128)(2,1)} %param.16), kind=kOutput, calls=%fused_computation.113 | convolution fusion | flops 50331648 | bytes 8409088 | tf_op jit(solution)/shard_map/dot_general | solution.py:816
  19.9 0.5 fusion.32
  20.4 0.5 iota_compare_fusion
  20.9 0.5 fusion.25.refs_0_
  21.5 1.1 copy-done.11
  22.6 8.6 %convolution_convert_fusion.2.q_ref.ko_ref.vo_ref.refs_5_.refs_6_.refs_7_ = bf16[640,3072]{1,0:T(8,128)(2,1)} fusion(bf16[640,1024]{1,0:T(8,128)(2,1)S(1)} %fusion.25.refs_0_, bf16[1024,3072]{1,0:T(8,128)(2,1)} %param.18), kind=kOutput, calls=%fused_computation.11 | convolution fusion | flops 4028497920 | bytes 11534336 | tf_op jit(solution)/shard_map/dot_general | solution.py:46
  31.1 0.6 compare_select_fusion.lim_ref.refs_4_
  31.7 11.2 %convolution_convert_fusion.1 = bf16[640,4096]{1,0:T(8,128)(2,1)} fusion(bf16[4096,1024]{1,0:T(8,128)(2,1)} %param.21, bf16[1,640,1024]{2,1,0:T(8,128)(2,1)} %param.12), kind=kOutput, calls=%fused_computation.10 | convolution fusion | flops 5371330560 | bytes 14942208 | tf_op jit(solution)/shard_map/dot_general | solution.py:52
  43.0 1.6 convert_reduce_fusion.1
  44.5 1.8 fusion.33
  46.3 1.9 fusion.22.refs_1_
  48.2 1.1 copy-done.12
  49.3 4.2 %fusion.8.kt_ref.vt_ref.refs_8_.refs_9_ = bf16[640,2048]{1,0:T(8,128)(2,1)} fusion(bf16[640,1024]{1,0:T(8,128)(2,1)S(1)} %fusion.22.refs_1_, bf16[1024,3072]{1,0:T(8,128)(2,1)S(1)} %bitcast.85), kind=kOutput, calls=%fused_computation.19 | convolution fusion | flops 2685665280 | bytes 8126464 | tf_op jit(solution)/shard_map/dot_general | solution.py:46
  53.5 22.4 %shard_map.178 = (bf16[640,1024]{1,0:T(8,128)(2,1)}, f32[640,1024]{1,0:T(8,128)}) custom-call(s32[2]{0:T(128)} %compare_select_fusion.lim_ref.refs_4_, bf16[640,3072]{1,0:T(8,128)(2,1)} %convolution_convert_fusion.2.q_ref.ko_ref.vo_ref.refs_5_.refs_6_.refs_7_, bf16[640,3072]{1,0:T(8,128)(2,1)} %convolution_convert_fusion.2.q_ref.ko_ref.vo_ref.refs_5_.refs_6_.refs_7_, ...), custom_call_target="tpu_custom_call" | custom-call | flops 13421772800 | bytes 10485760 | tf_op jit(solution)/shard_map/pallas_call | solution.py:163
  75.9 2.9 fusion.73
  78.8 0.4 multiply_reduce_fusion.2
  79.2 1.1 copy-done.3
  80.3 0.5 add_convert_fusion.1.refs_0_
  80.8 1.0 copy-done.13
  81.9 8.2 %fusion.75 = f32[640,4096]{1,0:T(8,128)S(1)} fusion(bf16[640,1024]{1,0:T(8,128)(2,1)S(1)} %add_convert_fusion.1.refs_0_, bf16[1024,4096]{1,0:T(8,128)(2,1)} %param.20), kind=kOutput, calls=%fused_computation.114 | convolution fusion | flops 5368709120 | bytes 20185088 | tf_op jit(solution)/shard_map/dot_general | solution.py:46
  90.1 6.8 %fusion.5 = (bf16[640,4096]{1,0:T(8,128)(2,1)}, bf16[640,4096]{1,0:T(8,128)(2,1)S(1)}) fusion(f32[640,4096]{1,0:T(8,128)S(1)} %fusion.75, bf16[640,4096]{1,0:T(8,128)(2,1)S(1)} %bitcast.78), kind=kLoop, calls=%fused_computation.6 | loop fusion | flops 36700160 | bytes 26214400 | tf_op jit(solution)/shard_map/convert_element_type | solution.py:835
  96.9 2.4 copy-done.6
  99.3 9.0 %convolution_convert_fusion = bf16[4096,1024]{1,0:T(8,128)(2,1)} fusion(bf16[640,4096]{1,0:T(8,128)(2,1)S(1)} %get-tuple-element.56, bf16[1,640,1024]{2,1,0:T(8,128)(2,1)S(1)} %copy-done.8), kind=kOutput, calls=%fused_computation.9 | convolution fusion | flops 5372903424 | bytes 14942208 | tf_op jit(solution)/shard_map/dot_general | solution.py:192
  108.3 0.0 reduce-scatter.2.cloned.1.call-update
  108.3 9.8 %fusion.76 = f32[640,1024]{1,0:T(8,128)S(1)} fusion(bf16[640,4096]{1,0:T(8,128)(2,1)} %get-tuple-element.55.refs_2_, bf16[1024,4096]{1,0:T(8,128)(2,1)} %param.20), kind=kOutput, calls=%fused_computation.115 | convolution fusion | flops 5368709120 | bytes 16252928 | tf_op jit(solution)/shard_map/dot_general | solution.py:52
  118.1 0.0 copy-start.9
  118.1 1.2 multiply_reduce_fusion
  119.4 0.2 copy-done.9
  119.5 13.9 %fusion.72 = (bf16[640,1024]{1,0:T(8,128)(2,1)S(1)}, f32[640,1024]{1,0:T(8,128)}) fusion(f32[640]{0:T(1024)S(1)} %broadcast_multiply_fusion.2, f32[640]{0:T(1024)S(1)} %add_rsqrt_fusion, f32[640,1024]{1,0:T(8,128)S(1)} %copy-done.4, f32[640]{0:T(1024)S(1)} %broadcast_multiply_fusion.4, f32[640]{0:T(1024)S(1)} %broadcast_multiply_fusion.3, ...), kind=kLoop, calls=%fused_computation.111 | loop fusion | flops 6553600 | bytes 10500096 | tf_op jit(solution)/shard_map/convert_element_type | solution.py:853
  133.4 2.6 convolution_convert_fusion.3.refs_10_
  136.1 100.6 %shard_map.179 = (f32[64,4096]{1,0:T(8,128)}, f32[64,1024]{1,0:T(8,128)}, bf16[640,1024]{1,0:T(8,128)(2,1)}, bf16[640,1024]{1,0:T(8,128)(2,1)}, bf16[640,1024]{1...) custom-call(bf16[640,1024]{1,0:T(8,128)(2,1)} %copy-done.13, ...), custom_call_target="tpu_custom_call" | custom-call | flops 40265318400 | bytes 30146564 | tf_op jit(solution)/shard_map/pallas_call | solution.py:762
  236.7 0.0 slice-start.4
  236.7 3.7 %fusion.36 = f32[640,1024]{1,0:T(8,128)S(1)} fusion(bf16[640,1024]{1,0:T(8,128)(2,1)} %get-tuple-element.35.refs_6_, bf16[1024,3072]{1,0:T(8,128)(2,1)} %param.18), kind=kOutput, calls=%fused_computation.55 | convolution fusion | flops 1342177280 | bytes 6029312 | tf_op jit(solution)/shard_map/dot_general | solution.py:52
  240.4 0.0 slice-start.5
  240.4 3.3 fusion.34
  243.8 1.6 fusion.38
  245.4 1.6 fusion.44
  247.0 0.0 copy-start.22
  247.0 1.6 add_add_fusion
  248.6 4.0 %fusion.70 = (f32[1024]{0:T(1024)S(1)}, f32[1024]{0:T(1024)S(1)}, bf16[640,1024]{1,0:T(8,128)(2,1)}, f32[1024]{0:T(1024)S(1)}, f32[1024]{0:T(1024)S(1)}) fusion(f32[640,1024]{1,0:T(8,128)S(1)} %fusion.44, f32[640]{0:T(1024)S(1)} %add_rsqrt_fusion.1, f32[640]{0:T(1024)S(1)} %broadcast_multiply_fusion.5, bf16[640,1024]{1,0:T(8,128)(2,1)} %collective-permute-done, ...), kind=kLoop, calls=%fused_computation.109 | loop fusion | flops 8515584 | bytes 9201664 | tf_op jit(solution)/shard_map/reduce_sum | solution.py:883
  252.6 0.6 copy-done.24
  253.2 57.7 %shard_map.180 = (f32[64,3072]{1,0:T(8,128)}, f32[16,40,128]{2,1,0:T(8,128)}, bf16[640,1024]{1,0:T(8,128)(2,1)}) custom-call(bf16[640,1024]{1,0:T(8,128)(2,1)} %copy-done.11, bf16[640,1024]{1,0:T(8,128)(2,1)} %copy-done.12, bf16[640,1024]{1,0:T(8,128)(2,1)} %get-tuple-element.31.refs_2_, bf16[640,1024]{1,0:T(8,128)(2,1)} %get-tuple-element.32.refs_3_, ...), custom_call_target="tpu_custom_call" | custom-call | flops 6710886400 | bytes 10496000 | tf_op jit(solution)/shard_map/pallas_call | solution.py:762
  311.0 1.0 copy.22
  312.0 3.1 fusion.53
  315.1 0.9 fusion.56
  316.0 1.6 fusion.54
  317.5 0.8 fusion.58
  318.3 2.0 fusion.67
  320.3 10.4 %fusion.49 = bf16[1,640,1024]{2,1,0:T(8,128)(2,1)} fusion(f32[640,1024]{1,0:T(8,128)S(1)} %copy-done.4, bf16[640,4096]{1,0:T(8,128)(2,1)} %copy-done.6, bf16[4096,1024]{1,0:T(8,128)(2,1)} %param.21), kind=kOutput, calls=%fused_computation.65 | convolution fusion | flops 5370019840 | bytes 17563648 | tf_op jit(solution)/shard_map/dot_general | solution.py:46
  330.8 1.0 collective-permute-start.1
  331.8 0.6 dynamic-slice_reduce_fusion
  332.4 4.0 %fusion.50 = bf16[1,640,1024]{2,1,0:T(8,128)(2,1)} fusion(f32[640,1024]{1,0:T(8,128)} %get-tuple-element.54, f32[640]{0:T(1024)S(1)} %broadcast_multiply_fusion, f32[640]{0:T(1024)S(1)} %broadcast_multiply_fusion.1, f32[640]{0:T(1024)S(1)} %copy-done.22, f32[640]{0:T(1024)S(1)} %copy-done.20, f32[1024]{0:T(1024)S(1)} %bitcast.92, f32[640,1024]{1,0:T(8,128)} %copy-done.5, ...), kind=kLoop, calls=%fused_computation.66 | loop fusion | flops 7864320 | bytes 9189376 | tf_op jit(solution)/shard_map/broadcast_in_dim | solution.py:944
  336.4 7.0 %collective-permute-done.1 = bf16[256,1024]{1,0:T(8,128)(2,1)S(1)} collective-permute-done((bf16[256,1024]{1,0:T(8,128)(2,1)}, bf16[256,1024]{1,0:T(8,128)(2,1)S(1)}, u32[]{:S(2)}, u32[]{:S(2)}) %collective-permute-start.1) | collective-permute-done | bytes 524320 | tf_op jit(solution)/shard_map/ppermute | solution.py:285
  343.4 1.2 convert_add_fusion.1
  344.6 0.9 copy.32
  345.5 0.7 copy.33
  346.2 1.0 copy.34
  (79 shorter events, 0.2 us)
Async XLA Ops:
  7.2 68.7 %copy-start = (bf16[1024,1024]{1,0:T(8,128)(2,1)S(1)}, bf16[1024,1024]{1,0:T(8,128)(2,1)}, u32[]{:S(2)}) copy-start(bf16[1024,1024]{1,0:T(8,128)(2,1)} %param.19) | copy-start | bytes 6291460
  7.2 323.6 %reduce-scatter.2.cloned.1.call-start = ((), (), s32[]{:S(2)}) async-start(), calls=%async_computation.1 | async-start | bytes 8912896 | tf_op jit(solution)/shard_map/reduce_scatter | solution.py:841
  7.2 35.7 %collective-permute-start = (bf16[640,1024]{1,0:T(8,128)(2,1)}, bf16[640,1024]{1,0:T(8,128)(2,1)}, u32[]{:S(2)}, u32[]{:S(2)}) collective-permute-start(bf16[640,1024]{1,0:T(8,128)(2,1)} %bitcast.76), channel_id=1, source_target_pairs={{1,0},{0,1},{3,2},{2,3},{5,4},{4,5},{7,6},{6,7},{9,8},{8,9},{11,10... | collective-permute-start | bytes 3932168 | tf_op jit(solution)/shard_map/ppermute | solution.py:801
  14.1 5.8 %copy-start.23 = (f32[4096]{0:T(1024)S(1)}, f32[4096]{0:T(1024)}, u32[]{:S(2)}) copy-start(f32[4096]{0:T(1024)} %param.17) | copy-start | bytes 49156
  14.1 5.8 %copy-start.2 = (bf16[1,640,1024]{2,1,0:T(8,128)(2,1)S(1)}, bf16[1,640,1024]{2,1,0:T(8,128)(2,1)}, u32[]{:S(2)}) copy-start(bf16[1,640,1024]{2,1,0:T(8,128)(2,1)} %param.11) | copy-start | bytes 3932164
  19.9 11.2 %copy-start.19 = (f32[640]{0:T(1024)}, f32[640]{0:T(1024)S(1)}, u32[]{:S(2)}) copy-start(f32[640]{0:T(1024)S(1)} %broadcast_multiply_fusion.6) | copy-start | bytes 7684
  20.4 10.7 %copy-start.21 = (f32[640]{0:T(1024)}, f32[640]{0:T(1024)S(1)}, u32[]{:S(2)}) copy-start(f32[640]{0:T(1024)S(1)} %add_rsqrt_fusion.2) | copy-start | bytes 7684
  21.5 1.1 copy-start.11
  31.1 18.1 %slice-start.2 = ((s8[6291456]{0:T(1024)(128)(4,1)}), s8[4194304]{0:T(1024)(128)(4,1)S(1)}, s32[]{:S(2)}) async-start(s8[6291456]{0:T(1024)(128)(4,1)} %bitcast.84), calls=%async_computation.4 | async-start | bytes 8388608
  31.7 17.6 %slice-start.3 = ((s8[6291456]{0:T(1024)(128)(4,1)}), s8[2097152]{0:T(1024)(128)(4,1)S(1)}, s32[]{:S(2)}) async-start(s8[6291456]{0:T(1024)(128)(4,1)} %bitcast.84), calls=%async_computation.5 | async-start | bytes 4194304
  48.2 1.1 copy-start.12
  78.8 1.5 copy-start.3
  80.3 9.7 %slice-start = ((s8[5242880]{0:T(1024)(128)(4,1)}), s8[4194304]{0:T(1024)(128)(4,1)S(1)}, s32[]{:S(2)}) async-start(s8[5242880]{0:T(1024)(128)(4,1)} %bitcast.77), calls=%async_computation.2 | async-start | bytes 8388608
  80.8 1.1 copy-start.13
  81.9 8.2 %slice-start.1 = ((s8[5242880]{0:T(1024)(128)(4,1)}), s8[1048576]{0:T(1024)(128)(4,1)S(1)}, s32[]{:S(2)}) async-start(s8[5242880]{0:T(1024)(128)(4,1)} %bitcast.77), calls=%async_computation.3 | async-start | bytes 2097152
  90.1 9.2 %copy-start.8 = (bf16[1,640,1024]{2,1,0:T(8,128)(2,1)S(1)}, bf16[1,640,1024]{2,1,0:T(8,128)(2,1)}, u32[]{:S(2)}) copy-start(bf16[1,640,1024]{2,1,0:T(8,128)(2,1)} %param.12) | copy-start | bytes 3932164
  96.9 2.4 copy-start.6
  108.3 9.8 %copy-start.4 = (f32[640,1024]{1,0:T(8,128)S(1)}, f32[640,1024]{1,0:T(8,128)}, u32[]{:S(2)}) copy-start(f32[640,1024]{1,0:T(8,128)} %copy-done.3) | copy-start | bytes 7864324
  118.1 1.4 copy-start.9
  133.4 2.6 copy-start.10
  236.7 3.7 %copy-start.27 = (bf16[640,1024]{1,0:T(8,128)(2,1)S(1)}, bf16[640,1024]{1,0:T(8,128)(2,1)}, u32[]{:S(2)}) copy-start(bf16[640,1024]{1,0:T(8,128)(2,1)} %get-tuple-element.31.refs_2_) | copy-start | bytes 3932164
  236.7 7.1 %slice-start.4 = ((s8[6291456]{0:T(1024)(128)(4,1)}), s8[4194304]{0:T(1024)(128)(4,1)S(1)}, s32[]{:S(2)}) async-start(s8[6291456]{0:T(1024)(128)(4,1)} %bitcast.86), calls=%async_computation.6 | async-start | bytes 8388608
  240.4 3.4 slice-start.5
  240.4 3.4 copy-start.28
  243.8 1.6 copy-start.26
  245.4 1.6 copy-start.14
  247.0 1.6 copy-start.20
  247.0 1.6 copy-start.22
  248.6 4.0 %copy-start.5 = (f32[640,1024]{1,0:T(8,128)}, f32[640,1024]{1,0:T(8,128)S(1)}, u32[]{:S(2)}) copy-start(f32[640,1024]{1,0:T(8,128)S(1)} %add_add_fusion) | copy-start | bytes 7864324
  248.6 4.0 %copy-start.25 = (pred[1,8]{1,0:T(4,128)(4,1)S(1)}, pred[1,8]{1,0:T(4,128)(4,1)}, u32[]{:S(2)}) copy-start(pred[1,8]{1,0:T(4,128)(4,1)} %iota_compare_fusion) | copy-start | bytes 28
  252.6 0.6 copy-start.24
  320.3 12.1 %copy-start.7 = (bf16[640,1024]{1,0:T(8,128)(2,1)S(1)}, bf16[640,1024]{1,0:T(8,128)(2,1)}, u32[]{:S(2)}) copy-start(bf16[640,1024]{1,0:T(8,128)(2,1)} %get-tuple-element.38) | copy-start | bytes 3932164
  330.8 12.7 %collective-permute-start.1 = (bf16[256,1024]{1,0:T(8,128)(2,1)}, bf16[256,1024]{1,0:T(8,128)(2,1)S(1)}, u32[]{:S(2)}, u32[]{:S(2)}) collective-permute-start(bf16[256,1024]{1,0:T(8,128)(2,1)} %reduce-scatter.2.cloned.1.call-done), channel_id=1, source_target_pairs={{0,1},{1,0},{2,3},{3,2},{4,5},{5,4},{6,7},{7,6},{8,9},{9,8},{10,11... | collective-permute-start | bytes 1572872 | tf_op jit(solution)/shard_map/ppermute | solution.py:285
  332.4 11.0 %copy-start.17 = (bf16[256,1024]{1,0:T(8,128)(2,1)S(1)}, bf16[256,1024]{1,0:T(8,128)(2,1)}, u32[]{:S(2)}) copy-start(bf16[256,1024]{1,0:T(8,128)(2,1)} %reduce-scatter.2.cloned.1.call-done) | copy-start | bytes 1572868
  336.4 8.2 %copy-start.16 = (f32[64,3072]{1,0:T(8,128)S(1)}, f32[64,3072]{1,0:T(8,128)}, u32[]{:S(2)}) copy-start(f32[64,3072]{1,0:T(8,128)} %get-tuple-element.80) | copy-start | bytes 2359300
  336.4 9.0 %copy-start.18 = (f32[64,1024]{1,0:T(8,128)S(1)}, f32[64,1024]{1,0:T(8,128)}, u32[]{:S(2)}) copy-start(f32[64,1024]{1,0:T(8,128)} %get-tuple-element.81) | copy-start | bytes 786436
  336.4 9.7 %copy-start.15 = (f32[64,4096]{1,0:T(8,128)S(1)}, f32[64,4096]{1,0:T(8,128)}, u32[]{:S(2)}) copy-start(f32[64,4096]{1,0:T(8,128)} %get-tuple-element.82) | copy-start | bytes 3145732
  343.4 3.7 %copy-start.1 = (bf16[1024,1024]{1,0:T(8,128)(2,1)S(1)}, bf16[1024,1024]{1,0:T(8,128)(2,1)}, u32[]{:S(2)}) copy-start(bf16[1024,1024]{1,0:T(8,128)(2,1)} %param.19) | copy-start | bytes 6291460
Sparse Core Ops, SparseCore 0:
  108.5 133.0 reduce-scatter.1

commit v4 on v3

--- a/solution.py
+++ b/solution.py
@@ -188,12 +188,6 @@
     )(lim, qkv, qkv, qkv, kv_rest, kv_rest, do, o, lse)
 
 
-def outer_sum(left, right):
-    return lax.dot_general(
-        left, right, (((0,), (0,)), ((), ())), preferred_element_type=jnp.float32
-    )
-
-
 def outer_kernel(plan, halves, first_tiles, side_ref, *refs):
     lefts, plan_rights, outs, turned = refs[: plan[0]], refs[plan[0] : plan[1]], refs[plan[1] : plan[1] + 4], refs[plan[1] + 4 :]
     step = pl.program_id(0)
@@ -480,6 +474,25 @@
         copy(name, unit).wait()
         return keep[number][unit % 2] + wide(recv[number][unit % 4])
 
+    def turn(which, start):
+        left, target = lefts[which], turned[which]
+        halves = target.shape[0]
+        if halves == 1:
+
+            @pl.loop(0, target.shape[1] // 128)
+            def _(i):
+                run = pl.ds(pl.multiple_of(i * 128, 128), 128)
+                target[0, run] = left[:, run].T
+
+        else:
+
+            @pl.loop(0, 16)
+            def _(i):
+                block = left[:, pl.ds(pl.multiple_of(i * 256 + start * 128, 128), 128)].T
+                run = pl.ds(pl.multiple_of(i * 64, 64), 64)
+                target[0, run] = block[:64]
+                target[1, run] = block[64:]
+
     def stage_zero(unit):
         at = 0
         for count, terms, turns in plan:
@@ -489,8 +502,8 @@
                 for which, start in turns:
 
                     @pl.when(unit == at + start)
-                    def _(which=which):
-                        turned[which][...] = lefts[which][...].T
+                    def _(which=which, start=start):
+                        turn(which, start // 8)
 
                 place = 0
                 for segment, pairs in terms:
@@ -499,7 +512,8 @@
                     def _(pairs=pairs):
                         total = None
                         for which, right in pairs:
-                            part = dot(turned[which][...], rights[right][...], 1, 0)
+                            half = ((unit - at) // 4) % turned[which].shape[0]
+                            part = dot(turned[which][half], rights[right][...], 1, 0)
                             total = part if total is None else total + part
                         post("d", unit, *choose(total.reshape(8, 2, 64, 256), 1, core))
 
@@ -634,7 +648,7 @@
 
 
 ATTENTION_STEPS = 32
-GIVES = 20
+GIVES = 10
 HOPS = {
     1: [
         ("d", "core", (8, 64, 256)),
@@ -661,35 +675,40 @@
 def sum_weights(weights, lefts, sides, vector=None, share=None, attention=None):
     tile = 256
     stages = 4 + sides
-    rows = lefts[0].shape[1]
     low = lambda *shape: pltpu.VMEM(shape, jnp.bfloat16)
     full = lambda *shape: pltpu.VMEM(shape, jnp.float32)
-    units = sum(segment[0][1].shape[1] for weight in weights for segment in weight) // tile
+    deep = [lefts[weight[0][0][0]].shape[1] // 1024 for weight in weights]
+    units = sum(
+        segment[0][1].shape[1] * depth // tile
+        for weight, depth in zip(weights, deep)
+        for segment in weight
+    )
     inputs, outputs, scratch = [], [], []
     for left in lefts:
         spec = pl.BlockSpec(left.shape, lambda i: (0, 0), pipeline_mode=pl.Buffered(1))
         inputs.append(("lefts", left, spec))
-        scratch.append(("turned", low(*left.shape[::-1])))
+        scratch.append(("turned", low(1 + left.shape[1] // 2048 // 2, 1024, left.shape[0])))
     seen, plan = set(), []
     at = flops = rights = 0
-    for weight in weights:
+    for weight, depth in zip(weights, deep):
         terms, turns = [], []
         place = 0
         for segment in weight:
-            count = segment[0][1].shape[1] // tile
+            across = segment[0][1].shape[1] // tile
+            count = across * depth
             pairs = []
             for which, right in segment:
                 if which not in seen:
                     seen.add(which)
-                    turns.append((which, place))
+                    turns += [(which, place + more) for more in range(0, count if depth > 1 else 1, 8)]
                 pairs.append((which, rights))
                 rights += 1
-                flops += 2 * rows * right.shape[0] * right.shape[1]
+                flops += 2 * 1024 * depth * right.shape[0] * right.shape[1]
                 spec = pl.BlockSpec(
                     (right.shape[0], tile),
-                    lambda i, start=at + place, count=count: (
+                    lambda i, start=at + place, count=count, across=across: (
                         0,
-                        jnp.clip(i - start, 0, count - 1),
+                        lax.rem(jnp.clip(i - start, 0, count - 1), across),
                     ),
                 )
                 inputs.append(("rights", right, spec))
@@ -698,12 +717,13 @@
         plan.append((place, tuple(terms), tuple(turns)))
         spec = pl.BlockSpec(
             (64, tile),
-            lambda i, start=at, count=place: (
-                0,
-                jnp.clip(i - LAG * stages - start, 0, count - 1),
+            lambda i, start=at, count=place, across=place // depth: (
+                jnp.clip(i - LAG * stages - start, 0, count - 1) // across,
+                lax.rem(jnp.clip(i - LAG * stages - start, 0, count - 1), across),
             ),
         )
-        outputs.append(("outs", jax.ShapeDtypeStruct((64, place * tile), jnp.float32), spec))
+        shape = (64 * depth, place // depth * tile)
+        outputs.append(("outs", jax.ShapeDtypeStruct(shape, jnp.float32), spec))
         at += place
     hops = HOPS[sides]
     for _, _, shape in hops:
@@ -837,30 +857,22 @@
 
     grad_out = cotangent.astype(jnp.float32)
     fused = seq_size == 2 and item_size == 16 and width == 1024
-    if fused:
-        sum_down = lax.psum_scatter(
-            outer_sum(act, cotangent).astype(jnp.bfloat16),
-            "items",
-            scatter_dimension=0,
-            tiled=True,
-        )
-    else:
-        down_pieces = outer(side, [act], [[(0, cotangent)]], item_size, 256)
+    grad_upper, out_frames = lax.optimization_barrier((grad_upper, out_frames))
     grad_ffn_in = lax.optimization_barrier(back_project(grad_upper, w_up))
     grad_scale_two = jnp.sum(grad_ffn_in * normed_two, 0)
     grad_shift_two = jnp.sum(grad_ffn_in, 0)
     grad_mid = grad_out + norm_back(grad_ffn_in * (1.0 + scale_two), normed_two, inv_two)
     grad_mid_low = grad_mid.astype(jnp.bfloat16)
     grad_att = back_project(grad_mid_low, w_out).astype(jnp.bfloat16)
-    up_terms = [[(0, grad_upper)]]
-    out_terms = [[(1, grad_mid_low)]]
+    down_terms = [[(0, cotangent)]]
     if fused:
-        sum_up, sum_out, grad_query, grad_key, grad_value, key_rest, value_rest = sum_weights(
-            [up_terms, out_terms],
-            [ffn_in, att],
+        sum_down, sum_up, sum_out, *grads = sum_weights(
+            [down_terms, [[(1, grad_upper)]], [[(2, grad_mid_low)]]],
+            [act, ffn_in, att],
             2,
             attention=(limits, qkv, kv_rest, grad_att, att, lse),
         )
+        grad_query, grad_key, grad_value, key_rest, value_rest = grads
     else:
         grad_query, grad_key, grad_value, key_rest, value_rest = attend_back(
             limits, qkv, kv_rest, grad_att, att, lse
@@ -896,17 +908,15 @@
         )
         grad_rest = [got_share]
         tagged = tagged[:, : 4 * width // 128 + 1].reshape(item_size, 4 * width + 128)
-        sum_down = sum_down.astype(jnp.float32) + swap(sum_down, "seq", 1).astype(jnp.float32)
     else:
         grad_rest = [
             give(share_low[i * row_count : (i + 1) * row_count], turn)
             for i, turn in enumerate(turns)
         ]
-        shift = lambda terms, by: [[(i - by, right) for i, right in run] for run in terms]
-        sum_down = finish(down_pieces, "items", "seq")
-        sum_up = finish(outer(side, [ffn_in], up_terms, item_size, 512), "items", "seq")
+        sum_down = finish(outer(side, [act], down_terms, item_size, 256), "items", "seq")
+        sum_up = finish(outer(side, [ffn_in], [[(0, grad_upper)]], item_size, 512), "items", "seq")
         sum_out = finish(
-            outer(side, [att], shift(out_terms, 1), item_size, 512), "items", "seq"
+            outer(side, [att], [[(0, grad_mid_low)]], item_size, 512), "items", "seq"
         )
         sum_qkv = finish(
             outer(side, [attn_in, attn_rest], qkv_terms, item_size, 512),

time: 361 us -> 346 us (0.958)
  Pallas kernels: 181 us -> 208 us
  between operations: 16.1 us -> 2.73 us
  matrix products: 90.5 us -> 81.8 us
  waiting for transfers between devices: 7.01 us -> 0.01 us
  other arithmetic: 44.6 us -> 39.3 us
    pallas_call x2, Pallas kernels: 158 us -> 185 us  [sum_weights(): pl.pallas_call(functools.partial(sum_kernel, units, tuple(plan), tuple(la...]
    dot_general x1 -> x0, matrix products: 9.02 us -> none  [outer_sum(): lax.dot_general(left, right, (((0,), (0,)), ((), ())), preferred_element_...]
    ppermute x1 -> x0, waiting for transfers between devices: 6.99 us -> none  [swap(): return lax.ppermute(values, axis, [(i, i ^ bit) for i in range(size)])]
    unnamed x76 -> x73, local copies, waits for them, and re-layouts: 11.2 us -> 7.83 us
  transfers between devices with their start and end apart: 3 -> 1, of which waited for: 1 -> 0; matrix products, arithmetic and copies ran while one was open for 28% -> 9% of each run, Pallas kernels for 45% -> 0%
where the time goes in v4:
time: 346 us; the launch traced here: 342 us
  Pallas kernels  208 us (60%)
  matrix products  81.8 us (24%)
  other arithmetic  39.3 us (11%)
  local copies, waits for them, and re-layouts  7.86 us (2%)
    pallas_call x2, Pallas kernels, sum_weights(): pl.pallas_call(functools.partial(sum_kernel, units, tuple(plan), tuple(la...  185 us
    dot_general x5, matrix products, project(): result = jnp.dot(flat, weight, preferred_element_type=jnp.float32)  36.1 us
    dot_general x8, matrix products, back_project(): lax.dot_general(flat, weight, (((1,), (1,)), ((), ())), preferred_element...  33.9 us
    pallas_call x1, Pallas kernels, attend(): pl.pallas_call(functools.partial(fwd_kernel, rows, blocks), grid_spec=plt...  22.4 us
    convert_element_type x1, other arithmetic, per_device(): grad_mid_low = grad_mid.astype(jnp.bfloat16)  13.2 us
    convert_element_type x1, other arithmetic, per_device(): act = gelu_exact(upper).astype(jnp.bfloat16)  7.97 us
    unnamed x73, local copies, waits for them, and re-layouts  7.83 us
  transfers between devices with their start and end apart: 1, of which 0 were waited for; matrix products, arithmetic and copies ran while one was open for 9% of the time, Pallas kernels for 0%

profile of v4, /device:TPU:0, one launch (start us, length us, event | category | flops | bytes accessed | tf_op | source)
XLA Modules:
  0.0 342.4 jit_solution(1089790637008922509)
XLA Ops:
  0.6 0.0 copy-start
  0.7 3.0 collective-permute-start
  3.7 1.6 convert_reduce_fusion
  6.6 0.9 convolution_bitcast_fusion
  7.5 0.0 copy-start.23
  7.5 0.0 copy-start.2
  7.5 5.8 %fusion.72 = f32[1,4096]{1,0:T(1,128)S(1)} fusion(f32[1024,1]{0,1:T(1,128)S(1)} %convolution_bitcast_fusion, bf16[1024,4096]{1,0:T(8,128)(2,1)} %param.16), kind=kOutput, calls=%fused_computation.109 | convolution fusion | flops 50331648 | bytes 8409088 | tf_op jit(solution)/shard_map/dot_general | solution.py:836
  13.3 0.0 copy-start.21
  13.3 0.0 copy-start.17
  13.4 0.5 fusion.32
  13.8 0.0 copy-start.19
  13.9 0.6 iota_compare_fusion
  14.4 0.5 fusion.25.refs_0_
  15.0 1.1 copy-done.9
  16.1 8.6 %convolution_convert_fusion.1.q_ref.ko_ref.vo_ref.refs_7_.refs_8_.refs_9_ = bf16[640,3072]{1,0:T(8,128)(2,1)} fusion(bf16[640,1024]{1,0:T(8,128)(2,1)S(1)} %fusion.25.refs_0_, bf16[1024,3072]{1,0:T(8,128)(2,1)} %param.18), kind=kOutput, calls=%fused_computation.10 | convolution fusion | flops 4028497920 | bytes 11534336 | tf_op jit(solution)/shard_map/dot_general | solution.py:46
  24.7 0.6 compare_select_fusion.lim_ref.refs_6_
  25.2 11.2 %convolution_convert_fusion = bf16[640,4096]{1,0:T(8,128)(2,1)} fusion(bf16[4096,1024]{1,0:T(8,128)(2,1)} %param.21, bf16[1,640,1024]{2,1,0:T(8,128)(2,1)} %param.12), kind=kOutput, calls=%fused_computation.9 | convolution fusion | flops 5371330560 | bytes 14942208 | tf_op jit(solution)/shard_map/dot_general | solution.py:52
  36.5 0.0 collective-permute-done
  36.5 1.6 convert_reduce_fusion.1
  38.1 1.8 fusion.33
  39.9 1.9 fusion.22.refs_1_
  41.7 1.0 copy-done.10
  42.8 4.2 %fusion.8.kt_ref.vt_ref.refs_10_.refs_11_ = bf16[640,2048]{1,0:T(8,128)(2,1)} fusion(bf16[640,1024]{1,0:T(8,128)(2,1)S(1)} %fusion.22.refs_1_, bf16[1024,3072]{1,0:T(8,128)(2,1)S(1)} %bitcast.80), kind=kOutput, calls=%fused_computation.18 | convolution fusion | flops 2685665280 | bytes 8126464 | tf_op jit(solution)/shard_map/dot_general | solution.py:46
  47.0 22.4 %shard_map.178 = (bf16[640,1024]{1,0:T(8,128)(2,1)}, f32[640,1024]{1,0:T(8,128)}) custom-call(s32[2]{0:T(128)} %compare_select_fusion.lim_ref.refs_6_, bf16[640,3072]{1,0:T(8,128)(2,1)} %convolution_convert_fusion.1.q_ref.ko_ref.vo_ref.refs_7_.refs_8_.refs_9_, bf16[640,3072]{1,0:T(8,128)(2,1)} %convolution_convert_fusion.1.q_ref.ko_ref.vo_ref.refs_7_.refs_8_.refs_9_, ...), custom_call_target="tpu_custom_call" | custom-call | flops 13421772800 | bytes 10485760 | tf_op jit(solution)/shard_map/pallas_call | solution.py:163
  69.4 2.9 fusion.71
  72.4 0.4 multiply_reduce_fusion.2
  72.8 0.5 add_convert_fusion.1.refs_1_
  73.3 8.5 %fusion.73 = f32[640,4096]{1,0:T(8,128)S(1)} fusion(bf16[640,1024]{1,0:T(8,128)(2,1)S(1)} %add_convert_fusion.1.refs_1_, bf16[1024,4096]{1,0:T(8,128)(2,1)} %param.20), kind=kOutput, calls=%fused_computation.110 | convolution fusion | flops 5368709120 | bytes 20185088 | tf_op jit(solution)/shard_map/dot_general | solution.py:46
  81.8 8.0 %multiply_convert_fusion = (bf16[640,4096]{1,0:T(8,128)(2,1)S(1)}, bf16[640,4096]{1,0:T(8,128)(2,1)S(1)}) fusion(f32[640,4096]{1,0:T(8,128)S(1)} %fusion.73, bf16[640,4096]{1,0:T(8,128)(2,1)} %convolution_convert_fusion), kind=kLoop, calls=%fused_computation.7 | loop fusion | flops 36700160 | bytes 26214400 | tf_op jit(solution)/shard_map/convert_element_type | solution.py:854
  89.7 11.9 %add_convert_fusion = bf16[640,1024]{1,0:T(8,128)(2,1)} fusion(f32[640,1024]{1,0:T(8,128)S(1)} %get-tuple-element.69, bf16[640,4096]{1,0:T(8,128)(2,1)S(1)} %get-tuple-element.61.refs_0_, bf16[4096,1024]{1,0:T(8,128)(2,1)} %param.21), kind=kOutput, calls=%fused_computation.47 | convolution fusion | flops 5370019840 | bytes 17563648 | tf_op jit(solution)/shard_map/dot_general | solution.py:46
  101.7 8.3 %fusion.74 = f32[640,1024]{1,0:T(8,128)S(1)} fusion(bf16[640,4096]{1,0:T(8,128)(2,1)S(1)} %get-tuple-element.34.refs_4_, bf16[1024,4096]{1,0:T(8,128)(2,1)} %param.20), kind=kOutput, calls=%fused_computation.111 | convolution fusion | flops 5368709120 | bytes 16252928 | tf_op jit(solution)/shard_map/dot_general | solution.py:52
  110.0 0.0 copy-start.7
  110.1 1.2 multiply_reduce_fusion
  111.3 0.1 copy-done.7
  111.4 13.2 %fusion.70 = (bf16[640,1024]{1,0:T(8,128)(2,1)S(1)}, f32[640,1024]{1,0:T(8,128)}) fusion(f32[640]{0:T(1024)S(1)} %broadcast_multiply_fusion.2, f32[640]{0:T(1024)S(1)} %add_rsqrt_fusion, f32[640,1024]{1,0:T(8,128)S(1)} %get-tuple-element.69, f32[640]{0:T(1024)S(1)} %broadcast_multiply_fusion.4, f32[640]{0:T(1024)S(1)} %broadcast_multiply_fusion.3, ...), kind=kLoop, calls=%fused_computation.107 | loop fusion | flops 6553600 | bytes 10500096 | tf_op jit(solution)/shard_map/convert_element_type | solution.py:865
  124.6 2.6 convolution_convert_fusion.2.refs_12_
  127.2 128.0 %shard_map.179 = (f32[256,1024]{1,0:T(8,128)}, f32[64,4096]{1,0:T(8,128)}, f32[64,1024]{1,0:T(8,128)}, bf16[640,1024]{1,0:T(8,128)(2,1)}, bf16[640,1024]{1,0:T(8...) custom-call(bf16[640,4096]{1,0:T(8,128)(2,1)} %copy-done.4, ...), custom_call_target="tpu_custom_call" | custom-call | flops 45634027520 | bytes 36700164 | tf_op jit(solution)/shard_map/pallas_call | solution.py:782
  255.3 0.0 slice-start.2
  255.3 3.7 %fusion.36 = f32[640,1024]{1,0:T(8,128)S(1)} fusion(bf16[640,1024]{1,0:T(8,128)(2,1)} %get-tuple-element.40.refs_6_, bf16[1024,3072]{1,0:T(8,128)(2,1)} %param.18), kind=kOutput, calls=%fused_computation.54 | convolution fusion | flops 1342177280 | bytes 6029312 | tf_op jit(solution)/shard_map/dot_general | solution.py:52
  259.0 0.0 slice-start.3
  259.0 3.3 fusion.34
  262.4 1.6 fusion.38
  263.9 1.6 fusion.44
  265.5 0.0 copy-start.18
  265.5 0.0 copy-start.20
  265.5 1.6 add_add_fusion
  267.1 3.4 fusion.68
  270.6 0.0 copy-start.24
  270.6 0.6 copy-done.24
  271.2 57.1 %shard_map.180 = (f32[64,3072]{1,0:T(8,128)}, f32[16,40,128]{2,1,0:T(8,128)}, bf16[640,1024]{1,0:T(8,128)(2,1)}) custom-call(bf16[640,1024]{1,0:T(8,128)(2,1)} %copy-done.9, bf16[640,1024]{1,0:T(8,128)(2,1)} %copy-done.10, bf16[640,1024]{1,0:T(8,128)(2,1)} %get-tuple-element.36.refs_2_, bf16[640,1024]{1,0:T(8,128)(2,1)} %get-tuple-element.37.refs_3_, ...), custom_call_target="tpu_custom_call" | custom-call | flops 6710886400 | bytes 10496000 | tf_op jit(solution)/shard_map/pallas_call | solution.py:782
  328.3 0.0 copy-start.22
  328.3 1.1 copy.22
  329.5 0.9 fusion.53
  330.3 1.6 fusion.51
  331.9 2.0 fusion.65
  333.9 0.8 fusion.55
  334.7 1.0 fusion.50
  335.7 0.6 dynamic-slice_reduce_fusion
  336.3 0.2 copy-done.3
  336.5 2.1 fusion.49
  338.6 0.9 copy.33
  339.5 0.7 copy.34
  340.2 1.0 copy.35
  341.2 1.0 copy.36
  (68 shorter events, 0.2 us)
Async XLA Ops:
  0.6 68.8 %copy-start = (bf16[1024,1024]{1,0:T(8,128)(2,1)S(1)}, bf16[1024,1024]{1,0:T(8,128)(2,1)}, u32[]{:S(2)}) copy-start(bf16[1024,1024]{1,0:T(8,128)(2,1)} %param.19) | copy-start | bytes 6291460
  0.7 35.8 %collective-permute-start = (bf16[640,1024]{1,0:T(8,128)(2,1)}, bf16[640,1024]{1,0:T(8,128)(2,1)}, u32[]{:S(2)}, u32[]{:S(2)}) collective-permute-start(bf16[640,1024]{1,0:T(8,128)(2,1)} %bitcast.72), channel_id=1, source_target_pairs={{1,0},{0,1},{3,2},{2,3},{5,4},{4,5},{7,6},{6,7},{9,8},{8,9},{11,10... | collective-permute-start | bytes 3932168 | tf_op jit(solution)/shard_map/ppermute | solution.py:821
  7.5 5.8 %copy-start.23 = (f32[4096]{0:T(1024)S(1)}, f32[4096]{0:T(1024)}, u32[]{:S(2)}) copy-start(f32[4096]{0:T(1024)} %param.17) | copy-start | bytes 49156
  7.5 5.8 %copy-start.2 = (bf16[1,640,1024]{2,1,0:T(8,128)(2,1)S(1)}, bf16[1,640,1024]{2,1,0:T(8,128)(2,1)}, u32[]{:S(2)}) copy-start(bf16[1,640,1024]{2,1,0:T(8,128)(2,1)} %param.11) | copy-start | bytes 3932164
  13.3 26.6 %copy-start.21 = (f32[1,1024]{1,0:T(1,128)}, f32[1,1024]{1,0:T(1,128)S(1)}, u32[]{:S(2)}) copy-start(f32[1,1024]{1,0:T(1,128)S(1)} %get-tuple-element.67) | copy-start | bytes 12292
  13.3 11.3 %copy-start.17 = (f32[640]{0:T(1024)}, f32[640]{0:T(1024)S(1)}, u32[]{:S(2)}) copy-start(f32[640]{0:T(1024)S(1)} %broadcast_multiply_fusion.6) | copy-start | bytes 7684
  13.8 10.8 %copy-start.19 = (f32[640]{0:T(1024)}, f32[640]{0:T(1024)S(1)}, u32[]{:S(2)}) copy-start(f32[640]{0:T(1024)S(1)} %add_rsqrt_fusion.2) | copy-start | bytes 7684
  15.0 1.1 copy-start.9
  24.7 18.1 %slice-start = ((s8[6291456]{0:T(1024)(128)(4,1)}), s8[4194304]{0:T(1024)(128)(4,1)S(1)}, s32[]{:S(2)}) async-start(s8[6291456]{0:T(1024)(128)(4,1)} %bitcast.79), calls=%async_computation | async-start | bytes 8388608
  25.2 17.6 %slice-start.1 = ((s8[6291456]{0:T(1024)(128)(4,1)}), s8[2097152]{0:T(1024)(128)(4,1)S(1)}, s32[]{:S(2)}) async-start(s8[6291456]{0:T(1024)(128)(4,1)} %bitcast.79), calls=%async_computation.1 | async-start | bytes 4194304
  41.7 1.1 copy-start.10
  73.3 8.5 %copy-start.11 = (bf16[640,1024]{1,0:T(8,128)(2,1)}, bf16[640,1024]{1,0:T(8,128)(2,1)S(1)}, u32[]{:S(2)}) copy-start(bf16[640,1024]{1,0:T(8,128)(2,1)S(1)} %add_convert_fusion.1.refs_1_) | copy-start | bytes 3932164
  89.7 12.0 %copy-start.4 = (bf16[640,4096]{1,0:T(8,128)(2,1)}, bf16[640,4096]{1,0:T(8,128)(2,1)S(1)}, u32[]{:S(2)}) copy-start(bf16[640,4096]{1,0:T(8,128)(2,1)S(1)} %get-tuple-element.61.refs_0_) | copy-start | bytes 15728644
  89.7 11.9 %copy-start.5 = (bf16[640,4096]{1,0:T(8,128)(2,1)}, bf16[640,4096]{1,0:T(8,128)(2,1)S(1)}, u32[]{:S(2)}) copy-start(bf16[640,4096]{1,0:T(8,128)(2,1)S(1)} %get-tuple-element.34.refs_4_) | copy-start | bytes 15728644
  110.0 1.3 copy-start.7
  124.6 2.6 copy-start.8
  255.3 3.7 %copy-start.27 = (bf16[640,1024]{1,0:T(8,128)(2,1)S(1)}, bf16[640,1024]{1,0:T(8,128)(2,1)}, u32[]{:S(2)}) copy-start(bf16[640,1024]{1,0:T(8,128)(2,1)} %get-tuple-element.36.refs_2_) | copy-start | bytes 3932164
  255.3 7.0 %slice-start.2 = ((s8[6291456]{0:T(1024)(128)(4,1)}), s8[4194304]{0:T(1024)(128)(4,1)S(1)}, s32[]{:S(2)}) async-start(s8[6291456]{0:T(1024)(128)(4,1)} %bitcast.81), calls=%async_computation.2 | async-start | bytes 8388608
  259.0 3.3 slice-start.3
  259.0 3.3 copy-start.28
  262.3 1.6 copy-start.26
  263.9 1.6 copy-start.12
  265.5 1.6 copy-start.18
  265.5 1.6 copy-start.20
  267.1 3.5 %copy-start.25 = (pred[1,8]{1,0:T(4,128)(4,1)S(1)}, pred[1,8]{1,0:T(4,128)(4,1)}, u32[]{:S(2)}) copy-start(pred[1,8]{1,0:T(4,128)(4,1)} %iota_compare_fusion) | copy-start | bytes 28
  270.6 0.6 copy-start.24
  328.3 6.4 %copy-start.6 = (bf16[640,1024]{1,0:T(8,128)(2,1)S(1)}, bf16[640,1024]{1,0:T(8,128)(2,1)}, u32[]{:S(2)}) copy-start(bf16[640,1024]{1,0:T(8,128)(2,1)} %get-tuple-element.43) | copy-start | bytes 3932164
  328.3 6.4 %copy-start.22 = (f32[1,1024]{1,0:T(1,128)S(1)}, f32[1,1024]{1,0:T(1,128)}, u32[]{:S(2)}) copy-start(f32[1,1024]{1,0:T(1,128)} %copy-done.21) | copy-start | bytes 12292
  334.7 1.7 copy-start.3
  336.5 2.1 copy-start.15
  336.5 3.0 copy-start.16
  338.6 1.6 copy-start.14
  338.6 2.6 copy-start.13
  338.6 3.5 %copy-start.1 = (bf16[1024,1024]{1,0:T(8,128)(2,1)S(1)}, bf16[1024,1024]{1,0:T(8,128)(2,1)}, u32[]{:S(2)}) copy-start(bf16[1024,1024]{1,0:T(8,128)(2,1)} %param.19) | copy-start | bytes 6291460

commit v5 on v4

--- a/solution.py
+++ b/solution.py
@@ -351,61 +351,60 @@
 
 
 def attention_step(step, lim_ref, q_ref, ko_ref, vo_ref, kt_ref, vt_ref, do_ref, o_ref, lse_ref,
-                   dq_ref, dko_ref, dvo_ref, dkt_ref, dvt_ref, qa_ref, doa_ref, dq_sum):
+                   grads, qa_ref, doa_ref, dq_sum):
     rows = q_ref.shape[0]
-    head, j = (step // 2) % 2, step % 2
+    j = step % 2
+    lanes = pl.ds(pl.multiple_of((step // 2) * 128, 128), 128)
     lane = lax.broadcasted_iota(jnp.int32, (1, 128), 1)
-    own = (lane // 64) == head
-    f = 64 * (1 - head)
+    low = lane < 64
+    wide = lambda ref: ref[...].astype(jnp.float32)
 
     @pl.when(j == 0)
     def _():
-        q = q_ref[...].astype(jnp.float32) * 0.125
-        do = do_ref[...].astype(jnp.float32)
-        prod = do * o_ref[...].astype(jnp.float32)
+        q = wide(q_ref) * 0.125
+        do = wide(do_ref)
+        prod = do * wide(o_ref)
         lh, lm, ll = split3(lse_ref[...])
-        delta = jnp.sum(jnp.where(own, prod, 0.0), -1, keepdims=True)
-        dh, dm, dl = split3(delta)
-        qa_ref[...] = jnp.where(own, q, jnp.where(lane == f, 1.0, jnp.where(lane == f + 1, -lh, jnp.where(lane == f + 2, -lm, jnp.where(lane == f + 3, -ll, 0.0))))).astype(jnp.bfloat16)
-        doa_ref[...] = jnp.where(own, do, jnp.where(lane == f, -dh, jnp.where(lane == f + 1, -dm, jnp.where(lane == f + 2, -dl, 0.0)))).astype(jnp.bfloat16)
+        for h in range(2):
+            own = low if h == 0 else jnp.logical_not(low)
+            f = 64 * (1 - h)
+            delta = jnp.sum(jnp.where(own, prod, 0.0), -1, keepdims=True)
+            dh, dm, dl = split3(delta)
+            qa_ref[h] = jnp.where(own, q, jnp.where(lane == f, 1.0, jnp.where(lane == f + 1, -lh, jnp.where(lane == f + 2, -lm, jnp.where(lane == f + 3, -ll, 0.0))))).astype(jnp.bfloat16)
+            doa_ref[h] = jnp.where(own, do, jnp.where(lane == f, -dh, jnp.where(lane == f + 1, -dm, jnp.where(lane == f + 2, -dl, 0.0)))).astype(jnp.bfloat16)
 
     row = lax.broadcasted_iota(jnp.int32, (rows, 1), 0)
-    wide = lambda ref: ref[...].astype(jnp.float32)
     k = jnp.where(j == 0, wide(ko_ref), wide(kt_ref))
     v = jnp.where(j == 0, wide(vo_ref), wide(vt_ref))
-    kone = jnp.where((lane > f) & (lane <= f + 3), 1.0, 0.0)
-    vone = jnp.where((lane >= f) & (lane < f + 3), 1.0, 0.0)
     bias = jnp.where(row < lim_ref[j], 0.0, -BIG)
-    ka = jnp.where(own, k, jnp.where(lane == f, bias, kone)).astype(jnp.bfloat16)
-    va = jnp.where(own, v, vone).astype(jnp.bfloat16)
-    qa, doa = qa_ref[...], doa_ref[...]
-    pt = jnp.exp(dot(ka, qa, 1, 1))
-    dpt = dot(va, doa, 1, 1)
-    dst = (pt * dpt).astype(jnp.bfloat16)
-    dv = dot(pt.astype(jnp.bfloat16), doa, 1, 0)
-    dk = dot(dst, qa, 1, 0)
-    part = dot(dst, ka, 0, 0)
-
-    def put(ref, values):
-        @pl.when(head == 0)
-        def _():
-            ref[...] = values.astype(ref.dtype)
-
-        @pl.when(head == 1)
-        def _():
-            ref[...] = jnp.where(lane < 64, wide(ref), values).astype(ref.dtype)
+    heads = []
+    for h in range(2):
+        own = low if h == 0 else jnp.logical_not(low)
+        f = 64 * (1 - h)
+        kone = jnp.where((lane > f) & (lane <= f + 3), 1.0, 0.0)
+        vone = jnp.where((lane >= f) & (lane < f + 3), 1.0, 0.0)
+        ka = jnp.where(own, k, jnp.where(lane == f, bias, kone)).astype(jnp.bfloat16)
+        va = jnp.where(own, v, vone).astype(jnp.bfloat16)
+        qa, doa = qa_ref[h], doa_ref[h]
+        pt = jnp.exp(dot(ka, qa, 1, 1))
+        dpt = dot(va, doa, 1, 1)
+        dst = (pt * dpt).astype(jnp.bfloat16)
+        dv = dot(pt.astype(jnp.bfloat16), doa, 1, 0)
+        dk = dot(dst, qa, 1, 0)
+        heads.append((dot(dst, ka, 0, 0), dk, dv))
+    part, dk, dv = (jnp.where(low, first, second) for first, second in zip(*heads))
 
     @pl.when(j == 0)
     def _():
         dq_sum[...] = part
-        put(dko_ref, dk)
-        put(dvo_ref, dv)
+        grads[1, :, lanes] = dk.astype(jnp.bfloat16)
+        grads[2, :, lanes] = dv.astype(jnp.bfloat16)
 
     @pl.when(j == 1)
     def _():
-        put(dq_ref, (dq_sum[...] + part) * 0.125)
-        put(dkt_ref, dk)
-        put(dvt_ref, dv)
+        grads[0, :, lanes] = ((dq_sum[...] + part) * 0.125).astype(jnp.bfloat16)
+        grads[3, :, lanes] = dk.astype(jnp.bfloat16)
+        grads[4, :, lanes] = dv.astype(jnp.bfloat16)
 
 
 def sum_kernel(units, plan, layout, sides, *refs):
@@ -414,7 +413,8 @@
     for name, count in layout:
         parts[name] = refs[at : at + count]
         at += count
-    lefts, rights, outs, turned = (parts[name] for name in ("lefts", "rights", "outs", "turned"))
+    lefts, rights, outs = (parts[name] for name in ("lefts", "rights", "outs"))
+    turned, grads = parts["turned"][0], parts["held"][0]
     send, recv, keep = parts["send"], parts["recv"], parts["keep"]
     out_sem, in_sem = parts["sems"]
     stages = 4 + sides
@@ -422,7 +422,7 @@
     tick = pl.program_id(0)
     item, seq = lax.axis_index("items"), lax.axis_index("seq")
     bit = lambda value, place: jnp.bitwise_and(value // (1 << place), 1)
-    core, y, z0, z1, x = bit(item, 0), bit(item, 1), bit(item, 2), bit(item, 3), seq
+    x = seq
     flip = lambda place: item + (1 - 2 * bit(item, place)) * (1 << place)
     partners = {
         "core": (flip(0), seq),
@@ -453,7 +453,7 @@
 
     def copy(name, unit):
         number, to = table[name]
-        slot, landing = unit % 2, unit % 4
+        slot, landing = unit % LAG, unit % (2 * LAG)
         return pltpu.make_async_remote_copy(
             src_ref=send[number].at[slot],
             dst_ref=recv[number].at[landing],
@@ -465,33 +465,33 @@
 
     def post(name, unit, mine, other):
         number, _ = table[name]
-        keep[number][unit % 2] = mine
-        send[number][unit % 2] = low(other)
+        keep[number][unit % LAG] = mine
+        send[number][unit % LAG] = low(other)
         copy(name, unit).start()
 
     def take(name, unit):
         number, _ = table[name]
         copy(name, unit).wait()
-        return keep[number][unit % 2] + wide(recv[number][unit % 4])
+        return keep[number][unit % LAG] + wide(recv[number][unit % (2 * LAG)])
+
+    def place_of(block):
+        differs = [lax.rem(bit(block, place) + bit(item, place), 2) for place in range(4)]
+        place = differs[0] * 8 + differs[1] * 4 + differs[2] * 2 + differs[3]
+        return pl.ds(pl.multiple_of(place * 64, 64), 64)
 
     def turn(which, start):
-        left, target = lefts[which], turned[which]
-        halves = target.shape[0]
-        if halves == 1:
-
-            @pl.loop(0, target.shape[1] // 128)
-            def _(i):
-                run = pl.ds(pl.multiple_of(i * 128, 128), 128)
-                target[0, run] = left[:, run].T
-
-        else:
-
-            @pl.loop(0, 16)
-            def _(i):
+        left = lefts[which]
+
+        @pl.loop(0, 16 if left.shape[1] > 1024 else 8)
+        def _(i):
+            if left.shape[1] > 1024:
                 block = left[:, pl.ds(pl.multiple_of(i * 256 + start * 128, 128), 128)].T
-                run = pl.ds(pl.multiple_of(i * 64, 64), 64)
-                target[0, run] = block[:64]
-                target[1, run] = block[64:]
+                turned[0, place_of(i)] = block[:64]
+                turned[1, place_of(i)] = block[64:]
+            else:
+                block = left[:, pl.ds(pl.multiple_of(i * 128, 128), 128)].T
+                turned[slot_of(which), place_of(2 * i)] = block[:64]
+                turned[slot_of(which), place_of(2 * i + 1)] = block[64:]
 
     def stage_zero(unit):
         at = 0
@@ -509,42 +509,60 @@
                 for segment, pairs in terms:
 
                     @pl.when((unit >= at + place) & (unit < at + place + segment))
-                    def _(pairs=pairs):
-                        total = None
-                        for which, right in pairs:
-                            half = ((unit - at) // 4) % turned[which].shape[0]
-                            part = dot(turned[which][half], rights[right][...], 1, 0)
-                            total = part if total is None else total + part
-                        post("d", unit, *choose(total.reshape(8, 2, 64, 256), 1, core))
+                    def _(pairs=pairs, place=place):
+                        def product(run):
+                            total = None
+                            for which, right in pairs:
+                                deep = lefts[which].shape[1] > 1024
+                                half = ((unit - at) // 4) % 2 if deep else slot_of(which)
+                                if right < HELD:
+                                    values = rights[right][...]
+                                else:
+                                    local = unit - at - place
+                                    column = pl.multiple_of((local % 4) * 256, 256)
+                                    values = grads[right - HELD + local // 4, :, pl.ds(column, 256)]
+                                part = dot(turned[half, run], values, 1, 0)
+                                total = part if total is None else total + part
+                            return total.reshape(8, 64, 256)
+
+                        send[0][unit % LAG] = low(product(slice(512, 1024)))
+                        copy("d", unit).start()
+                        keep[0][unit % LAG] = product(slice(0, 512))
 
                     place += segment
 
             at += count
+
+    def halves(values):
+        count = values.shape[0] // 2
+        return values[:count], values[count:]
 
     def stage_one(unit):
         total = take("d", unit)
-        post("ay", unit, *choose(total[:, :, :cut].reshape(4, 2, 64, cut), 1, y))
+        post("ay", unit, *halves(total[:, :, :cut]))
         if sides == 2:
             post("bx", unit, *choose(total[:, :, cut:].reshape(8, 2, 32, cut), 1, x))
 
     def stage_two(unit):
-        post("az", unit, *choose(take("ay", unit).reshape(2, 2, 64, cut), 1, z0))
+        post("az", unit, *halves(take("ay", unit)))
         if sides == 2:
-            post("by", unit, *choose(take("bx", unit).reshape(4, 2, 32, cut), 1, y))
+            post("by", unit, *halves(take("bx", unit)))
 
     def stage_three(unit):
-        post("aw", unit, *choose(take("az", unit), 0, z1))
+        total = take("az", unit)
+        post("aw", unit, total[0], total[1])
         if sides == 2:
-            post("bz", unit, *choose(take("by", unit).reshape(2, 2, 32, cut), 1, z0))
+            post("bz", unit, *halves(take("by", unit)))
 
     def stage_four(unit):
         total = low(take("aw", unit))
         post("ax", unit, wide(total), total)
         if sides == 2:
-            post("bw", unit, *choose(take("bz", unit), 0, z1))
+            rest = take("bz", unit)
+            post("bw", unit, rest[0], rest[1])
 
     def stage_five(unit):
-        parts["last"][0][unit % 2] = take("ax", unit)
+        parts["last"][0][unit % LAG] = take("ax", unit)
         total = low(take("bw", unit))
         post("bg", unit, wide(total), total)
 
@@ -554,12 +572,12 @@
         else:
             number, _ = table["bg"]
             copy("bg", unit).wait()
-            other = wide(recv[number][unit % 4])
-            mine = keep[number][unit % 2]
+            other = wide(recv[number][unit % (2 * LAG)])
+            mine = keep[number][unit % LAG]
             top = jnp.where(x == 0, mine, other)
             bottom = jnp.where(x == 0, other, mine)
             block = jnp.concatenate(
-                [parts["last"][0][unit % 2], jnp.concatenate([top, bottom], 0)], 1
+                [parts["last"][0][unit % LAG], jnp.concatenate([top, bottom], 0)], 1
             )
         at = 0
         for (count, _, _), out in zip(plan, outs):
@@ -579,76 +597,112 @@
         def _(number=number, unit=unit):
             steps[number](unit)
 
-    if parts["attention"]:
-
-        @pl.when(tick < ATTENTION_STEPS)
-        def _():
-            attention_step(tick, *parts["attention"], *parts["grads"], *parts["held"])
-
-    if parts["vector"]:
-        vector, gathered_out = parts["vector"][0], parts["gathered"][0]
-        gathered, got_vector, vec_out, vec_in = parts["gather"]
-        give_ref, got_ref = parts["give"][0], parts["got"][0]
-        give_out, give_in = parts["give_sems"]
-        ticks = pl.num_programs(0)
-        chunk = give_ref.shape[0] // GIVES
-
-        def other_copy(source, target, out, into, to):
-            return pltpu.make_async_remote_copy(
-                src_ref=source,
-                dst_ref=target,
-                send_sem=out,
-                recv_sem=into,
-                device_id=partners[to],
-                device_id_type=MESH,
-            )
-
-        give_copy = lambda source, target: other_copy(
-            source, target, give_out.at[0], give_in.at[0], "x"
-        )
-
-        @pl.when(tick < GIVES)
-        def _():
-            run = pl.ds(pl.multiple_of(tick * chunk, chunk), chunk)
-            give_copy(give_ref.at[run], got_ref.at[run]).start()
-
-        @pl.when(tick == ticks - 1)
-        def _():
-            give_copy(give_ref, got_ref).wait()
-
-        first = other_copy(vector, got_vector, vec_out.at[0], vec_in.at[0], "x")
-        hops = []
-        for number, to in enumerate(("core", "y", "z0", "z1")):
-            count = 1 << number
-            run = gathered.at[pl.ds((item // count) * count, count)]
-            hops.append(other_copy(run, run, vec_out.at[number + 1], vec_in.at[number + 1], to))
-
-        @pl.when(tick == 0)
-        def _():
-            first.start()
-
-        @pl.when(tick == LAG)
-        def _():
-            first.wait()
-            heights = lax.broadcasted_iota(jnp.int32, vector.shape, 0)
-            gathered[item] = vector[...] + jnp.where(
-                heights < vector.shape[0] - 8, got_vector[...], 0.0
-            )
-            hops[0].start()
-
-        for number in range(4):
-
-            @pl.when(tick == LAG * (number + 2))
-            def _(number=number):
-                hops[number].wait()
-                if number < 3:
-                    hops[number + 1].start()
-                else:
-                    gathered_out[...] = gathered[...]
-
-
-ATTENTION_STEPS = 32
-GIVES = 10
+    @pl.when((tick < 2 * ATTENTION_STEPS) & (lax.rem(tick, 2) == 0))
+    def _():
+        attention_step(tick // 2, *parts["attention"], *parts["held"])
+
+    vector, weight, normed, normed_rest = parts["project"]
+    partial_out, got_ref, gathered_out, frames_out = parts["results"]
+    gathered, got_vector, own_vector, give_ref = parts["gather"]
+    vec_out, vec_in, give_out, give_in = parts["gather_sems"]
+
+    @pl.when(tick == 0)
+    def _():
+        own_vector[...] = vector[...]
+
+    @pl.when((tick >= SHARE) & (tick < SHARE + 8) & (lax.rem(tick, 2) == 0))
+    def _():
+        column = (tick - SHARE) // 2
+        query, key, value = (weight[:, which * 1024 : (which + 1) * 1024] for which in range(3))
+        share = dot(grads[3], key, 1, 1) + dot(grads[4], value, 1, 1)
+        partial = dot(grads[0], query, 1, 1) + dot(grads[1], key, 1, 1) + dot(grads[2], value, 1, 1)
+        give_ref[:, pl.ds(pl.multiple_of(column * 256, 256), 256)] = low(share)
+        partial_out[...] = partial
+        scale = jnp.sum(partial * normed[...] + share * normed_rest[...], 0, keepdims=True)
+        shift = jnp.sum(partial + share, 0, keepdims=True)
+        for part in range(2):
+            lanes = slice(part * 128, (part + 1) * 128)
+            own_vector[pl.ds(column * 2 + part, 1)] = scale[:, lanes]
+            own_vector[pl.ds(8 + column * 2 + part, 1)] = shift[:, lanes]
+
+    weight_down, mid = parts["dense"]
+
+    @pl.when((tick >= DENSE) & (tick < DENSE + 16) & (lax.rem(tick, 4) == DENSE % 4))
+    def _():
+        half = mid.shape[0] // 2
+
+        @pl.loop(0, 2)
+        def _(i):
+            run = pl.ds(pl.multiple_of(i * half, half), half)
+            frames_out[run] = low(mid[run] + dot(lefts[0][run], weight_down[...], 1, 0))
+
+    def other_copy(source, target, out, into, to):
+        return pltpu.make_async_remote_copy(
+            src_ref=source,
+            dst_ref=target,
+            send_sem=out,
+            recv_sem=into,
+            device_id=partners[to],
+            device_id_type=MESH,
+        )
+
+    give_copy = lambda source, target: other_copy(
+        source, target, give_out.at[0], give_in.at[0], "x"
+    )
+    chunk = give_ref.shape[0] // GIVES
+    begin = SHARE + 8
+
+    @pl.when((tick >= begin) & (tick < begin + GIVES))
+    def _():
+        run = pl.ds(pl.multiple_of((tick - begin) * chunk, chunk), chunk)
+        give_copy(give_ref.at[run], got_ref.at[run]).start()
+
+    @pl.when(tick == pl.num_programs(0) - 1)
+    def _():
+        give_copy(give_ref, got_ref).wait()
+
+    first = other_copy(own_vector, got_vector, vec_out.at[0], vec_in.at[0], "x")
+    hops = []
+    for number, to in enumerate(("core", "y", "z0", "z1")):
+        count = 1 << number
+        run = gathered.at[pl.ds((item // count) * count, count)]
+        hops.append(other_copy(run, run, vec_out.at[number + 1], vec_in.at[number + 1], to))
+
+    @pl.when(tick == begin)
+    def _():
+        first.start()
+
+    @pl.when(tick == begin + 2)
+    def _():
+        first.wait()
+        heights = lax.broadcasted_iota(jnp.int32, vector.shape, 0)
+        gathered[item] = own_vector[...] + jnp.where(
+            heights < vector.shape[0] - 8, got_vector[...], 0.0
+        )
+        hops[0].start()
+
+    for number in range(4):
+
+        @pl.when(tick == begin + 2 * (number + 2))
+        def _(number=number):
+            hops[number].wait()
+            if number < 3:
+                hops[number + 1].start()
+            else:
+                gathered_out[...] = gathered[...]
+
+
+ATTENTION_STEPS = 16
+SHARE = 32
+HELD = 100
+
+
+def slot_of(which):
+    return (which + 1) % 2
+
+
+DENSE = 41
+GIVES = 20
 HOPS = {
     1: [
         ("d", "core", (8, 64, 256)),
@@ -672,14 +726,15 @@
 }
 
 
-def sum_weights(weights, lefts, sides, vector=None, share=None, attention=None):
+def sum_weights(weights, lefts, sides, attention, project, dense):
     tile = 256
     stages = 4 + sides
     low = lambda *shape: pltpu.VMEM(shape, jnp.bfloat16)
     full = lambda *shape: pltpu.VMEM(shape, jnp.float32)
     deep = [lefts[weight[0][0][0]].shape[1] // 1024 for weight in weights]
+    wide_of = lambda right: 1024 * len(right) if isinstance(right, range) else right.shape[1]
     units = sum(
-        segment[0][1].shape[1] * depth // tile
+        wide_of(segment[0][1]) * depth // tile
         for weight, depth in zip(weights, deep)
         for segment in weight
     )
@@ -687,23 +742,25 @@
     for left in lefts:
         spec = pl.BlockSpec(left.shape, lambda i: (0, 0), pipeline_mode=pl.Buffered(1))
         inputs.append(("lefts", left, spec))
-        scratch.append(("turned", low(1 + left.shape[1] // 2048 // 2, 1024, left.shape[0])))
     seen, plan = set(), []
     at = flops = rights = 0
     for weight, depth in zip(weights, deep):
         terms, turns = [], []
         place = 0
         for segment in weight:
-            across = segment[0][1].shape[1] // tile
+            across = wide_of(segment[0][1]) // tile
             count = across * depth
             pairs = []
             for which, right in segment:
                 if which not in seen:
                     seen.add(which)
                     turns += [(which, place + more) for more in range(0, count if depth > 1 else 1, 8)]
+                flops += 2 * 1024 * depth * lefts[0].shape[0] * wide_of(right)
+                if isinstance(right, range):
+                    pairs.append((which, HELD + right.start))
+                    continue
                 pairs.append((which, rights))
                 rights += 1
-                flops += 2 * 1024 * depth * right.shape[0] * right.shape[1]
                 spec = pl.BlockSpec(
                     (right.shape[0], tile),
                     lambda i, start=at + place, count=count, across=across: (
@@ -727,51 +784,51 @@
         at += place
     hops = HOPS[sides]
     for _, _, shape in hops:
-        scratch.append(("send", low(2, *shape)))
-        scratch.append(("recv", low(4, *shape)))
-        scratch.append(("keep", full(2, *shape)))
-    scratch.append(("last", full(2, 64, 128)))
-    scratch.append(("sems", pltpu.SemaphoreType.DMA((len(hops), 2))))
-    scratch.append(("sems", pltpu.SemaphoreType.DMA((len(hops), 4))))
-    transcendentals = 0
-    if vector is not None:
-        anywhere = pl.BlockSpec(memory_space=pl.ANY)
-        inputs.append(("vector", vector, pl.BlockSpec(vector.shape, lambda i: (0, 0))))
-        inputs.append(("give", share, anywhere))
-        shape = (16,) + vector.shape
-        outputs.append(("gathered", jax.ShapeDtypeStruct(shape, jnp.float32), pl.BlockSpec(shape, lambda i: (0, 0, 0))))
-        outputs.append(("got", jax.ShapeDtypeStruct(share.shape, share.dtype), anywhere))
-        scratch += [("gather", full(*shape)), ("gather", full(*vector.shape))]
-        scratch += [("gather", pltpu.SemaphoreType.DMA((5,)))] * 2
-        scratch += [("give_sems", pltpu.SemaphoreType.DMA((1,)))] * 2
-    if attention is not None:
-        lim, qkv, kv_rest, do, o, lse = attention
-        count, width = do.shape
-        pairs = width // 128
-        place = lambda skip: pl.BlockSpec(
-            (count, 128), lambda i: (0, jnp.minimum(i // 4, pairs - 1) + skip)
-        )
-        inputs.append(("attention", lim, pl.BlockSpec(memory_space=pltpu.SMEM)))
-        for operand, skip in (
-            (qkv, 0),
-            (qkv, pairs),
-            (qkv, 2 * pairs),
-            (kv_rest, 0),
-            (kv_rest, pairs),
-            (do, 0),
-            (o, 0),
-            (lse, 0),
-        ):
-            inputs.append(("attention", operand, place(skip)))
-        for _ in range(5):
-            outputs.append(("grads", jax.ShapeDtypeStruct(do.shape, jnp.bfloat16), place(0)))
-        scratch += [("held", low(count, 128)), ("held", low(count, 128)), ("held", full(count, 128))]
-        flops += 40 * count * 2 * count * width
-        transcendentals += count * 2 * count * width // 64
+        scratch.append(("send", low(LAG, *shape)))
+        scratch.append(("recv", low(2 * LAG, *shape)))
+        scratch.append(("keep", full(LAG, *shape)))
+    scratch.append(("last", full(LAG, 64, 128)))
+    scratch.append(("sems", pltpu.SemaphoreType.DMA((len(hops), LAG))))
+    scratch.append(("sems", pltpu.SemaphoreType.DMA((len(hops), 2 * LAG))))
+    lim, qkv, kv_rest, do, o, lse = attention
+    count, width = do.shape
+    blocks = width // 128
+    place = lambda skip: pl.BlockSpec(
+        (count, 128), lambda i: (0, jnp.minimum(i // 4, blocks - 1) + skip)
+    )
+    inputs.append(("attention", lim, pl.BlockSpec(memory_space=pltpu.SMEM)))
+    skips = (0, blocks, 2 * blocks, 0, blocks, 0, 0, 0)
+    for operand, skip in zip((qkv, qkv, qkv, kv_rest, kv_rest, do, o, lse), skips):
+        inputs.append(("attention", operand, place(skip)))
+    scratch += [("turned", low(2, 1024, count)), ("held", low(5, count, width))]
+    scratch += [("held", low(2, count, 128)), ("held", low(2, count, 128)), ("held", full(count, 128))]
+    vector, w_qkv, normed, normed_rest = project
+    share_of = lambda i: jnp.clip((i - SHARE) // 2, 0, 3)
+    dense_of = lambda i: (0, jnp.clip((i - DENSE) // 4, 0, 3))
+    column = pl.BlockSpec((count, tile), lambda i: (0, share_of(i)))
+    inputs.append(("project", vector, pl.BlockSpec(vector.shape, lambda i: (0, 0))))
+    inputs.append(("project", w_qkv, pl.BlockSpec((tile, w_qkv.shape[1]), lambda i: (share_of(i), 0))))
+    inputs += [("project", normed, column), ("project", normed_rest, column)]
+    for operand in dense:
+        inputs.append(("dense", operand, pl.BlockSpec((operand.shape[0], tile), dense_of)))
+    shape = (16,) + vector.shape
+    result = lambda shape, dtype, spec: ("results", jax.ShapeDtypeStruct(shape, dtype), spec)
+    outputs += [
+        result(do.shape, jnp.float32, column),
+        result(do.shape, jnp.bfloat16, pl.BlockSpec(memory_space=pl.ANY)),
+        result(shape, jnp.float32, pl.BlockSpec(shape, lambda i: (0, 0, 0))),
+        result(do.shape, jnp.bfloat16, pl.BlockSpec((count, tile), dense_of)),
+    ]
+    scratch += [("gather", full(*shape)), ("gather", full(*vector.shape)), ("gather", full(*vector.shape))]
+    scratch.append(("gather", low(*do.shape)))
+    scratch += [("gather_sems", pltpu.SemaphoreType.DMA((5,)))] * 2
+    scratch += [("gather_sems", pltpu.SemaphoreType.DMA((1,)))] * 2
+    flops += (80 * count + 14 * width) * count * width
+    transcendentals = 2 * count * count * width // 64
     groups = (
-        ("lefts", "rights", "vector", "give", "attention"),
-        ("outs", "gathered", "got", "grads"),
-        ("turned", "send", "recv", "keep", "last", "sems", "gather", "give_sems", "held"),
+        ("lefts", "rights", "attention", "project", "dense"),
+        ("outs", "results"),
+        ("turned", "held", "send", "recv", "keep", "last", "sems", "gather", "gather_sems"),
     )
     layout, ordered = [], []
     for names, entries in zip(groups, (inputs, outputs, scratch)):
@@ -787,7 +844,7 @@
         out_shape=[shape for shape, _ in ordered[1]],
         scratch_shapes=[shape for shape, in ordered[2]],
         compiler_params=pltpu.CompilerParams(
-            vmem_limit_bytes=58 << 20, collective_id=sides - 1, has_side_effects=True
+            vmem_limit_bytes=63 << 20, collective_id=sides - 1, has_side_effects=True
         ),
         cost_estimate=pl.CostEstimate(
             flops=flops,
@@ -853,76 +910,72 @@
     upper = project(ffn_in, w_up)
     act = gelu_exact(upper).astype(jnp.bfloat16)
     grad_upper = (grad_act.astype(jnp.float32) * gelu_slope(upper)).astype(jnp.bfloat16)
-    out_frames = (mid + project(act, w_down)).astype(jnp.bfloat16)
 
     grad_out = cotangent.astype(jnp.float32)
     fused = seq_size == 2 and item_size == 16 and width == 1024
-    grad_upper, out_frames = lax.optimization_barrier((grad_upper, out_frames))
     grad_ffn_in = lax.optimization_barrier(back_project(grad_upper, w_up))
     grad_scale_two = jnp.sum(grad_ffn_in * normed_two, 0)
     grad_shift_two = jnp.sum(grad_ffn_in, 0)
     grad_mid = grad_out + norm_back(grad_ffn_in * (1.0 + scale_two), normed_two, inv_two)
     grad_mid_low = grad_mid.astype(jnp.bfloat16)
     grad_att = back_project(grad_mid_low, w_out).astype(jnp.bfloat16)
-    down_terms = [[(0, cotangent)]]
-    if fused:
-        sum_down, sum_up, sum_out, *grads = sum_weights(
-            [down_terms, [[(1, grad_upper)]], [[(2, grad_mid_low)]]],
-            [act, ffn_in, att],
-            2,
-            attention=(limits, qkv, kv_rest, grad_att, att, lse),
-        )
-        grad_query, grad_key, grad_value, key_rest, value_rest = grads
-    else:
-        grad_query, grad_key, grad_value, key_rest, value_rest = attend_back(
-            limits, qkv, kv_rest, grad_att, att, lse
-        )
-    qkv_terms = [
-        [(0, grad_query)],
-        [(0, grad_key), (1, key_rest)],
-        [(0, grad_value), (1, value_rest)],
-    ]
-    w_key, w_value = w_qkv[:, width : 2 * width], w_qkv[:, 2 * width :]
-    share = back_project(key_rest, w_key) + back_project(value_rest, w_value)
-    partial = (
-        back_project(grad_query, w_qkv[:, :width])
-        + back_project(grad_key, w_key)
-        + back_project(grad_value, w_value)
-    )
-    partial, share = lax.optimization_barrier((partial, share))
-    share_low = share.astype(jnp.bfloat16)
-    grad_scale_one = jnp.sum(partial * normed_one, 0) + jnp.sum(share * normed_rest, 0)
-    grad_shift_one = jnp.sum(partial, 0) + jnp.sum(share, 0)
-    grad_modul = jnp.concatenate(
-        [grad_scale_one, grad_shift_one, grad_scale_two, grad_shift_two]
-    )[None, :]
     if fused:
         vector = jnp.concatenate(
             [
-                grad_modul.reshape(4 * width // 128, 128),
+                jnp.zeros((2 * width // 128, 128), jnp.float32),
+                jnp.concatenate([grad_scale_two, grad_shift_two]).reshape(2 * width // 128, 128),
                 jnp.pad(onehot, ((0, 7), (0, 128 - section_count))),
             ]
         )
-        sum_qkv, tagged, got_share = sum_weights(
-            [qkv_terms], [attn_in, attn_rest], 1, vector=vector, share=share_low
+        sum_down, sum_up, sum_out, sum_qkv, partial, got_share, tagged, out_frames = sum_weights(
+            [
+                [[(0, cotangent)]],
+                [[(1, grad_upper)]],
+                [[(2, grad_mid_low)]],
+                [[(3, range(0, 1))], [(3, range(1, 3)), (4, range(3, 5))]],
+            ],
+            [act, ffn_in, att, attn_in, attn_rest],
+            2,
+            (limits, qkv, kv_rest, grad_att, att, lse),
+            (vector, w_qkv, normed_one, normed_rest),
+            (w_down, mid),
         )
         grad_rest = [got_share]
         tagged = tagged[:, : 4 * width // 128 + 1].reshape(item_size, 4 * width + 128)
     else:
+        out_frames = (mid + project(act, w_down)).astype(jnp.bfloat16)
+        grad_query, grad_key, grad_value, key_rest, value_rest = attend_back(
+            limits, qkv, kv_rest, grad_att, att, lse
+        )
+        w_key, w_value = w_qkv[:, width : 2 * width], w_qkv[:, 2 * width :]
+        share = back_project(key_rest, w_key) + back_project(value_rest, w_value)
+        partial = (
+            back_project(grad_query, w_qkv[:, :width])
+            + back_project(grad_key, w_key)
+            + back_project(grad_value, w_value)
+        )
+        share_low = share.astype(jnp.bfloat16)
         grad_rest = [
             give(share_low[i * row_count : (i + 1) * row_count], turn)
             for i, turn in enumerate(turns)
         ]
-        sum_down = finish(outer(side, [act], down_terms, item_size, 256), "items", "seq")
-        sum_up = finish(outer(side, [ffn_in], [[(0, grad_upper)]], item_size, 512), "items", "seq")
-        sum_out = finish(
-            outer(side, [att], [[(0, grad_mid_low)]], item_size, 512), "items", "seq"
-        )
-        sum_qkv = finish(
-            outer(side, [attn_in, attn_rest], qkv_terms, item_size, 512),
-            "items",
-            "seq",
-        )
+        grad_scale_one = jnp.sum(partial * normed_one, 0) + jnp.sum(share * normed_rest, 0)
+        grad_shift_one = jnp.sum(partial, 0) + jnp.sum(share, 0)
+        grad_modul = jnp.concatenate(
+            [grad_scale_one, grad_shift_one, grad_scale_two, grad_shift_two]
+        )[None, :]
+        qkv_terms = [
+            [(0, grad_query)],
+            [(0, grad_key), (1, key_rest)],
+            [(0, grad_value), (1, value_rest)],
+        ]
+        sums = lambda lefts, terms, tile: finish(
+            outer(side, lefts, terms, item_size, tile), "items", "seq"
+        )
+        sum_down = sums([act], [[(0, cotangent)]], 256)
+        sum_up = sums([ffn_in], [[(0, grad_upper)]], 512)
+        sum_out = sums([att], [[(0, grad_mid_low)]], 512)
+        sum_qkv = sums([attn_in, attn_rest], qkv_terms, 512)
         for bit in bits_of("seq"):
             grad_modul = grad_modul + swap(grad_modul, "seq", bit)
         tagged = jnp.concatenate(

time: 346 us -> 327 us (0.945)
  matrix products: 81.8 us -> 61.6 us
  Pallas kernels: 208 us -> 227 us
  other arithmetic: 39.3 us -> 24.8 us
    pallas_call x2 -> x1, Pallas kernels: 185 us -> 204 us  [sum_weights(): pl.pallas_call(functools.partial(sum_kernel, units, tuple(plan), tuple(la...]
    convert_element_type x1, other arithmetic: 13.2 us -> 2.22 us  [per_device(): grad_mid_low = grad_mid.astype(jnp.bfloat16)]
    dot_general x8 -> x3, matrix products: 33.9 us -> 23.6 us  [back_project(): lax.dot_general(flat, weight, (((1,), (1,)), ((), ())), preferred_element...]
    dot_general x5 -> x4, matrix products: 36.1 us -> 27.6 us  [project(): result = jnp.dot(flat, weight, preferred_element_type=jnp.float32)]
    mul x0 -> x2, other arithmetic: none -> 4.16 us  [normalize(): return (centered * inverse, inverse)]
    convert_element_type x3 -> x1, other arithmetic: 10.4 us -> 6.81 us  [per_device(): (grad_act.astype(jnp.float32) * gelu_slope(upper)).astype(jnp.bfloat16)]
    unnamed x73 -> x52, local copies, waits for them, and re-layouts: 7.83 us -> 7.7 us
where the time goes in v5:
time: 327 us; the launch traced here: 326 us
  Pallas kernels  227 us (69%)
  matrix products  61.6 us (19%)
  other arithmetic  24.8 us (8%)
  local copies, waits for them, and re-layouts  7.73 us (2%)
    pallas_call x1, Pallas kernels, sum_weights(): pl.pallas_call(functools.partial(sum_kernel, units, tuple(plan), tuple(la...  204 us
    dot_general x4, matrix products, project(): result = jnp.dot(flat, weight, preferred_element_type=jnp.float32)  27.6 us
    dot_general x3, matrix products, back_project(): lax.dot_general(flat, weight, (((1,), (1,)), ((), ())), preferred_element...  23.6 us
    pallas_call x1, Pallas kernels, attend(): pl.pallas_call(functools.partial(fwd_kernel, rows, blocks), grid_spec=plt...  22.3 us
    unnamed x52, local copies, waits for them, and re-layouts  7.7 us
    convert_element_type x1, other arithmetic, per_device(): (grad_act.astype(jnp.float32) * gelu_slope(upper)).astype(jnp.bfloat16)  6.81 us
  transfers between devices with their start and end apart: 1, of which 0 were waited for; matrix products, arithmetic and copies ran while one was open for 9% of the time, Pallas kernels for 0%

profile of v5, /device:TPU:0, one launch (start us, length us, event | category | flops | bytes accessed | tf_op | source)
XLA Modules:
  0.0 326.1 jit_solution(13816249713755314137)
XLA Ops:
  0.6 0.0 copy-start
  0.7 3.0 collective-permute-start
  3.7 1.6 convert_reduce_fusion
  6.6 0.0 copy-done
  6.6 0.1 convolution_bitcast_fusion
  6.7 0.0 copy-start.18
  6.7 0.0 copy-start.2
  6.8 5.8 %fusion.38 = f32[1,4096]{1,0:T(1,128)S(1)} fusion(f32[1024,1]{0,1:T(1,128)S(1)} %convolution_bitcast_fusion, bf16[1024,4096]{1,0:T(8,128)(2,1)} %param.16), kind=kOutput, calls=%fused_computation.78 | convolution fusion | flops 50331648 | bytes 8409088 | tf_op jit(solution)/shard_map/dot_general | solution.py:893
  12.5 0.0 copy-done.18
  12.6 0.0 copy-done.2
  12.6 0.5 fusion.15
  13.1 2.1 fusion.13
  15.2 9.0 %convolution_convert_fusion.1.q_ref.ko_ref.vo_ref.refs_9_.refs_10_.refs_11_ = bf16[640,3072]{1,0:T(8,128)(2,1)} fusion(bf16[640,1024]{1,0:T(8,128)(2,1)S(1)} %get-tuple-element.48.refs_3_, bf16[1024,3072]{1,0:T(8,128)(2,1)} %refs_18_.1), kind=kOutput, calls=%fused_computation.10 | convolution fusion | flops 4028497920 | bytes 11534336 | tf_op jit(solution)/shard_map/dot_general | solution.py:46
  24.2 0.0 copy-done.9
  24.2 0.6 compare_select_fusion.lim_ref.refs_8_
  24.8 11.0 %convolution_convert_fusion = bf16[640,4096]{1,0:T(8,128)(2,1)} fusion(bf16[4096,1024]{1,0:T(8,128)(2,1)} %refs_21_.1, bf16[1,640,1024]{2,1,0:T(8,128)(2,1)} %param.12), kind=kOutput, calls=%fused_computation.9 | convolution fusion | flops 5371330560 | bytes 14942208 | tf_op jit(solution)/shard_map/dot_general | solution.py:52
  35.8 0.0 collective-permute-done
  35.8 0.2 convert_reduce_fusion.1
  36.1 0.5 fusion.16
  36.5 2.1 fusion.11
  38.6 1.1 copy-done.10
  39.7 6.4 %fusion.8.kt_ref.vt_ref.refs_12_.refs_13_ = bf16[640,2048]{1,0:T(8,128)(2,1)} fusion(bf16[640,1024]{1,0:T(8,128)(2,1)S(1)} %get-tuple-element.46.refs_4_, bf16[1024,3072]{1,0:T(8,128)(2,1)} %refs_18_.1), kind=kOutput, calls=%fused_computation.18 | convolution fusion | flops 2685665280 | bytes 8126464 | tf_op jit(solution)/shard_map/dot_general | solution.py:46
  46.1 22.3 %shard_map.178 = (bf16[640,1024]{1,0:T(8,128)(2,1)}, f32[640,1024]{1,0:T(8,128)}) custom-call(s32[2]{0:T(128)} %compare_select_fusion.lim_ref.refs_8_, bf16[640,3072]{1,0:T(8,128)(2,1)} %convolution_convert_fusion.1.q_ref.ko_ref.vo_ref.refs_9_.refs_10_.refs_11_, bf16[640,3072]{1,0:T(8,128)(2,1)} %convolution_convert_fusion.1.q_ref.ko_ref.vo_ref.refs_9_.refs_10_.refs_11_, ...), custom_call_target="tpu_custom_call" | custom-call | flops 13421772800 | bytes 10485760 | tf_op jit(solution)/shard_map/pallas_call | solution.py:163
  68.4 0.0 copy-done.19
  68.4 3.0 fusion.37
  71.4 0.4 multiply_reduce_fusion.3
  71.8 0.0 slice-start
  71.8 0.5 add_convert_fusion.1.refs_1_
  72.3 0.0 copy-start.13
  72.3 0.0 slice-start.1
  72.3 9.2 %fusion.39 = f32[640,4096]{1,0:T(8,128)S(1)} fusion(bf16[640,1024]{1,0:T(8,128)(2,1)S(1)} %add_convert_fusion.1.refs_1_, bf16[1024,4096]{1,0:T(8,128)(2,1)} %param.20), kind=kOutput, calls=%fused_computation.79 | convolution fusion | flops 5368709120 | bytes 20185088 | tf_op jit(solution)/shard_map/dot_general | solution.py:46
  81.5 0.0 copy-done.13
  81.5 0.0 slice-done
  81.5 0.0 slice-done.1
  81.5 6.8 %fusion.5 = (bf16[640,4096]{1,0:T(8,128)(2,1)S(1)}, bf16[640,4096]{1,0:T(8,128)(2,1)}) fusion(f32[640,4096]{1,0:T(8,128)S(1)} %fusion.39, bf16[640,4096]{1,0:T(8,128)(2,1)S(1)} %bitcast.64), kind=kLoop, calls=%fused_computation.6 | loop fusion | flops 36700160 | bytes 26214400 | tf_op jit(solution)/shard_map/convert_element_type | solution.py:912
  88.4 9.9 %fusion.40 = f32[640,1024]{1,0:T(8,128)S(1)} fusion(bf16[640,4096]{1,0:T(8,128)(2,1)S(1)} %get-tuple-element.43.refs_6_, bf16[1024,4096]{1,0:T(8,128)(2,1)} %param.20), kind=kOutput, calls=%fused_computation.80 | convolution fusion | flops 5368709120 | bytes 16252928 | tf_op jit(solution)/shard_map/dot_general | solution.py:52
  98.3 0.0 copy-done.6
  98.3 0.0 copy-start.8
  98.3 1.0 multiply_reduce_fusion.1
  99.4 0.0 copy-done.1
  99.4 0.2 copy-done.8
  99.6 2.2 fusion.36
  101.8 0.0 copy-done.20
  101.8 2.7 convolution_convert_fusion.2.refs_14_
  104.5 0.0 copy-done.11
  104.5 0.7 pad_maximum_fusion.refs_17_
  105.2 204.4 %shard_map.179 = (f32[256,1024]{1,0:T(8,128)}, f32[64,4096]{1,0:T(8,128)}, f32[64,1024]{1,0:T(8,128)}, f32[64,3072]{1,0:T(8,128)}, f32[640,1024]{1,0:T(8,128)}, ...) custom-call(bf16[640,4096]{1,0:T(8,128)(2,1)} %get-tuple-element.44.refs_0_, ...), custom_call_target="tpu_custom_call" | custom-call | flops 61740154880 | bytes 57944068 | tf_op jit(solution)/shard_map/pallas_call | solution.py:839
  309.6 0.0 copy-start.3
  309.6 0.0 copy-start.7
  309.6 1.2 copy.22
  310.8 0.2 fusion.21
  311.0 1.6 fusion.19
  312.6 2.0 fusion.33
  314.6 0.8 fusion.23
  315.4 0.0 copy-done.3
  315.4 2.8 fusion.18
  318.2 0.6 dynamic-slice_reduce_fusion
  318.8 2.1 fusion.17
  321.0 1.1 copy.30
  322.0 0.5 copy-done.16
  322.6 0.9 copy.31
  323.4 0.7 copy.32
  324.1 1.0 copy.33
  325.1 1.0 copy.34
  (38 shorter events, 0.2 us)
Async XLA Ops:
  0.6 5.9 %copy-start = (f32[8,1024]{1,0:T(8,128)S(1)}, f32[8,1024]{1,0:T(8,128)}, u32[]{:S(2)}) copy-start(f32[8,1024]{1,0:T(8,128)} %param.15) | copy-start | bytes 98308
  0.7 35.1 %collective-permute-start = (bf16[640,1024]{1,0:T(8,128)(2,1)}, bf16[640,1024]{1,0:T(8,128)(2,1)S(1)}, u32[]{:S(2)}, u32[]{:S(2)}) collective-permute-start(bf16[640,1024]{1,0:T(8,128)(2,1)} %bitcast.62), channel_id=1, source_target_pairs={{1,0},{0,1},{3,2},{2,3},{5,4},{4,5},{7,6},{6,7},{9,8},{8,9},{11,10... | collective-permute-start | bytes 3932168 | tf_op jit(solution)/shard_map/ppermute | solution.py:878
  6.7 5.8 %copy-start.18 = (f32[4096]{0:T(1024)S(1)}, f32[4096]{0:T(1024)}, u32[]{:S(2)}) copy-start(f32[4096]{0:T(1024)} %param.17) | copy-start | bytes 49156
  6.7 5.8 %copy-start.2 = (bf16[1,640,1024]{2,1,0:T(8,128)(2,1)S(1)}, bf16[1,640,1024]{2,1,0:T(8,128)(2,1)}, u32[]{:S(2)}) copy-start(bf16[1,640,1024]{2,1,0:T(8,128)(2,1)} %param.11) | copy-start | bytes 3932164
  15.2 9.0 %copy-start.9 = (bf16[640,1024]{1,0:T(8,128)(2,1)}, bf16[640,1024]{1,0:T(8,128)(2,1)S(1)}, u32[]{:S(2)}) copy-start(bf16[640,1024]{1,0:T(8,128)(2,1)S(1)} %get-tuple-element.48.refs_3_) | copy-start | bytes 3932164
  38.6 1.1 copy-start.10
  46.1 22.3 %copy-start.19 = (bf16[1024,1024]{1,0:T(8,128)(2,1)S(1)}, bf16[1024,1024]{1,0:T(8,128)(2,1)}, u32[]{:S(2)}) copy-start(bf16[1024,1024]{1,0:T(8,128)(2,1)} %param.19) | copy-start | bytes 6291460
  71.3 28.0 %copy-start.1 = (f32[640,1024]{1,0:T(8,128)}, f32[640,1024]{1,0:T(8,128)S(1)}, u32[]{:S(2)}) copy-start(f32[640,1024]{1,0:T(8,128)S(1)} %get-tuple-element.54.refs_22_) | copy-start | bytes 7864324
  71.8 9.7 %slice-start = ((s8[5242880]{0:T(1024)(128)(4,1)}), s8[4194304]{0:T(1024)(128)(4,1)S(1)}, s32[]{:S(2)}) async-start(s8[5242880]{0:T(1024)(128)(4,1)} %bitcast.63), calls=%async_computation | async-start | bytes 8388608
  72.3 9.2 %copy-start.13 = (bf16[640,1024]{1,0:T(8,128)(2,1)}, bf16[640,1024]{1,0:T(8,128)(2,1)S(1)}, u32[]{:S(2)}) copy-start(bf16[640,1024]{1,0:T(8,128)(2,1)S(1)} %add_convert_fusion.1.refs_1_) | copy-start | bytes 3932164
  72.3 9.2 %slice-start.1 = ((s8[5242880]{0:T(1024)(128)(4,1)}), s8[1048576]{0:T(1024)(128)(4,1)S(1)}, s32[]{:S(2)}) async-start(s8[5242880]{0:T(1024)(128)(4,1)} %bitcast.63), calls=%async_computation.1 | async-start | bytes 2097152
  88.3 9.9 %copy-start.6 = (bf16[640,4096]{1,0:T(8,128)(2,1)}, bf16[640,4096]{1,0:T(8,128)(2,1)S(1)}, u32[]{:S(2)}) copy-start(bf16[640,4096]{1,0:T(8,128)(2,1)S(1)} %get-tuple-element.43.refs_6_) | copy-start | bytes 15728644
  98.3 1.3 copy-start.8
  99.6 2.2 copy-start.20
  101.8 2.7 copy-start.11
  309.6 5.8 %copy-start.3 = (bf16[1,640,1024]{2,1,0:T(8,128)(2,1)S(1)}, bf16[1,640,1024]{2,1,0:T(8,128)(2,1)}, u32[]{:S(2)}) copy-start(bf16[1,640,1024]{2,1,0:T(8,128)(2,1)} %param.11) | copy-start | bytes 3932164
  309.6 5.8 %copy-start.7 = (bf16[640,1024]{1,0:T(8,128)(2,1)S(1)}, bf16[640,1024]{1,0:T(8,128)(2,1)}, u32[]{:S(2)}) copy-start(bf16[640,1024]{1,0:T(8,128)(2,1)} %get-tuple-element.29) | copy-start | bytes 3932164
  315.4 3.5 %copy-start.4 = (f32[640,1024]{1,0:T(8,128)S(1)}, f32[640,1024]{1,0:T(8,128)}, u32[]{:S(2)}) copy-start(f32[640,1024]{1,0:T(8,128)} %get-tuple-element.42) | copy-start | bytes 7864324
  315.4 3.5 %copy-start.5 = (f32[640,1024]{1,0:T(8,128)S(1)}, f32[640,1024]{1,0:T(8,128)}, u32[]{:S(2)}) copy-start(f32[640,1024]{1,0:T(8,128)} %get-tuple-element.28) | copy-start | bytes 7864324
  318.8 2.1 copy-start.12
  320.9 1.6 copy-start.16
  320.9 2.5 copy-start.17
  320.9 3.2 copy-start.15
  322.6 2.6 copy-start.14

commit v6 on v5

--- a/solution.py
+++ b/solution.py
@@ -610,9 +610,9 @@
     def _():
         own_vector[...] = vector[...]
 
-    @pl.when((tick >= SHARE) & (tick < SHARE + 8) & (lax.rem(tick, 2) == 0))
-    def _():
-        column = (tick - SHARE) // 2
+    @pl.when((tick >= SHARE) & (tick < SHARE + 4))
+    def _():
+        column = tick - SHARE
         query, key, value = (weight[:, which * 1024 : (which + 1) * 1024] for which in range(3))
         share = dot(grads[3], key, 1, 1) + dot(grads[4], value, 1, 1)
         partial = dot(grads[0], query, 1, 1) + dot(grads[1], key, 1, 1) + dot(grads[2], value, 1, 1)
@@ -650,7 +650,7 @@
         source, target, give_out.at[0], give_in.at[0], "x"
     )
     chunk = give_ref.shape[0] // GIVES
-    begin = SHARE + 8
+    begin = SHARE + 4
 
     @pl.when((tick >= begin) & (tick < begin + GIVES))
     def _():
@@ -803,7 +803,7 @@
     scratch += [("turned", low(2, 1024, count)), ("held", low(5, count, width))]
     scratch += [("held", low(2, count, 128)), ("held", low(2, count, 128)), ("held", full(count, 128))]
     vector, w_qkv, normed, normed_rest = project
-    share_of = lambda i: jnp.clip((i - SHARE) // 2, 0, 3)
+    share_of = lambda i: jnp.clip(i - SHARE, 0, 3)
     dense_of = lambda i: (0, jnp.clip((i - DENSE) // 4, 0, 3))
     column = pl.BlockSpec((count, tile), lambda i: (0, share_of(i)))
     inputs.append(("project", vector, pl.BlockSpec(vector.shape, lambda i: (0, 0))))

time: 327 us -> 323 us (0.988)
  Pallas kernels: 227 us -> 223 us
    pallas_call x1, Pallas kernels: 204 us -> 201 us  [sum_weights(): pl.pallas_call(functools.partial(sum_kernel, units, tuple(plan), tuple(la...]
  transfers between devices with their start and end apart: 1 -> 1, of which waited for: 0 -> 0; matrix products, arithmetic and copies ran while one was open for 9% -> 10% of each run, Pallas kernels for 0% -> 0%
where the time goes in v6:
time: 323 us; the launch traced here: 322 us
  Pallas kernels  223 us (69%)
  matrix products  61.6 us (19%)
  other arithmetic  24.8 us (8%)
  local copies, waits for them, and re-layouts  7.73 us (2%)
    pallas_call x1, Pallas kernels, sum_weights(): pl.pallas_call(functools.partial(sum_kernel, units, tuple(plan), tuple(la...  201 us
    dot_general x4, matrix products, project(): result = jnp.dot(flat, weight, preferred_element_type=jnp.float32)  27.6 us
    dot_general x3, matrix products, back_project(): lax.dot_general(flat, weight, (((1,), (1,)), ((), ())), preferred_element...  23.6 us
    pallas_call x1, Pallas kernels, attend(): pl.pallas_call(functools.partial(fwd_kernel, rows, blocks), grid_spec=plt...  22.3 us
    unnamed x52, local copies, waits for them, and re-layouts  7.7 us
    convert_element_type x1, other arithmetic, per_device(): (grad_act.astype(jnp.float32) * gelu_slope(upper)).astype(jnp.bfloat16)  6.81 us
  transfers between devices with their start and end apart: 1, of which 0 were waited for; matrix products, arithmetic and copies ran while one was open for 10% of the time, Pallas kernels for 0%

profile of v6, /device:TPU:0, one launch (start us, length us, event | category | flops | bytes accessed | tf_op | source)
XLA Modules:
  0.0 322.4 jit_solution(16100382463995182962)
XLA Ops:
  0.6 0.0 copy-start
  0.7 3.0 collective-permute-start
  3.7 1.6 convert_reduce_fusion
  6.6 0.0 copy-done
  6.6 0.1 convolution_bitcast_fusion
  6.7 0.0 copy-start.18
  6.7 0.0 copy-start.2
  6.8 5.8 %fusion.38 = f32[1,4096]{1,0:T(1,128)S(1)} fusion(f32[1024,1]{0,1:T(1,128)S(1)} %convolution_bitcast_fusion, bf16[1024,4096]{1,0:T(8,128)(2,1)} %param.16), kind=kOutput, calls=%fused_computation.78 | convolution fusion | flops 50331648 | bytes 8409088 | tf_op jit(solution)/shard_map/dot_general | solution.py:893
  12.5 0.0 copy-done.18
  12.6 0.0 copy-done.2
  12.6 0.5 fusion.15
  13.1 2.1 fusion.13
  15.2 9.0 %convolution_convert_fusion.1.q_ref.ko_ref.vo_ref.refs_9_.refs_10_.refs_11_ = bf16[640,3072]{1,0:T(8,128)(2,1)} fusion(bf16[640,1024]{1,0:T(8,128)(2,1)S(1)} %get-tuple-element.48.refs_3_, bf16[1024,3072]{1,0:T(8,128)(2,1)} %refs_18_.1), kind=kOutput, calls=%fused_computation.10 | convolution fusion | flops 4028497920 | bytes 11534336 | tf_op jit(solution)/shard_map/dot_general | solution.py:46
  24.2 0.0 copy-done.9
  24.2 0.6 compare_select_fusion.lim_ref.refs_8_
  24.8 11.0 %convolution_convert_fusion = bf16[640,4096]{1,0:T(8,128)(2,1)} fusion(bf16[4096,1024]{1,0:T(8,128)(2,1)} %refs_21_.1, bf16[1,640,1024]{2,1,0:T(8,128)(2,1)} %param.12), kind=kOutput, calls=%fused_computation.9 | convolution fusion | flops 5371330560 | bytes 14942208 | tf_op jit(solution)/shard_map/dot_general | solution.py:52
  35.8 0.0 collective-permute-done
  35.8 0.2 convert_reduce_fusion.1
  36.1 0.5 fusion.16
  36.5 2.1 fusion.11
  38.6 1.1 copy-done.10
  39.7 6.4 %fusion.8.kt_ref.vt_ref.refs_12_.refs_13_ = bf16[640,2048]{1,0:T(8,128)(2,1)} fusion(bf16[640,1024]{1,0:T(8,128)(2,1)S(1)} %get-tuple-element.46.refs_4_, bf16[1024,3072]{1,0:T(8,128)(2,1)} %refs_18_.1), kind=kOutput, calls=%fused_computation.18 | convolution fusion | flops 2685665280 | bytes 8126464 | tf_op jit(solution)/shard_map/dot_general | solution.py:46
  46.1 22.3 %shard_map.178 = (bf16[640,1024]{1,0:T(8,128)(2,1)}, f32[640,1024]{1,0:T(8,128)}) custom-call(s32[2]{0:T(128)} %compare_select_fusion.lim_ref.refs_8_, bf16[640,3072]{1,0:T(8,128)(2,1)} %convolution_convert_fusion.1.q_ref.ko_ref.vo_ref.refs_9_.refs_10_.refs_11_, bf16[640,3072]{1,0:T(8,128)(2,1)} %convolution_convert_fusion.1.q_ref.ko_ref.vo_ref.refs_9_.refs_10_.refs_11_, ...), custom_call_target="tpu_custom_call" | custom-call | flops 13421772800 | bytes 10485760 | tf_op jit(solution)/shard_map/pallas_call | solution.py:163
  68.4 0.0 copy-done.19
  68.4 3.0 fusion.37
  71.4 0.4 multiply_reduce_fusion.3
  71.8 0.0 slice-start
  71.8 0.5 add_convert_fusion.1.refs_1_
  72.3 0.0 copy-start.13
  72.3 0.0 slice-start.1
  72.3 9.2 %fusion.39 = f32[640,4096]{1,0:T(8,128)S(1)} fusion(bf16[640,1024]{1,0:T(8,128)(2,1)S(1)} %add_convert_fusion.1.refs_1_, bf16[1024,4096]{1,0:T(8,128)(2,1)} %param.20), kind=kOutput, calls=%fused_computation.79 | convolution fusion | flops 5368709120 | bytes 20185088 | tf_op jit(solution)/shard_map/dot_general | solution.py:46
  81.5 0.0 copy-done.13
  81.5 0.0 slice-done
  81.5 0.0 slice-done.1
  81.5 6.8 %fusion.5 = (bf16[640,4096]{1,0:T(8,128)(2,1)S(1)}, bf16[640,4096]{1,0:T(8,128)(2,1)}) fusion(f32[640,4096]{1,0:T(8,128)S(1)} %fusion.39, bf16[640,4096]{1,0:T(8,128)(2,1)S(1)} %bitcast.64), kind=kLoop, calls=%fused_computation.6 | loop fusion | flops 36700160 | bytes 26214400 | tf_op jit(solution)/shard_map/convert_element_type | solution.py:912
  88.4 9.9 %fusion.40 = f32[640,1024]{1,0:T(8,128)S(1)} fusion(bf16[640,4096]{1,0:T(8,128)(2,1)S(1)} %get-tuple-element.43.refs_6_, bf16[1024,4096]{1,0:T(8,128)(2,1)} %param.20), kind=kOutput, calls=%fused_computation.80 | convolution fusion | flops 5368709120 | bytes 16252928 | tf_op jit(solution)/shard_map/dot_general | solution.py:52
  98.3 0.0 copy-done.6
  98.3 0.0 copy-start.8
  98.3 1.0 multiply_reduce_fusion.1
  99.4 0.0 copy-done.1
  99.4 0.2 copy-done.8
  99.6 2.2 fusion.36
  101.8 0.0 copy-done.20
  101.8 2.7 convolution_convert_fusion.2.refs_14_
  104.5 0.7 pad_maximum_fusion.refs_17_
  105.2 200.7 %shard_map.179 = (f32[256,1024]{1,0:T(8,128)}, f32[64,4096]{1,0:T(8,128)}, f32[64,1024]{1,0:T(8,128)}, f32[64,3072]{1,0:T(8,128)}, f32[640,1024]{1,0:T(8,128)}, ...) custom-call(bf16[640,4096]{1,0:T(8,128)(2,1)} %get-tuple-element.44.refs_0_, ...), custom_call_target="tpu_custom_call" | custom-call | flops 61740154880 | bytes 57944068 | tf_op jit(solution)/shard_map/pallas_call | solution.py:839
  305.9 0.0 copy-start.3
  306.0 1.2 copy.22
  307.1 0.2 fusion.21
  307.3 1.6 fusion.19
  308.9 2.0 fusion.33
  310.9 0.8 fusion.23
  311.7 0.0 copy-done.3
  311.7 2.8 fusion.18
  314.6 0.6 dynamic-slice_reduce_fusion
  315.2 0.0 copy-done.4
  315.2 2.1 fusion.17
  317.3 1.1 copy.30
  318.4 0.5 copy-done.16
  318.9 0.9 copy.31
  319.8 0.7 copy.32
  320.5 0.0 copy-done.15
  320.5 1.0 copy.33
  321.5 1.0 copy.34
  (38 shorter events, 0.2 us)
Async XLA Ops:
  0.6 5.9 %copy-start = (f32[8,1024]{1,0:T(8,128)S(1)}, f32[8,1024]{1,0:T(8,128)}, u32[]{:S(2)}) copy-start(f32[8,1024]{1,0:T(8,128)} %param.15) | copy-start | bytes 98308
  0.7 35.1 %collective-permute-start = (bf16[640,1024]{1,0:T(8,128)(2,1)}, bf16[640,1024]{1,0:T(8,128)(2,1)S(1)}, u32[]{:S(2)}, u32[]{:S(2)}) collective-permute-start(bf16[640,1024]{1,0:T(8,128)(2,1)} %bitcast.62), channel_id=1, source_target_pairs={{1,0},{0,1},{3,2},{2,3},{5,4},{4,5},{7,6},{6,7},{9,8},{8,9},{11,10... | collective-permute-start | bytes 3932168 | tf_op jit(solution)/shard_map/ppermute | solution.py:878
  6.7 5.8 %copy-start.18 = (f32[4096]{0:T(1024)S(1)}, f32[4096]{0:T(1024)}, u32[]{:S(2)}) copy-start(f32[4096]{0:T(1024)} %param.17) | copy-start | bytes 49156
  6.7 5.8 %copy-start.2 = (bf16[1,640,1024]{2,1,0:T(8,128)(2,1)S(1)}, bf16[1,640,1024]{2,1,0:T(8,128)(2,1)}, u32[]{:S(2)}) copy-start(bf16[1,640,1024]{2,1,0:T(8,128)(2,1)} %param.11) | copy-start | bytes 3932164
  15.2 9.0 %copy-start.9 = (bf16[640,1024]{1,0:T(8,128)(2,1)}, bf16[640,1024]{1,0:T(8,128)(2,1)S(1)}, u32[]{:S(2)}) copy-start(bf16[640,1024]{1,0:T(8,128)(2,1)S(1)} %get-tuple-element.48.refs_3_) | copy-start | bytes 3932164
  38.6 1.1 copy-start.10
  46.1 22.3 %copy-start.19 = (bf16[1024,1024]{1,0:T(8,128)(2,1)S(1)}, bf16[1024,1024]{1,0:T(8,128)(2,1)}, u32[]{:S(2)}) copy-start(bf16[1024,1024]{1,0:T(8,128)(2,1)} %param.19) | copy-start | bytes 6291460
  71.3 28.0 %copy-start.1 = (f32[640,1024]{1,0:T(8,128)}, f32[640,1024]{1,0:T(8,128)S(1)}, u32[]{:S(2)}) copy-start(f32[640,1024]{1,0:T(8,128)S(1)} %get-tuple-element.54.refs_22_) | copy-start | bytes 7864324
  71.8 9.7 %slice-start = ((s8[5242880]{0:T(1024)(128)(4,1)}), s8[4194304]{0:T(1024)(128)(4,1)S(1)}, s32[]{:S(2)}) async-start(s8[5242880]{0:T(1024)(128)(4,1)} %bitcast.63), calls=%async_computation | async-start | bytes 8388608
  72.3 9.2 %copy-start.13 = (bf16[640,1024]{1,0:T(8,128)(2,1)}, bf16[640,1024]{1,0:T(8,128)(2,1)S(1)}, u32[]{:S(2)}) copy-start(bf16[640,1024]{1,0:T(8,128)(2,1)S(1)} %add_convert_fusion.1.refs_1_) | copy-start | bytes 3932164
  72.3 9.2 %slice-start.1 = ((s8[5242880]{0:T(1024)(128)(4,1)}), s8[1048576]{0:T(1024)(128)(4,1)S(1)}, s32[]{:S(2)}) async-start(s8[5242880]{0:T(1024)(128)(4,1)} %bitcast.63), calls=%async_computation.1 | async-start | bytes 2097152
  88.3 9.9 %copy-start.6 = (bf16[640,4096]{1,0:T(8,128)(2,1)}, bf16[640,4096]{1,0:T(8,128)(2,1)S(1)}, u32[]{:S(2)}) copy-start(bf16[640,4096]{1,0:T(8,128)(2,1)S(1)} %get-tuple-element.43.refs_6_) | copy-start | bytes 15728644
  98.3 1.3 copy-start.8
  99.6 2.2 copy-start.20
  101.8 2.7 copy-start.11
  305.9 5.8 %copy-start.3 = (bf16[1,640,1024]{2,1,0:T(8,128)(2,1)S(1)}, bf16[1,640,1024]{2,1,0:T(8,128)(2,1)}, u32[]{:S(2)}) copy-start(bf16[1,640,1024]{2,1,0:T(8,128)(2,1)} %param.11) | copy-start | bytes 3932164
  305.9 5.8 %copy-start.7 = (bf16[640,1024]{1,0:T(8,128)(2,1)S(1)}, bf16[640,1024]{1,0:T(8,128)(2,1)}, u32[]{:S(2)}) copy-start(bf16[640,1024]{1,0:T(8,128)(2,1)} %get-tuple-element.29) | copy-start | bytes 3932164
  311.7 3.5 %copy-start.4 = (f32[640,1024]{1,0:T(8,128)S(1)}, f32[640,1024]{1,0:T(8,128)}, u32[]{:S(2)}) copy-start(f32[640,1024]{1,0:T(8,128)} %get-tuple-element.42) | copy-start | bytes 7864324
  311.7 3.5 %copy-start.5 = (f32[640,1024]{1,0:T(8,128)S(1)}, f32[640,1024]{1,0:T(8,128)}, u32[]{:S(2)}) copy-start(f32[640,1024]{1,0:T(8,128)} %get-tuple-element.28) | copy-start | bytes 7864324
  315.2 2.1 copy-start.12
  317.3 1.6 copy-start.16
  317.3 2.5 copy-start.17
  317.3 3.2 copy-start.15
  318.9 2.6 copy-start.14
